TPU v7x, 32 devices: a whole 2x2x4 slice. The times are simulated.
32 devices in a mesh: dp: 8 (over z, x), tensor: 4 (over y, core).
Axes of the slice: x: 2, y: 2, z: 4, core: 2. Of those that a mesh axis runs over, the one named last changes fastest.
Arguments:
- inputs: float32 [4, 8192, 768], P(None, ('dp', 'tensor')), may hold values from -6 to 6
- w_qkv: float32 [3, 768, 768], P(None, None, 'tensor'), may hold values from -0.21875 to 0.21875
- w_out: float32 [768, 768], P('tensor'), may hold values from -3 to 3
- w_gate_up: float32 [2, 768, 2048], P(None, None, 'tensor'), may hold values from -0.21875 to 0.21875
- w_down: float32 [2048, 768], P('tensor'), may hold values from -0.125 to 0.125
- gain_attn: float32 [768], replicated, may hold values from 0.5 to 1.5
- gain_mlp: float32 [768], replicated, may hold values from 0.5 to 1.5
- piece_starts: int32 [4, 8, 2], P(None, 'dp'), may hold values from 0 to 768, as said below
- out_grad: float32 [4, 8192, 768], P(None, ('dp', 'tensor')), may hold values from -6 to 6
Outputs:
- outputs: float32 [4, 8192, 768], P(None, ('dp', 'tensor'))
- input_grad: float32 [4, 8192, 768], P(None, ('dp', 'tensor'))
- grad_qkv: float32 [3, 768, 768], P(None, None, 'tensor')
- grad_out: float32 [768, 768], P('tensor')
- grad_gate_up: float32 [2, 768, 2048], P(None, None, 'tensor')
- grad_down: float32 [2048, 768], P('tensor')
- grad_gain_attn: float32 [768], replicated
- grad_gain_mlp: float32 [768], replicated
Inputs may be any that keep to these rules, and one draw needn't show every extreme that they name: `piece_starts`: each sequence has 2 image pieces of 256 tokens; the k-th lies wholly inside the k-th of 2 equal parts of the sequence, so pieces never intersect.
All inputs are finite; a program needn't handle non-finite values.
Results may differ from a plain program's by a relative error of at most 0.02.
The roundings to bfloat16 on the way count: a program that leaves them out, or rounds other values in their place, can miss the bound.
Values may be sent and summed in bfloat16 or wider, within the bound.
No kernel may reach another device: no remote copies, remote signals or barrier semaphores. Data moves between devices by JAX's collectives and lax.ppermute only.
A program may use at most 320 MiB of HBM per device.

v0:
```python
import jax
import jax.numpy as jnp
from jax import lax
from jax.sharding import PartitionSpec as P

HD = 64
LEN = 1024
PIECE = 256


epsilon = 1e-06


def rope_tables(length, width):
    halfway = width // 2
    inverse = 10000.0 ** (-jnp.arange(halfway, dtype=jnp.float32) * 2.0 / width)
    angles = jnp.arange(length, dtype=jnp.float32)[:, None] * inverse[None, :]
    return (jnp.cos(angles)[:, None, :], jnp.sin(angles)[:, None, :])


def rotate(vector, cosine, sine):
    halfway = vector.shape[-1] // 2
    first = vector[..., :halfway]
    second = vector[..., halfway:]
    return jnp.concatenate(
        [first * cosine - second * sine, second * cosine + first * sine], axis=-1
    )


def unrotate(vector, cosine, sine):
    halfway = vector.shape[-1] // 2
    first = vector[..., :halfway]
    second = vector[..., halfway:]
    return jnp.concatenate(
        [first * cosine + second * sine, second * cosine - first * sine], axis=-1
    )


def piece_mask(starts, length, piece_len):
    position = jnp.arange(length, dtype=jnp.int32)
    inside = (position[:, None] >= starts[None, :]) & (
        position[:, None] < starts[None, :] + piece_len
    )
    numbers = jnp.arange(1, starts.shape[0] + 1, dtype=jnp.int32)
    labels = jnp.sum(inside.astype(jnp.int32) * numbers[None, :], axis=1)
    causal = position[None, :] <= position[:, None]
    same_piece = (labels[:, None] == labels[None, :]) & (labels[:, None] > 0)
    return causal | same_piece


def norm_scale(tokens_mb):
    return lax.rsqrt(jnp.mean(tokens_mb * tokens_mb, axis=-1, keepdims=True) + epsilon)


def norm_back(grad_normed, unit_rows, scale_rows, gain):
    scaled = grad_normed * gain
    return scale_rows * (scaled - unit_rows * jnp.mean(scaled * unit_rows, axis=-1, keepdims=True))


def gather_rows(normed):
    return lax.all_gather(normed, "tensor", axis=0, tiled=True)


def branch_sum(partial_value):
    return lax.psum_scatter(
        partial_value.astype(jnp.bfloat16), "tensor", scatter_dimension=0, tiled=True
    ).astype(jnp.float32)


def gather_grads(gradient):
    return lax.all_gather(gradient, "tensor", axis=0, tiled=True)


def scatter_grads(partial_value):
    return lax.psum_scatter(
        partial_value.astype(jnp.bfloat16), "tensor", scatter_dimension=0, tiled=True
    ).astype(jnp.float32)


def reduce_whole(totals):
    return lax.psum((totals[0], totals[1], totals[2], totals[3]), "dp")


def attend_forward(operands):
    queries, keys_rot, values_seq, allowed = operands
    factor = queries.shape[-1] ** (-0.5)
    scores = (
        jnp.einsum("qhd,khd->hqk", queries, keys_rot, preferred_element_type=jnp.float32) * factor
    )
    scores = jnp.where(allowed[None], scores, -jnp.inf)
    largest = jnp.max(scores, axis=-1, keepdims=True)
    logsum = largest + jnp.log(jnp.sum(jnp.exp(scores - largest), axis=-1, keepdims=True))
    weights_soft = jnp.exp(scores - logsum).astype(jnp.bfloat16)
    mixed = jnp.einsum("hqk,khd->qhd", weights_soft, values_seq, preferred_element_type=jnp.float32)
    return (mixed, logsum[..., 0])


def attend_backward(operands):
    queries, keys_rot, values_seq, grad_mixed, logsum, allowed = operands
    factor = queries.shape[-1] ** (-0.5)
    scores = (
        jnp.einsum("qhd,khd->hqk", queries, keys_rot, preferred_element_type=jnp.float32) * factor
    )
    scores = jnp.where(allowed[None], scores, -jnp.inf)
    weights_soft = jnp.exp(scores - logsum[..., None])
    grad_values = jnp.einsum(
        "hqk,qhd->khd",
        weights_soft.astype(jnp.bfloat16),
        grad_mixed,
        preferred_element_type=jnp.float32,
    )
    grad_soft = jnp.einsum(
        "qhd,khd->hqk", grad_mixed, values_seq, preferred_element_type=jnp.float32
    )
    inner_sum = jnp.sum(weights_soft * grad_soft, axis=-1, keepdims=True)
    grad_scores = (weights_soft * (grad_soft - inner_sum)).astype(jnp.bfloat16)
    grad_queries = (
        jnp.einsum("hqk,khd->qhd", grad_scores, keys_rot, preferred_element_type=jnp.float32)
        * factor
    )
    grad_keys = (
        jnp.einsum("hqk,qhd->khd", grad_scores, queries, preferred_element_type=jnp.float32)
        * factor
    )
    return (grad_queries, grad_keys, grad_values)


def local(inputs, w_qkv, w_out, w_gate_up, w_down, gain_attn, gain_mlp, piece_starts, out_grad):
    qkv_low = w_qkv.astype(jnp.bfloat16)
    out_low = w_out.astype(jnp.bfloat16)
    pair_low = w_gate_up.astype(jnp.bfloat16)
    down_low = w_down.astype(jnp.bfloat16)
    width_local = w_qkv.shape[2]
    heads_local = width_local // HD
    seq_count = piece_starts.shape[1]
    count = inputs.shape[0]
    cosine, sine = rope_tables(LEN, HD)
    zeros_all = (
        jnp.zeros(w_qkv.shape, jnp.float32),
        jnp.zeros(w_out.shape, jnp.float32),
        jnp.zeros(w_gate_up.shape, jnp.float32),
        jnp.zeros(w_down.shape, jnp.float32),
    )
    totals = zeros_all
    gain_one_acc = jnp.zeros(gain_attn.shape, jnp.float32)
    gain_two_acc = jnp.zeros(gain_mlp.shape, jnp.float32)
    result_list = []
    grad_list = []
    for micro in range(count):
        tokens_mb = inputs[micro]
        upstream = out_grad[micro]
        allowed = jax.vmap(lambda row_starts: piece_mask(row_starts, LEN, PIECE))(
            piece_starts[micro]
        )
        scale_one = norm_scale(tokens_mb)
        unit_one = tokens_mb * scale_one
        normed_one = (unit_one * gain_attn).astype(jnp.bfloat16)
        gathered_one = gather_rows(normed_one)
        projected = jnp.einsum(
            "gd,cdk->cgk", gathered_one, qkv_low, preferred_element_type=jnp.float32
        )
        projected = projected.reshape(3, seq_count, LEN, heads_local, HD)
        queries = rotate(projected[0], cosine, sine).astype(jnp.bfloat16)
        keys_rot = rotate(projected[1], cosine, sine).astype(jnp.bfloat16)
        values_seq = projected[2].astype(jnp.bfloat16)
        mixed, logsum = lax.map(attend_forward, (queries, keys_rot, values_seq, allowed))
        mixed_low = mixed.reshape(-1, width_local).astype(jnp.bfloat16)
        after = tokens_mb + branch_sum(
            jnp.dot(mixed_low, out_low, preferred_element_type=jnp.float32)
        )
        scale_two = norm_scale(after)
        unit_two = after * scale_two
        normed_two = (unit_two * gain_mlp).astype(jnp.bfloat16)
        gathered_two = gather_rows(normed_two)
        gate_up = jnp.einsum(
            "gd,cdf->cgf", gathered_two, pair_low, preferred_element_type=jnp.float32
        )
        gate = gate_up[0]
        upward = gate_up[1]
        sigma = jax.nn.sigmoid(gate)
        hidden = (gate * sigma * upward).astype(jnp.bfloat16)
        result_list.append(
            after + branch_sum(jnp.dot(hidden, down_low, preferred_element_type=jnp.float32))
        )
        grad_full = gather_grads(upstream.astype(jnp.bfloat16))
        grad_down_mb = jnp.einsum(
            "gf,gd->fd", hidden, grad_full, preferred_element_type=jnp.float32
        )
        grad_hidden = jnp.einsum(
            "gd,fd->gf", grad_full, down_low, preferred_element_type=jnp.float32
        )
        grad_gate = grad_hidden * upward * sigma * (1.0 + gate * (1.0 - sigma))
        grad_upward = grad_hidden * gate * sigma
        grad_pair = jnp.stack([grad_gate, grad_upward]).astype(jnp.bfloat16)
        grad_pair_mb = jnp.einsum(
            "gd,cgf->cdf", gathered_two, grad_pair, preferred_element_type=jnp.float32
        )
        grad_normed_two = scatter_grads(
            jnp.einsum("cgf,cdf->gd", grad_pair, pair_low, preferred_element_type=jnp.float32)
        )
        gain_two_acc = gain_two_acc + jnp.sum(grad_normed_two * unit_two, axis=0)
        grad_after = upstream + norm_back(grad_normed_two, unit_two, scale_two, gain_mlp)
        grad_branch = gather_grads(grad_after.astype(jnp.bfloat16))
        grad_out_mb = jnp.einsum(
            "gk,gd->kd", mixed_low, grad_branch, preferred_element_type=jnp.float32
        )
        grad_mixed = jnp.einsum(
            "gd,kd->gk", grad_branch, out_low, preferred_element_type=jnp.float32
        )
        grad_mixed = grad_mixed.astype(jnp.bfloat16).reshape(seq_count, LEN, heads_local, HD)
        grad_queries, grad_keys, grad_values = lax.map(
            attend_backward, (queries, keys_rot, values_seq, grad_mixed, logsum, allowed)
        )
        grad_proj = jnp.stack(
            [unrotate(grad_queries, cosine, sine), unrotate(grad_keys, cosine, sine), grad_values]
        )
        grad_proj = grad_proj.astype(jnp.bfloat16).reshape(3, -1, width_local)
        grad_qkv_mb = jnp.einsum(
            "gd,cgk->cdk", gathered_one, grad_proj, preferred_element_type=jnp.float32
        )
        grad_normed_one = scatter_grads(
            jnp.einsum("cgk,cdk->gd", grad_proj, qkv_low, preferred_element_type=jnp.float32)
        )
        gain_one_acc = gain_one_acc + jnp.sum(grad_normed_one * unit_one, axis=0)
        grad_list.append(grad_after + norm_back(grad_normed_one, unit_one, scale_one, gain_attn))
        totals = (
            totals[0] + grad_qkv_mb,
            totals[1] + grad_out_mb,
            totals[2] + grad_pair_mb,
            totals[3] + grad_down_mb,
        )
    final = reduce_whole(totals)
    gain_totals = lax.psum((gain_one_acc, gain_two_acc), ("dp", "tensor"))
    return (
        jnp.stack(result_list),
        jnp.stack(grad_list),
        final[0],
        final[1],
        final[2],
        final[3],
        gain_totals[0],
        gain_totals[1],
    )


def solution(mesh):
    placed = (
        P(None, ("dp", "tensor"), None),
        P(None, None, "tensor"),
        P("tensor", None),
        P(None, None, "tensor"),
        P("tensor", None),
        P(),
        P(),
        P(None, "dp", None),
        P(None, ("dp", "tensor"), None),
    )
    return jax.shard_map(
        local,
        mesh=mesh,
        in_specs=placed,
        out_specs=(
            P(None, ("dp", "tensor"), None),
            P(None, ("dp", "tensor"), None),
            P(None, None, "tensor"),
            P("tensor", None),
            P(None, None, "tensor"),
            P("tensor", None),
            P(),
            P(),
        ),
        check_vma=False,
    )
```

profile of v0, /device:TPU:0, one launch (start us, length us, event | category | flops | bytes accessed | tf_op | source)
XLA Modules:
  0.0 1152.1 jit_solution(4119396728582324825)
XLA Ops:
  22.3 11.7 %all-gather.21.cloned.1.call-done = bf16[1024,768]{1,0:T(8,128)(2,1)} async-done(((bf16[256,768]{1,0:T(8,128)(2,1)}), bf16[1024,768]{1,0:T(8,128)(2,1)}) %all-gather.21.cloned.1.call-update) | async-done | bytes 1572880 | tf_op jit(solution)/shard_map/all_gather | solution.py:61
  37.5 18.3 %all-gather.17.cloned.1.call-done = bf16[1024,768]{1,0:T(8,128)(2,1)} async-done(((bf16[256,768]{1,0:T(8,128)(2,1)}), bf16[1024,768]{1,0:T(8,128)(2,1)}) %all-gather.17.cloned.1.call-update) | async-done | bytes 1572880 | tf_op jit(solution)/shard_map/all_gather | solution.py:61
  60.1 17.5 %all-gather.25.cloned.1.call-done = bf16[1024,768]{1,0:T(8,128)(2,1)} async-done(((bf16[256,768]{1,0:T(8,128)(2,1)}), bf16[1024,768]{1,0:T(8,128)(2,1)}) %all-gather.25.cloned.1.call-update) | async-done | bytes 1572880 | tf_op jit(solution)/shard_map/all_gather | solution.py:61
  161.2 31.1 %reduce-scatter.25.cloned.1.call-done = bf16[256,768]{1,0:T(8,128)(2,1)} async-done(((bf16[1024,768]{1,0:T(8,128)(2,1)}), bf16[256,768]{1,0:T(8,128)(2,1)}) %reduce-scatter.25.cloned.1.call-update) | async-done | bytes 393232 | tf_op jit(solution)/shard_map/reduce_scatter | solution.py:65
  192.3 31.1 %reduce-scatter.29.cloned.1.call-done = bf16[256,768]{1,0:T(8,128)(2,1)} async-done(((bf16[1024,768]{1,0:T(8,128)(2,1)}), bf16[256,768]{1,0:T(8,128)(2,1)}) %reduce-scatter.29.cloned.1.call-update) | async-done | bytes 393232 | tf_op jit(solution)/shard_map/reduce_scatter | solution.py:65
  236.7 11.4 all-gather.27.cloned.1.call-done
  253.8 16.0 %all-gather.41.cloned.1.call-done = bf16[1024,768]{1,0:T(8,128)(2,1)} async-done(((bf16[256,768]{1,0:T(8,128)(2,1)}), bf16[1024,768]{1,0:T(8,128)(2,1)}) %all-gather.41.cloned.1.call-update) | async-done | bytes 1572880 | tf_op jit(solution)/shard_map/all_gather | solution.py:71
  279.9 11.7 %all-gather.19.cloned.1.call-done = bf16[1024,768]{1,0:T(8,128)(2,1)} async-done(((bf16[256,768]{1,0:T(8,128)(2,1)}), bf16[1024,768]{1,0:T(8,128)(2,1)}) %all-gather.19.cloned.1.call-update) | async-done | bytes 1572880 | tf_op jit(solution)/shard_map/all_gather | solution.py:61
  296.8 15.9 %all-gather.33.cloned.1.call-done = bf16[1024,768]{1,0:T(8,128)(2,1)} async-done(((bf16[256,768]{1,0:T(8,128)(2,1)}), bf16[1024,768]{1,0:T(8,128)(2,1)}) %all-gather.33.cloned.1.call-update) | async-done | bytes 1572880 | tf_op jit(solution)/shard_map/all_gather | solution.py:71
  322.7 21.1 %reduce-scatter.41.cloned.1.call-done = bf16[256,768]{1,0:T(8,128)(2,1)} async-done(((bf16[1024,768]{1,0:T(8,128)(2,1)}), bf16[256,768]{1,0:T(8,128)(2,1)}) %reduce-scatter.41.cloned.1.call-update) | async-done | bytes 393232 | tf_op jit(solution)/shard_map/reduce_scatter | solution.py:75
  343.8 31.0 %reduce-scatter.33.cloned.1.call-done = bf16[256,768]{1,0:T(8,128)(2,1)} async-done(((bf16[1024,768]{1,0:T(8,128)(2,1)}), bf16[256,768]{1,0:T(8,128)(2,1)}) %reduce-scatter.33.cloned.1.call-update) | async-done | bytes 393232 | tf_op jit(solution)/shard_map/reduce_scatter | solution.py:75
  379.9 18.0 %all-gather.31.cloned.1.call-done = bf16[1024,768]{1,0:T(8,128)(2,1)} async-done(((bf16[256,768]{1,0:T(8,128)(2,1)}), bf16[1024,768]{1,0:T(8,128)(2,1)}) %all-gather.31.cloned.1.call-update) | async-done | bytes 1572880 | tf_op jit(solution)/shard_map/all_gather | solution.py:61
  403.5 15.5 %all-gather.45.cloned.1.call-done = bf16[1024,768]{1,0:T(8,128)(2,1)} async-done(((bf16[256,768]{1,0:T(8,128)(2,1)}), bf16[1024,768]{1,0:T(8,128)(2,1)}) %all-gather.45.cloned.1.call-update) | async-done | bytes 1572880 | tf_op jit(solution)/shard_map/all_gather | solution.py:71
  429.5 11.1 all-gather.23.cloned.1.call-done
  446.2 15.5 %all-gather.37.cloned.1.call-done = bf16[1024,768]{1,0:T(8,128)(2,1)} async-done(((bf16[256,768]{1,0:T(8,128)(2,1)}), bf16[1024,768]{1,0:T(8,128)(2,1)}) %all-gather.37.cloned.1.call-update) | async-done | bytes 1572880 | tf_op jit(solution)/shard_map/all_gather | solution.py:71
  479.4 13.5 %reduce-scatter.45.cloned.1.call-done = bf16[256,768]{1,0:T(8,128)(2,1)} async-done(((bf16[1024,768]{1,0:T(8,128)(2,1)}), bf16[256,768]{1,0:T(8,128)(2,1)}) %reduce-scatter.45.cloned.1.call-update) | async-done | bytes 393232 | tf_op jit(solution)/shard_map/reduce_scatter | solution.py:75
  492.8 31.0 %reduce-scatter.37.cloned.1.call-done = bf16[256,768]{1,0:T(8,128)(2,1)} async-done(((bf16[1024,768]{1,0:T(8,128)(2,1)}), bf16[256,768]{1,0:T(8,128)(2,1)}) %reduce-scatter.37.cloned.1.call-update) | async-done | bytes 393232 | tf_op jit(solution)/shard_map/reduce_scatter | solution.py:75
  526.1 28.8 %reduce-scatter.19.cloned.1.call-done = bf16[256,768]{1,0:T(8,128)(2,1)} async-done(((bf16[1024,768]{1,0:T(8,128)(2,1)}), bf16[256,768]{1,0:T(8,128)(2,1)}) %reduce-scatter.19.cloned.1.call-update) | async-done | bytes 393232 | tf_op jit(solution)/shard_map/reduce_scatter | solution.py:65
  554.9 31.2 %reduce-scatter.23.cloned.1.call-done = bf16[256,768]{1,0:T(8,128)(2,1)} async-done(((bf16[1024,768]{1,0:T(8,128)(2,1)}), bf16[256,768]{1,0:T(8,128)(2,1)}) %reduce-scatter.23.cloned.1.call-update) | async-done | bytes 393232 | tf_op jit(solution)/shard_map/reduce_scatter | solution.py:65
  594.2 16.1 %all-gather.35.cloned.1.call-done = bf16[1024,768]{1,0:T(8,128)(2,1)} async-done(((bf16[256,768]{1,0:T(8,128)(2,1)}), bf16[1024,768]{1,0:T(8,128)(2,1)}) %all-gather.35.cloned.1.call-update) | async-done | bytes 1572880 | tf_op jit(solution)/shard_map/all_gather | solution.py:71
  665.2 13.6 %multiply_convert_fusion.1 = bf16[3,1024,1024]{1,2,0:T(8,128)(2,1)} fusion(f32[3,1024,1024]{1,2,0:T(8,128)} %get-tuple-element.398, f32[3,1024,1024]{1,2,0:T(8,128)} %copy-done.3, f32[3,1024]{1,0:T(4,128)S(1)} %get-tuple-element.397, f32[3,1024]{1,0:T(4,128)S(1)} %log_add_fusion.1, pred[1024,1024]{0,1:T(8,128)(4,1)S(1)} %copy-done.11), kind=kLoop, calls=%fused_computation.2 | loop fusion | flops 18874368 | bytes 32530432 | tf_op jit(solution)/shard_map/while/body/eval_jaxpr/convert_element_type | solution.py:116
  811.7 28.2 %reduce-scatter.47.cloned.1.call-done = bf16[256,768]{1,0:T(8,128)(2,1)} async-done(((bf16[1024,768]{1,0:T(8,128)(2,1)}), bf16[256,768]{1,0:T(8,128)(2,1)}) %reduce-scatter.47.cloned.1.call-update) | async-done | bytes 393232 | tf_op jit(solution)/shard_map/reduce_scatter | solution.py:75
  843.6 39.6 %all-reduce = (f32[768]{0:T(1024)}, f32[768]{0:T(1024)}) all-reduce(f32[768]{0:T(1024)} %add_add_fusion.2, f32[768]{0:T(1024)S(1)} %add_add_fusion.1), channel_id=1, replica_groups=mesh['dp'=8,'tensor'=4] {'dp','tensor'}, use_global_device_ids=true, to_apply=%region_56.57 | all-reduce | flops 1536 | bytes 12288 | tf_op jit(solution)/shard_map/psum | solution.py:233
  908.1 229.6 %all-reduce.4.cloned.1.call-done = (f32[3,768,192]{1,2,0:T(8,128)}, f32[192,768]{1,0:T(8,128)}, f32[2,768,512]{1,2,0:T(8,128)}, f32[512,768]{1,0:T(8,128)}) async-done(((f32[3,768,192]{1,2,0:T(8,128)}, f32[192,768]{1,0:T(8,128)}, f32[2,768,512]{1,2,0:T(8,128)}, f32[512,768]{1,0:T(8,128)}), (f32[3,768,192]{1,2,0:T(8,128)}, f32[192,768]{1,0:T(8,128)}, f32[2,768,512]{1,2,0:T(8,128)}, ...) | async-done | bytes 7077904 | tf_op jit(solution)/shard_map/psum | solution.py:81
  (645 shorter events, 426.5 us)
Async XLA Ops:
  12.2 65.4 %all-gather.25.cloned.1.call-start = ((), (), s32[]{:S(2)}) async-start(), calls=%async_computation.24 | async-start | bytes 1966080 | tf_op jit(solution)/shard_map/all_gather | solution.py:61
  13.0 103.4 %all-gather.29.cloned.1.call-start = ((), (), s32[]{:S(2)}) async-start(), calls=%async_computation.28 | async-start | bytes 1966080 | tf_op jit(solution)/shard_map/all_gather | solution.py:61
  13.5 144.6 %reduce-scatter.17.cloned.1.call-start = ((), (), s32[]{:S(2)}) async-start(), calls=%async_computation.17 | async-start | bytes 1966080 | tf_op jit(solution)/shard_map/reduce_scatter | solution.py:65
  98.4 62.8 %reduce-scatter.21.cloned.1.call-start = ((), (), s32[]{:S(2)}) async-start(), calls=%async_computation.21 | async-start | bytes 1966080 | tf_op jit(solution)/shard_map/reduce_scatter | solution.py:65
  121.3 71.0 %reduce-scatter.25.cloned.1.call-start = ((), (), s32[]{:S(2)}) async-start(), calls=%async_computation.25 | async-start | bytes 1966080 | tf_op jit(solution)/shard_map/reduce_scatter | solution.py:65
  139.7 83.7 %reduce-scatter.29.cloned.1.call-start = ((), (), s32[]{:S(2)}) async-start(), calls=%async_computation.29 | async-start | bytes 1966080 | tf_op jit(solution)/shard_map/reduce_scatter | solution.py:65
  158.0 90.1 %all-gather.27.cloned.1.call-start = ((), (), s32[]{:S(2)}) async-start(), calls=%async_computation.26 | async-start | bytes 1966080 | tf_op jit(solution)/shard_map/all_gather | solution.py:61
  232.4 80.3 %all-gather.33.cloned.1.call-start = ((), (), s32[]{:S(2)}) async-start(), calls=%async_computation.32 | async-start | bytes 1966080 | tf_op jit(solution)/shard_map/all_gather | solution.py:71
  232.9 110.9 %reduce-scatter.41.cloned.1.call-start = ((), (), s32[]{:S(2)}) async-start(), calls=%async_computation.41 | async-start | bytes 1966080 | tf_op jit(solution)/shard_map/reduce_scatter | solution.py:75
  279.6 95.2 %reduce-scatter.33.cloned.1.call-start = ((), (), s32[]{:S(2)}) async-start(), calls=%async_computation.33 | async-start | bytes 1966080 | tf_op jit(solution)/shard_map/reduce_scatter | solution.py:75
  322.6 75.3 %all-gather.31.cloned.1.call-start = ((), (), s32[]{:S(2)}) async-start(), calls=%async_computation.30 | async-start | bytes 1966080 | tf_op jit(solution)/shard_map/all_gather | solution.py:61
  379.2 82.4 %all-gather.37.cloned.1.call-start = ((), (), s32[]{:S(2)}) async-start(), calls=%async_computation.36 | async-start | bytes 1966080 | tf_op jit(solution)/shard_map/all_gather | solution.py:71
  379.8 113.0 %reduce-scatter.45.cloned.1.call-start = ((), (), s32[]{:S(2)}) async-start(), calls=%async_computation.45 | async-start | bytes 1966080 | tf_op jit(solution)/shard_map/reduce_scatter | solution.py:75
  429.1 94.7 %reduce-scatter.37.cloned.1.call-start = ((), (), s32[]{:S(2)}) async-start(), calls=%async_computation.37 | async-start | bytes 1966080 | tf_op jit(solution)/shard_map/reduce_scatter | solution.py:75
  471.8 83.1 %reduce-scatter.19.cloned.1.call-start = ((), (), s32[]{:S(2)}) async-start(), calls=%async_computation.19 | async-start | bytes 1966080 | tf_op jit(solution)/shard_map/reduce_scatter | solution.py:65
  475.6 110.5 %reduce-scatter.23.cloned.1.call-start = ((), (), s32[]{:S(2)}) async-start(), calls=%async_computation.23 | async-start | bytes 1966080 | tf_op jit(solution)/shard_map/reduce_scatter | solution.py:65
  479.3 131.0 %all-gather.35.cloned.1.call-start = ((), (), s32[]{:S(2)}) async-start(), calls=%async_computation.34 | async-start | bytes 1966080 | tf_op jit(solution)/shard_map/all_gather | solution.py:71
  591.8 115.7 %all-gather.47.cloned.1.call-start = ((), (), s32[]{:S(2)}) async-start(), calls=%async_computation.46 | async-start | bytes 1966080 | tf_op jit(solution)/shard_map/all_gather | solution.py:71
  594.2 217.5 %reduce-scatter.35.cloned.1.call-start = ((), (), s32[]{:S(2)}) async-start(), calls=%async_computation.35 | async-start | bytes 1966080 | tf_op jit(solution)/shard_map/reduce_scatter | solution.py:75
  707.4 104.3 %reduce-scatter.43.cloned.1.call-start = ((), (), s32[]{:S(2)}) async-start(), calls=%async_computation.43 | async-start | bytes 1966080 | tf_op jit(solution)/shard_map/reduce_scatter | solution.py:75
  763.0 77.0 %reduce-scatter.47.cloned.1.call-start = ((), (), s32[]{:S(2)}) async-start(), calls=%async_computation.47 | async-start | bytes 1966080 | tf_op jit(solution)/shard_map/reduce_scatter | solution.py:75
  774.6 118.0 %reduce-scatter.31.cloned.1.call-start = ((), (), s32[]{:S(2)}) async-start(), calls=%async_computation.31 | async-start | bytes 1966080 | tf_op jit(solution)/shard_map/reduce_scatter | solution.py:65
  776.8 124.4 %reduce-scatter.27.cloned.1.call-start = ((), (), s32[]{:S(2)}) async-start(), calls=%async_computation.27 | async-start | bytes 1966080 | tf_op jit(solution)/shard_map/reduce_scatter | solution.py:65
  780.3 357.4 %all-reduce.4.cloned.1.call-start = ((), (), s32[]{:S(2)}) async-start(), calls=%async_computation.48 | async-start | bytes 14155776 | tf_op jit(solution)/shard_map/psum | solution.py:81
  (213 other events, 3654.9 us)
Sparse Core Ops, SparseCore 0:
  11.6 22.3 all-gather.20
  36.1 19.6 all-gather.16
  102.2 27.9 reduce-scatter.16
  133.2 27.9 reduce-scatter.20
  164.3 27.9 reduce-scatter.24
  195.4 27.9 reduce-scatter.28
  228.5 19.6 all-gather.26
  250.1 19.6 all-gather.40
  293.0 19.6 all-gather.32
  315.8 27.9 reduce-scatter.40
  346.8 28.0 reduce-scatter.32
  399.3 19.6 all-gather.44
  442.0 19.6 all-gather.36
  464.8 27.9 reduce-scatter.44
  495.8 28.0 reduce-scatter.36
  526.9 27.9 reduce-scatter.18
  558.0 28.0 reduce-scatter.22
  707.5 27.9 reduce-scatter.34
  749.8 27.9 reduce-scatter.42
  781.0 27.9 reduce-scatter.38
  811.9 27.9 reduce-scatter.46
  842.5 27.9 reduce-scatter.30
  873.1 28.0 reduce-scatter.26
  906.1 231.5 all-reduce.3
  (9 shorter events, 176.1 us)
where the time goes:
time: 1160 us; the launch traced here: 1150 us
  waiting for transfers between devices  673 us (58%)
  matrix products  258 us (22%)
  other arithmetic  118 us (10%)
  local copies, waits for them, and re-layouts  44.3 us (4%)
  blocking collectives  39.6 us (3%)
  between operations  17.3 us (1%)
    psum x1, waiting for transfers between devices, reduce_whole(): return lax.psum((totals[0], totals[1], totals[2], totals[3]), 'dp')  230 us
    reduce_scatter x8, waiting for transfers between devices, branch_sum(): lax.psum_scatter(partial_value.astype(jnp.bfloat16), 'tensor', scatter_di...  131 us
    reduce_scatter x8, waiting for transfers between devices, scatter_grads(): lax.psum_scatter(partial_value.astype(jnp.bfloat16), 'tensor', scatter_di...  125 us
    all_gather x8, waiting for transfers between devices, gather_rows(): return lax.all_gather(normed, 'tensor', axis=0, tiled=True)  99.6 us
    all_gather x8, waiting for transfers between devices, gather_grads(): return lax.all_gather(gradient, 'tensor', axis=0, tiled=True)  82 us
    dot_general x4, matrix products, attend_backward(): jnp.einsum('qhd,khd->hqk', grad_mixed, values_seq, preferred_element_type...  39.7 us
    psum x1, blocking collectives, local(): gain_totals = lax.psum((gain_one_acc, gain_two_acc), ('dp', 'tensor'))  39.6 us
    convert_element_type x4, other arithmetic, attend_backward(): grad_scores = (weights_soft * (grad_soft - inner_sum)).astype(jnp.bfloat16)  37.7 us
  transfers between devices with their start and end apart: 33, of which 25 were waited for; matrix products, arithmetic and copies ran while one was open for 32% of the time, Pallas kernels for 0%

commit v1 on v0

v1 whole, which is shorter than its diff:
```python
import functools
import jax
import jax.numpy as jnp
import numpy as np
from jax import lax
from jax.experimental import pallas as pl
from jax.experimental.pallas import tpu as pltpu
from jax.sharding import PartitionSpec as P

HD = 64
LEN = 1024
PIECE = 256
HALF = 512
EPS = 1e-06
F32 = jnp.float32
BF16 = jnp.bfloat16
VMEM_LIMIT = 60 * 1024 * 1024


def nn(a, b):
    return lax.dot_general(a, b, (((1,), (0,)), ((), ())), preferred_element_type=F32)


def nt(a, b):
    return lax.dot_general(a, b, (((1,), (1,)), ((), ())), preferred_element_type=F32)


def call(body, name, out_shape, args, flops, trans=0, **kw):
    read = sum(int(np.prod(a.shape)) * a.dtype.itemsize for a in args)
    made = sum(int(np.prod(o.shape)) * np.dtype(o.dtype).itemsize for o in out_shape)
    return pl.pallas_call(
        body,
        name=name,
        out_shape=out_shape,
        compiler_params=pltpu.CompilerParams(vmem_limit_bytes=VMEM_LIMIT),
        cost_estimate=pl.CostEstimate(
            flops=int(flops), bytes_accessed=read + made, transcendentals=int(trans)
        ),
        **kw,
    )(*args)


def struct(shape, dtype):
    return jax.ShapeDtypeStruct(shape, dtype)


def project(n1_ref, weights, cos_ref, sin_ref, q_ref, k_ref, v_ref):
    step = 256
    for block in range(LEN // step):
        cols = slice(block * step, (block + 1) * step)
        rows = n1_ref[cols, :]
        cosine = cos_ref[:, cols]
        sine = sin_ref[:, cols]
        for slot, w_ref in enumerate(weights):
            for part, ref in ((0, q_ref), (1, k_ref), (2, v_ref)):
                made = nt(w_ref[part], rows)
                for head in range(3):
                    low = made[head * HD : head * HD + HD // 2]
                    high = made[head * HD + HD // 2 : (head + 1) * HD]
                    if part < 2:
                        low, high = low * cosine - high * sine, high * cosine + low * sine
                    if part == 0:
                        low, high = low * HD**-0.5, high * HD**-0.5
                    at = slot * HD
                    ref[head, at : at + HD // 2, cols] = low.astype(BF16)
                    ref[head, at + HD // 2 : at + HD, cols] = high.astype(BF16)


def in_order(here, pieces, ref):
    step = ref.shape[0] // 4
    for quarter in range(4):
        for slot, piece in enumerate(pieces):

            @pl.when((here ^ slot) == quarter)
            def _():
                ref[quarter * step : (quarter + 1) * step, :] = piece[...]


def project_first_body(meta_ref, p0, p1, p2, p3, gain_ref, w0, w1, cos_ref, sin_ref, x_ref, n1_ref, q_ref, k_ref, v_ref):
    step = 256
    gain = gain_ref[...]
    in_order(meta_ref[2], (p0, p1, p2, p3), x_ref)
    for block in range(LEN // step):
        rows = slice(block * step, (block + 1) * step)
        x = x_ref[rows, :].astype(F32)
        scale = lax.rsqrt(jnp.mean(x * x, axis=-1, keepdims=True) + EPS)
        n1_ref[rows, :] = (x * scale * gain).astype(BF16)
    project(n1_ref, (w0, w1), cos_ref, sin_ref, q_ref, k_ref, v_ref)


def project_next_body(n1_ref, w0, w1, cos_ref, sin_ref, q_ref, k_ref, v_ref):
    project(n1_ref, (w0, w1), cos_ref, sin_ref, q_ref, k_ref, v_ref)


HEADS3 = (3, 2 * HD, LEN)


VM = pl.BlockSpec(memory_space=pltpu.VMEM)
SM = pl.BlockSpec(memory_space=pltpu.SMEM)


def project_first(meta, pieces, gain, w0, w1, cosine, sine):
    width = gain.shape[1]
    out = [struct((LEN, width), BF16)] * 2 + [struct(HEADS3, BF16)] * 3
    args = (meta, *pieces, gain, w0, w1, cosine, sine)
    return call(
        project_first_body,
        "project_first",
        out,
        args,
        2 * LEN * width * 18 * HD,
        in_specs=[SM] + [VM] * (len(args) - 1),
        out_specs=[VM] * len(out),
    )


def project_next(n1, w0, w1, cosine, sine):
    width = n1.shape[1]
    out = [struct(HEADS3, BF16)] * 3
    return call(project_next_body, "project_next", out, (n1, w0, w1, cosine, sine), 2 * LEN * width * 18 * HD)


def limits(starts_ref):
    pos = lax.broadcasted_iota(jnp.int32, (1, LEN), 1)
    lim = pos
    for piece in range(2):
        first = starts_ref[piece]
        lim = jnp.where((pos >= first) & (pos < first + PIECE), first + PIECE - 1, lim)
    return lim


def one_head(block, head):
    zero = jnp.zeros((HD, block.shape[1]), block.dtype)
    part = block[head * HD : (head + 1) * HD]
    return jnp.concatenate([part, zero] if head == 0 else [zero, part], axis=0)


NEG = -1e30


def attend_body(qb, starts_ref, q_ref, k_ref, v_ref, mt_ref, m_ref, lse_ref):
    lim = limits(starts_ref)
    k_rows = k_ref[0].T
    for head in range(2):
        q_one = one_head(q_ref[0], head)
        v_one = v_ref[0, head * HD : (head + 1) * HD, :]
        for block in range(LEN // qb):
            cols = slice(block * qb, (block + 1) * qb)
            keys = HALF if (block + 1) * qb <= HALF else LEN
            scores = nn(k_rows[:keys], q_one[:, cols])
            edge = scores[keys - HALF :]
            pos = lax.broadcasted_iota(jnp.int32, (HALF, qb), 0) + (keys - HALF)
            edge = jnp.where(pos <= lim[:, cols], edge, NEG)
            most = jnp.max(edge, axis=0, keepdims=True)
            if keys > HALF:
                body = scores[:HALF]
                most = jnp.maximum(most, jnp.max(body, axis=0, keepdims=True))
            soft = jnp.exp(edge - most)
            total = jnp.sum(soft, axis=0, keepdims=True)
            mixed = nn(v_one[:, keys - HALF : keys], soft.astype(BF16))
            if keys > HALF:
                soft = jnp.exp(body - most)
                total = total + jnp.sum(soft, axis=0, keepdims=True)
                mixed = mixed + nn(v_one[:, :HALF], soft.astype(BF16))
            mt_ref[0, head * HD : (head + 1) * HD, cols] = (mixed * (1.0 / total)).astype(BF16)
            lse_ref[0, head : head + 1, cols] = most + jnp.log(total)
    m_ref[...] = mt_ref[0].T


def attend(starts, q, k, v, qb=256):
    block = pl.BlockSpec((1, 2 * HD, LEN), lambda i: (i, 0, 0))
    out = [struct(HEADS3, BF16), struct((LEN, 6 * HD), BF16), struct((3, 2, LEN), F32)]
    return call(
        functools.partial(attend_body, qb),
        "attend",
        out,
        (starts, q, k, v),
        6 * 2 * LEN * LEN * 256 * 2 * 0.75,
        6 * LEN * LEN * 0.75,
        grid=(3,),
        in_specs=[pl.BlockSpec(memory_space=pltpu.SMEM), block, block, block],
        out_specs=[
            block,
            pl.BlockSpec((LEN, 2 * HD), lambda i: (0, i)),
            pl.BlockSpec((1, 2, LEN), lambda i: (i, 0, 0)),
        ],
    )


def attend_back_body(qb, starts_ref, cos_ref, sin_ref, n1_ref, *refs):
    sets = (refs[0:5], refs[5:10])
    do_ref = refs[10]
    dt_ref, dw_ref, acc_ref = refs[11:]
    lim = limits(starts_ref)
    for which, (q_ref, k_ref, v_ref, mt_ref, lse_ref) in enumerate(sets):
        q = q_ref[0]
        k = k_ref[0]
        v = v_ref[0]
        do = do_ref[which * 2 * HD : (which + 1) * 2 * HD, :]
        k_rows = k.T
        v_rows = v.T
        both = do.astype(F32) * mt_ref[0].astype(F32)
        for head in range(2):
            mine = slice(head * HD, (head + 1) * HD)
            inner = jnp.sum(both[mine], axis=0, keepdims=True)
            q_one = one_head(q, head)
            do_one = one_head(do, head)
            lse = lse_ref[0, head : head + 1, :]
            for block in range(LEN // qb):
                cols = slice(block * qb, (block + 1) * qb)
                wide = (block + 1) * qb > HALF
                dq = None
                for part in range(2 if wide else 1):
                    keys = slice(part * HALF, (part + 1) * HALF)
                    scores = nn(k_rows[keys], q_one[:, cols])
                    if part == (1 if wide else 0):
                        pos = lax.broadcasted_iota(jnp.int32, (HALF, qb), 0) + part * HALF
                        scores = jnp.where(pos <= lim[:, cols], scores, NEG)
                    soft = jnp.exp(scores - lse[:, cols])
                    grad = nn(v_rows[keys], do_one[:, cols])
                    grad = (soft * (grad - inner[:, cols])).astype(BF16)
                    more = nn(k[mine, keys], grad)
                    dq = more if dq is None else dq + more
                    dk = nt(q[mine, cols], grad)
                    dv = nt(do[mine, cols], soft.astype(BF16))
                    fresh = block == (0 if part == 0 else HALF // qb)
                    if fresh:
                        acc_ref[1, mine, keys] = dk
                        acc_ref[2, mine, keys] = dv
                    else:
                        acc_ref[1, mine, keys] += dk
                        acc_ref[2, mine, keys] += dv
                acc_ref[0, mine, cols] = dq * HD**-0.5
        cosine = cos_ref[...]
        sine = sin_ref[...]
        for part in range(3):
            for head in range(2):
                at = head * HD
                low = acc_ref[part, at : at + HD // 2, :]
                high = acc_ref[part, at + HD // 2 : at + HD, :]
                if part < 2:
                    low, high = low * cosine + high * sine, high * cosine - low * sine
                to = which * 2 * HD + at
                dt_ref[part, to : to + HD // 2, :] = low.astype(BF16)
                dt_ref[part, to + HD // 2 : to + HD, :] = high.astype(BF16)
    for part in range(3):
        made = nn(dt_ref[part], n1_ref[...])
        for slot in range(4):
            dw_ref[slot, part] = made[slot * HD : (slot + 1) * HD].astype(BF16)


def attend_back(turn, starts, cosine, sine, n1, sets, do, qb=256):
    width = n1.shape[1]
    head = pl.BlockSpec((1, 2 * HD, LEN), lambda i: (turn, 0, 0))
    full = lambda a: pl.BlockSpec(a.shape, lambda i, n=a.ndim: (0,) * n)
    lse = pl.BlockSpec((1, 2, LEN), lambda i: (turn, 0, 0))
    args = (starts, cosine, sine, n1, *sets[0], *sets[1], do)
    out = [struct((3, 4 * HD, LEN), BF16), struct((4, 3, HD, width), BF16)]
    return call(
        functools.partial(attend_back_body, qb),
        "attend_back",
        out,
        args,
        4 * 5 * LEN * LEN * 256 * 2 * 0.75 + 2 * LEN * width * 12 * HD,
        4 * LEN * LEN * 0.75,
        grid=(1,),
        in_specs=[pl.BlockSpec(memory_space=pltpu.SMEM), full(cosine), full(sine), full(n1)]
        + [head, head, head, head, lse] * 2
        + [pl.BlockSpec((4 * HD, LEN), lambda i: (turn, 0))],
        out_specs=[full(o) for o in out],
        scratch_shapes=[pltpu.VMEM((3, 2 * HD, LEN), F32)],
    )


def turn_rows(w_refs):
    return jnp.concatenate(
        [w[turn * HD : (turn + 1) * HD, :] for turn in range(3) for w in w_refs], axis=0
    )


def after_body(
    meta_ref, x_ref, ma_ref, mb_ref, w0, w1, w2, w3, gain_ref, g0, g1, g2, g3,
    after_ref, n2_ref, n2t_ref, g_ref, gt_ref,
):
    slot = pl.program_id(0) ^ meta_ref[2]
    for which, piece in enumerate((g0, g1, g2, g3)):

        @pl.when(slot == which)
        def _():
            g_ref[...] = piece[...]

    first = turn_rows((w0, w1))
    second = turn_rows((w2, w3))
    after = x_ref[...].astype(F32) + nn(ma_ref[...], first) + nn(mb_ref[...], second)
    after_ref[...] = after
    scale = lax.rsqrt(jnp.mean(after * after, axis=-1, keepdims=True) + EPS)
    normed = (after * scale * gain_ref[...]).astype(BF16)
    n2_ref[...] = normed
    n2t_ref[...] = normed.T
    gt_ref[...] = g_ref[...].T


def after_attention(meta, x, mixed_a, mixed_b, wo, gain, g):
    width = x.shape[1]
    step = 256
    rows = lambda n: pl.BlockSpec((step, n), lambda i: (i, 0))
    cols = pl.BlockSpec((width, step), lambda i: (0, i))
    full = lambda a: pl.BlockSpec(a.shape, lambda i, n=a.ndim: (0,) * n)
    args = (meta, x, mixed_a, mixed_b, *wo, gain, *g)
    out = [
        struct((LEN, width), F32),
        struct((LEN, width), BF16),
        struct((width, LEN), BF16),
        struct((LEN, width), BF16),
        struct((width, LEN), BF16),
    ]
    return call(
        after_body,
        "after_attention",
        out,
        args,
        2 * LEN * width * width,
        grid=(LEN // step,),
        in_specs=[SM, rows(width), rows(6 * HD), rows(6 * HD)]
        + [full(w) for w in wo]
        + [full(gain)]
        + [full(p) for p in g],
        out_specs=[rows(width), rows(width), cols, rows(width), cols],
    )


def mlp_body(split, meta_ref, n2_ref, n2t_ref, g_ref, gt_ref, *refs):
    block = 256
    step = 256
    if split:
        gua0, gub0, gua1, gub1, wda0, wdb0, wda1, wdb1 = refs[:8]
        out_ref, back_ref, dw0, dw1, hid, dga, dup, gus, wds = refs[8:]
        bit = meta_ref[3]
        for slot, (one, two) in enumerate(((gua0, gub0), (gua1, gub1))):
            gus[slot, bit] = one[0]
            gus[slot, 1 - bit] = two[0]
        for slot, (one, two) in enumerate(((wda0, wdb0), (wda1, wdb1))):
            wds[slot, bit] = one[0]
            wds[slot, 1 - bit] = two[0]
        take_gu = lambda slot, which, cols: gus[slot, which, :, cols]
        take_wd = lambda slot, part: wds[slot, part]
    else:
        gu0, gu1, wd0, wd1 = refs[:4]
        out_ref, back_ref, dw0, dw1, hid, dga, dup = refs[4:]
        take_gu = lambda slot, which, cols: (gu0, gu1)[slot][which, :, cols]
        take_wd = lambda slot, part: (wd0, wd1)[slot][part]
    out_ref[...] = jnp.zeros_like(out_ref)
    back_ref[...] = jnp.zeros_like(back_ref)
    for slot, dw_ref in ((1, dw1), (0, dw0)):
        for part in range(2):
            cols = slice(part * block, (part + 1) * block)
            wg = take_gu(slot, 0, cols)
            wu = take_gu(slot, 1, cols)
            wl = take_wd(slot, part)

            @pl.loop(0, LEN // step)
            def _(turn):
                rows = pl.ds(pl.multiple_of(turn * step, step), step)
                n2 = n2_ref[rows, :]
                gate = nn(n2, wg)
                up = nn(n2, wu)
                grad = nt(g_ref[rows, :], wl)
                sigma = 1.0 / (1.0 + jnp.exp(-gate))
                silu = gate * sigma
                hidden = (silu * up).astype(BF16)
                grad_up = (grad * silu).astype(BF16)
                grad_gate = (grad * up * (sigma * (1.0 + gate * (1.0 - sigma)))).astype(BF16)
                hid[rows, :] = hidden
                dga[rows, :] = grad_gate
                dup[rows, :] = grad_up
                out_ref[rows, :] += nn(hidden, wl)
                back_ref[rows, :] += nt(grad_gate, wg) + nt(grad_up, wu)

            dw_ref[0, :, cols] = nn(n2t_ref[...], dga[...]).astype(BF16)
            dw_ref[1, :, cols] = nn(n2t_ref[...], dup[...]).astype(BF16)
            dw_ref[2, :, cols] = nn(gt_ref[...], hid[...]).astype(BF16)


def mlp(meta, n2, n2t, g, gt, weights):
    width = n2.shape[1]
    split = len(weights) == 8
    units = 512
    out = [
        struct((LEN, width), F32),
        struct((LEN, width), F32),
        struct((3, width, units), BF16),
        struct((3, width, units), BF16),
    ]
    args = (meta, n2, n2t, g, gt, *weights)
    scratch = [pltpu.VMEM((LEN, 256), BF16)] * 3
    if split:
        scratch += [pltpu.VMEM((2, 2, width, units), BF16), pltpu.VMEM((2, 2, units // 2, width), BF16)]
    return call(
        functools.partial(mlp_body, split),
        "mlp",
        out,
        args,
        2 * LEN * width * units * 2 * 9,
        LEN * units * 2,
        in_specs=[SM] + [VM] * (len(args) - 1),
        out_specs=[VM] * 4,
        scratch_shapes=scratch,
    )


def norm_back(grad, value, gain):
    scale = lax.rsqrt(jnp.mean(value * value, axis=-1, keepdims=True) + EPS)
    unit = value * scale
    gain_grad = jnp.sum(grad * unit, axis=0, keepdims=True)
    e = grad * gain
    return scale * (e - unit * jnp.mean(e * unit, axis=-1, keepdims=True)), gain_grad


def give(meta_ref, value, refs):
    slot = pl.program_id(0) ^ meta_ref[2]
    for which, ref in enumerate(refs):

        @pl.when(slot == which)
        def _():
            ref[...] = value


def middle_body(
    meta_ref, x_ref, after_ref, oa_ref, ob_ref, ba_ref, bb_ref, g_ref, gain_ref, mta_ref, mtb_ref,
    w0, w1, w2, w3, e0, e1, e2, e3, da_ref, do_ref, dwo_ref, gain_out, acc,
):
    step = pl.program_id(0)
    after = after_ref[...]
    delta = (after - x_ref[...].astype(F32) + oa_ref[...] + ob_ref[...]).astype(BF16)
    give(meta_ref, delta, (e0, e1, e2, e3))
    back, gain_grad = norm_back(ba_ref[...] + bb_ref[...], after, gain_ref[...])
    grad_after = g_ref[...].astype(F32) + back
    da_ref[...] = grad_after
    low = grad_after.astype(BF16)

    @pl.when(step == 0)
    def _():
        gain_out[...] = jnp.zeros_like(gain_out)
        acc[...] = jnp.zeros_like(acc)

    gain_out[...] += gain_grad
    weights = turn_rows((w0, w1, w2, w3))
    do_ref[...] = nt(weights, low).astype(BF16)
    for turn in range(3):
        for which, mt in enumerate((mta_ref, mtb_ref)):
            acc[turn, which] += nn(mt[turn], low)

    @pl.when(step == pl.num_programs(0) - 1)
    def _():
        for turn in range(3):
            for slot in range(4):
                at = (slot % 2) * HD
                dwo_ref[slot, turn] = acc[turn, slot // 2, at : at + HD, :].astype(BF16)


def middle(meta, x, after, outs, backs, g, gain, mts, wo):
    width = x.shape[1]
    step = 256
    rows = pl.BlockSpec((step, width), lambda i: (i, 0))
    full = lambda a: pl.BlockSpec(a.shape, lambda i, n=a.ndim: (0,) * n)
    heads = pl.BlockSpec((3, 2 * HD, step), lambda i: (0, 0, i))
    args = (meta, x, after, *outs, *backs, g, gain, *mts, *wo)
    out = [struct((step, width), BF16)] * 4 + [
        struct((LEN, width), F32),
        struct((12 * HD, LEN), BF16),
        struct((4, 3, HD, width), BF16),
        struct((1, width), F32),
    ]
    return call(
        middle_body,
        "middle",
        out,
        args,
        4 * LEN * width * width,
        grid=(LEN // step,),
        in_specs=[SM] + [rows] * 7 + [full(gain), heads, heads] + [full(w) for w in wo],
        out_specs=[full(o) for o in out[:4]]
        + [rows, pl.BlockSpec((12 * HD, step), lambda i: (0, i)), full(out[6]), full(out[7])],
        scratch_shapes=[pltpu.VMEM((3, 2, 2 * HD, width), F32)],
    )


def token_grad_body(turns, last, *refs):
    dts = refs[: len(turns)]
    weights = refs[len(turns) : len(turns) + 4]
    rest = refs[len(turns) + 4 :]
    step = pl.program_id(0)
    total = None
    for turn, dt in zip(turns, dts):
        for part in range(3):
            w = jnp.concatenate([w[part, turn * HD : (turn + 1) * HD, :] for w in weights], axis=0)
            more = nn(dt[part].T, w)
            total = more if total is None else total + more
    if not last:
        rest[0][...] = total
        return
    meta_ref, before_ref, x_ref, da_ref, g_ref, gain_ref, e0, e1, e2, e3, gain_out = rest
    total = total + before_ref[...]
    back, gain_grad = norm_back(total, x_ref[...].astype(F32), gain_ref[...])
    give(meta_ref, (da_ref[...] - g_ref[...].astype(F32) + back).astype(BF16), (e0, e1, e2, e3))

    @pl.when(step == 0)
    def _():
        gain_out[...] = jnp.zeros_like(gain_out)

    gain_out[...] += gain_grad


def token_grad(turns, dts, weights, rest=None):
    width = weights[0].shape[2]
    step = 256
    rows = pl.BlockSpec((step, width), lambda i: (i, 0))
    full = lambda a: pl.BlockSpec(a.shape, lambda i, n=a.ndim: (0,) * n)
    cols = pl.BlockSpec((3, 4 * HD, step), lambda i: (0, 0, i))
    specs = [cols] * len(dts) + [full(w) for w in weights]
    args = (*dts, *weights)
    if rest is None:
        out = [struct((LEN, width), F32)]
        out_specs = [rows]
    else:
        out = [struct((step, width), BF16)] * 4 + [struct((1, width), F32)]
        out_specs = [full(o) for o in out]
        specs = specs + [SM] + [rows] * 4 + [full(rest[5])]
        args = args + tuple(rest)
    return call(
        functools.partial(token_grad_body, turns, rest is not None),
        "token_grad",
        out,
        args,
        2 * LEN * width * 12 * HD * len(turns),
        grid=(LEN // step,),
        in_specs=specs,
        out_specs=out_specs,
    )


def rope_tables(length, width):
    halfway = width // 2
    inverse = 10000.0 ** (-jnp.arange(halfway, dtype=F32) * 2.0 / width)
    angles = inverse[:, None] * jnp.arange(length, dtype=F32)[None, :]
    return jnp.cos(angles), jnp.sin(angles)


def swap(value, axis, size, mask):
    return lax.ppermute(value, axis, [(i, i ^ mask) for i in range(size)])


def sum_split_body(n, count, index_ref, *refs):
    ins, outs = refs[:count], refs[count:]
    total = ins[0][0].astype(F32)
    for ref in ins[1:]:
        total = total + ref[0].astype(F32)
    total = total.astype(BF16)
    slot = pl.program_id(0) ^ index_ref[0]
    for which, ref in enumerate(outs):

        @pl.when(slot == which)
        def _():
            ref[...] = total


def sum_split(addends, n, index):
    rows, cols = addends[0].shape
    parts = [a.reshape(n, rows // n, cols) for a in addends]
    out = [struct((rows // n, cols), BF16)] * n
    full = pl.BlockSpec((rows // n, cols), lambda i: (0, 0))
    return call(
        functools.partial(sum_split_body, n, len(addends)),
        "sum_split",
        out,
        (index.reshape(1), *parts),
        rows * cols * len(addends),
        grid=(n,),
        in_specs=[SM] + [pl.BlockSpec((1, rows // n, cols), lambda i: (i, 0, 0))] * len(addends),
        out_specs=[full] * n,
    )


def join_body(index_ref, *refs):
    slot = pl.program_id(0) ^ index_ref[0]
    for which, ref in enumerate(refs[:-1]):

        @pl.when(slot == which)
        def _():
            refs[-1][0] = ref[...]


def join(pieces, index):
    n = len(pieces)
    rows, cols = pieces[0].shape
    full = pl.BlockSpec((rows, cols), lambda i: (0, 0))
    made = call(
        join_body,
        "join",
        [struct((n, rows, cols), BF16)],
        (index.reshape(1), *pieces),
        rows * cols * n,
        grid=(n,),
        in_specs=[SM] + [full] * n,
        out_specs=[pl.BlockSpec((1, rows, cols), lambda i: (i, 0, 0))],
    )[0]
    return made.reshape(n * rows, cols)


def stages_of(size, widths):
    bits = size.bit_length() - 1
    out = []
    shift = 0
    for width in widths:
        width = min(width, bits - shift)
        if width > 0:
            out.append((shift, 1 << width))
            shift += width
    while shift < bits:
        width = min(widths[-1], bits - shift)
        out.append((shift, 1 << width))
        shift += width
    return out


def scatter_sum(addends, stages, here, size, keep_last=False):
    for shift, n in stages:
        index = (here >> shift) & (n - 1)
        pieces = sum_split(addends, n, index)
        addends = [pieces[0]] + [swap(pieces[j], "dp", size, j << shift) for j in range(1, n)]
    return sum_split(addends, 1, jnp.zeros_like(here))[0]


def gather_stage(piece, stage, here, size):
    shift, n = stage
    return [piece] + [swap(piece, "dp", size, j << shift) for j in range(1, n)]


def gather_all(piece, stages, here, size):
    for shift, n in reversed(stages):
        index = (here >> shift) & (n - 1)
        piece = join(gather_stage(piece, (shift, n), here, size), index)
    return piece


def add_home_body(meta_ref, in_ref, p0, p1, p2, p3, out_ref):
    slot = pl.program_id(0) ^ meta_ref[2]
    for which, piece in enumerate((p0, p1, p2, p3)):

        @pl.when(slot == which)
        def _():
            out_ref[0] = in_ref[0] + piece[...].astype(F32)


def add_home(meta, base, pieces):
    count, rows, width = base.shape
    block = pl.BlockSpec((1, rows, width), lambda i: (i, 0, 0))
    full = pl.BlockSpec((rows, width), lambda i: (0, 0))
    return call(
        add_home_body,
        "add_home",
        [struct(base.shape, F32)],
        (meta, base, *pieces),
        base.size,
        grid=(count,),
        in_specs=[SM, block] + [full] * 4,
        out_specs=[block],
    )[0]


def mlp_out_body(pair_ref, last_ref, gu_ref, wd_ref):
    step = pl.program_id(0)

    @pl.when(step < 4)
    def _():
        gu_ref[...] = pair_ref[...].astype(F32)

    @pl.when(step >= 4)
    def _():
        wd_ref[...] = last_ref[...].astype(F32).T


def mlp_out(whole, width, units):
    rows = width // 2
    return call(
        mlp_out_body,
        "mlp_out",
        [struct((2 * width, units), F32), struct((units, width), F32)],
        (whole, whole),
        whole.size,
        grid=(6,),
        in_specs=[
            pl.BlockSpec((rows, units), lambda i: (jnp.minimum(i, 3), 0)),
            pl.BlockSpec((rows, units), lambda i: (jnp.maximum(i, 4), 0)),
        ],
        out_specs=[
            pl.BlockSpec((rows, units), lambda i: (jnp.minimum(i, 3), 0)),
            pl.BlockSpec((units, rows), lambda i: (0, jnp.maximum(i - 4, 0))),
        ],
    )


def attn_out_body(early_ref, late_ref, qkv_ref, wo_ref):
    wo_ref[...] = early_ref[: 3 * HD, :].astype(F32)
    for part in range(3):
        at = part * HD
        parts = [early_ref[3 * HD + at : 3 * HD + at + HD, :], early_ref[6 * HD + at : 6 * HD + at + HD, :]]
        parts.append(late_ref[at : at + HD, :])
        qkv_ref[part] = jnp.concatenate(parts, axis=0).astype(F32).T


def attn_out(early, late):
    width = early.shape[1]
    return call(
        attn_out_body,
        "attn_out",
        [struct((3, width, 3 * HD), F32), struct((3 * HD, width), F32)],
        (early, late),
        early.size,
    )


def sum_all_body(count, index_ref, *refs):
    hold = refs[-1]
    for which in range(count):
        hold[index_ref[0] ^ which] = refs[which][...]
    total = hold[0]
    for which in range(1, count):
        total = total + hold[which]
    refs[count][...] = total


def sum_all(value, axis, size, stages, here):
    for shift, n in stages:
        index = (here >> shift) & (n - 1)
        pieces = [value] + [swap(value, axis, size, j << shift) for j in range(1, n)]
        value = call(
            functools.partial(sum_all_body, n),
            "sum_all",
            [struct(value.shape, F32)],
            (index.reshape(1), *pieces),
            value.size * n,
            in_specs=[SM] + [VM] * n,
            out_specs=[VM],
            scratch_shapes=[pltpu.VMEM((n,) + value.shape, F32)],
        )[0]
    return value


def send_home(pieces, size):
    return [pieces[0]] + [swap(pieces[k], "tensor", size, k) for k in range(1, 4)]


def local(n_dp, inputs, w_qkv, w_out, w_gate_up, w_down, gain_attn, gain_mlp, piece_starts, out_grad):
    width = inputs.shape[2]
    units = w_down.shape[0]
    here = lax.axis_index("tensor").astype(jnp.int32)
    row = lax.axis_index("dp").astype(jnp.int32)
    bit = row & 1
    mine = lax.dynamic_index_in_dim(piece_starts, here, 0, keepdims=False)[0]
    meta = jnp.concatenate([mine, jnp.stack([here, bit])])
    one = gain_attn[None]
    two = gain_mlp[None]
    cosine, sine = rope_tables(LEN, HD)
    tensor = functools.partial(swap, axis="tensor", size=4)

    def quarters(whole):
        picks = [
            lax.dynamic_index_in_dim(whole, here ^ k, 0, keepdims=False).astype(BF16) for k in range(4)
        ]
        return [picks[0]] + [tensor(picks[k], mask=k) for k in range(1, 4)]

    xs = quarters(inputs)
    wq0 = jnp.swapaxes(w_qkv, 1, 2).astype(BF16)
    wq1 = tensor(wq0, mask=1)
    wq2 = tensor(wq0, mask=2)
    wq3 = tensor(wq2, mask=1)
    wo0 = w_out.astype(BF16)
    wo1 = tensor(wo0, mask=1)
    wo2 = tensor(wo0, mask=2)
    wo3 = tensor(wo2, mask=1)
    gs = quarters(out_grad)
    wq = (wq0, wq1, wq2, wq3)
    wo = (wo0, wo1, wo2, wo3)
    gu0 = w_gate_up.astype(BF16)
    wd0 = w_down.astype(BF16).reshape(2, units // 2, width)
    gu1 = tensor(gu0, mask=1)
    wd1 = tensor(wd0, mask=1)

    def far(shard):
        half = lax.dynamic_slice_in_dim(shard, bit, 1, 0)
        direct = tensor(half, mask=2)
        round_about = swap(direct, "dp", n_dp, 1)
        return direct, round_about, tensor(direct, mask=1), tensor(round_about, mask=1)

    gu_far = far(gu0)
    wd_far = far(wd0)

    x, n1, qa, ka, va = project_first(meta, xs, one, wq0, wq1, cosine, sine)
    mta, ma, la = attend(meta, qa, ka, va)
    qb, kb, vb = project_next(n1, wq2, wq3, cosine, sine)
    mtb, mb, lb = attend(meta, qb, kb, vb)
    after, n2, n2t, g, gt = after_attention(meta, x, ma, mb, wo, two, gs)
    oa, ba, dw0, dw1 = mlp(meta, n2, n2t, g, gt, (gu0, gu1, wd0, wd1))
    in1 = tensor(dw1, mask=1)
    ob, bb, dw2, dw3 = mlp(meta, n2, n2t, g, gt, gu_far + wd_far)
    in3 = tensor(dw3, mask=1)
    middle_out = middle(meta, x, after, (oa, ob), (ba, bb), g, two, (mta, mtb), wo)
    back_home = send_home(middle_out[:4], 4)
    da, do, dwo, gain_two = middle_out[4:]
    flat = lambda a: a.reshape(-1, a.shape[-1])
    zero = jnp.zeros((), jnp.int32)
    wide = stages_of(n_dp, (1, 2))
    tall = stages_of(n_dp, (3, 3))
    low = sum_split([flat(dw2), flat(in3)], 1, zero)[0]
    piece = scatter_sum([flat(dw0), flat(in1), tensor(low, mask=2)], wide, row, n_dp)
    grad_pair, grad_down = mlp_out(gather_all(piece, wide, row, n_dp), width, units)
    sets = ((qa, ka, va, mta, la), (qb, kb, vb, mtb, lb))
    dts = []
    dws = []
    for turn in range(3):
        dt, dw = attend_back(turn, meta, cosine, sine, n1, sets, do)
        dts.append(dt)
        dws.append(dw)

    def core_sum(parts, stages):
        slots = [jnp.concatenate([flat(p[s]) for p in parts]) if len(parts) > 1 else flat(parts[0][s]) for s in range(4)]
        in1 = tensor(slots[1], mask=1)
        in3 = tensor(slots[3], mask=1)
        low = sum_split([slots[2], in3], 1, zero)[0]
        piece = scatter_sum([slots[0], in1, tensor(low, mask=2)], stages, row, n_dp)
        return gather_all(piece, stages, row, n_dp)

    early = core_sum((dwo, dws[0], dws[1]), wide)
    (before,) = token_grad((0, 1), dts[:2], wq)
    late = core_sum((dws[2],), tall)
    *grads, gain_one = token_grad((2,), dts[2:], wq, (meta, before, x, da, g, one))
    grad_home = send_home(grads, 4)
    gains = jnp.concatenate([gain_one, gain_two])
    gains = sum_all(gains, "tensor", 4, [(0, 4)], here)
    gains = sum_all(gains, "dp", n_dp, tall, row)
    grad_qkv, grad_out = attn_out(early, late)
    return (
        add_home(meta, inputs, back_home),
        add_home(meta, out_grad, grad_home),
        grad_qkv,
        grad_out,
        grad_pair.reshape(2, width, units),
        grad_down,
        gains[0],
        gains[1],
    )


def solution(mesh):
    rows = P(None, ("dp", "tensor"), None)
    weights = (P(None, None, "tensor"), P("tensor", None), P(None, None, "tensor"), P("tensor", None))
    return jax.shard_map(
        functools.partial(local, mesh.shape["dp"]),
        mesh=mesh,
        in_specs=(rows, *weights, P(), P(), P(None, "dp", None), rows),
        out_specs=(rows, rows, *weights, P(), P()),
        check_vma=False,
    )
```

time: 1160 us -> 516 us (0.44)
  waiting for transfers between devices: 673 us -> 142 us
  matrix products: 258 us -> 0 us
  Pallas kernels: 0 us -> 250 us
  other arithmetic: 118 us -> 12.2 us
  starting transfers between devices: 2.68 us -> 78.5 us
  blocking collectives: 39.6 us -> 0 us
  local copies, waits for them, and re-layouts: 44.3 us -> 25.5 us
  between operations: 17.3 us -> 1.38 us
    reduce_scatter x16 -> x0, waiting for transfers between devices: 256 us -> none  [the longest x8 131 us: branch_sum(): lax.psum_scatter(partial_value.astype(jnp.bfloat16), 'tensor', scatter_di...]
    pallas_call x0 -> x35, Pallas kernels: none -> 250 us  [call(): pl.pallas_call(body, name=name, out_shape=out_shape, compiler_params=pltp...]
    dot_general x68 -> x0, matrix products: 247 us -> none  [the longest x4 39.7 us: attend_backward(): jnp.einsum('qhd,khd->hqk', grad_mixed, values_seq, preferred_element_type...]
    psum x1 -> x0, waiting for transfers between devices: 230 us -> none  [reduce_whole(): return lax.psum((totals[0], totals[1], totals[2], totals[3]), 'dp')]
    all_gather x16 -> x0, waiting for transfers between devices: 182 us -> none  [the longest x8 99.6 us: gather_rows(): return lax.all_gather(normed, 'tensor', axis=0, tiled=True)]
    ppermute x0 -> x77, waiting for transfers between devices: none -> 142 us  [swap(): return lax.ppermute(value, axis, [(i, i ^ mask) for i in range(size)])]
    ppermute x0 -> x77, starting transfers between devices: none -> 78.5 us  [swap(): return lax.ppermute(value, axis, [(i, i ^ mask) for i in range(size)])]
    convert_element_type x12 -> x4, other arithmetic: 51.8 us -> 4.49 us  [the longest x1 2.09 us: local(): gu0 = w_gate_up.astype(BF16)]
  transfers between devices with their start and end apart: 33 -> 77, of which waited for: 25 -> 22; matrix products, arithmetic and copies ran while one was open for 32% -> 6% of each run, Pallas kernels for 0% -> 47%
where the time goes in v1:
time: 516 us; the launch traced here: 510 us
  Pallas kernels  250 us (48%)
  waiting for transfers between devices  142 us (28%)
  starting transfers between devices  78.5 us (15%)
  local copies, waits for them, and re-layouts  25.5 us (5%)
  other arithmetic  12.2 us (2%)
    pallas_call x35, Pallas kernels, call(): pl.pallas_call(body, name=name, out_shape=out_shape, compiler_params=pltp...  250 us
    ppermute x77, waiting for transfers between devices, swap(): return lax.ppermute(value, axis, [(i, i ^ mask) for i in range(size)])  142 us
    ppermute x77, starting transfers between devices, swap(): return lax.ppermute(value, axis, [(i, i ^ mask) for i in range(size)])  78.5 us
    unnamed x159, local copies, waits for them, and re-layouts  10.9 us
  transfers between devices with their start and end apart: 77, of which 22 were waited for; matrix products, arithmetic and copies ran while one was open for 6% of the time, Pallas kernels for 47%

profile of v1, /device:TPU:0, one launch (start us, length us, event | category | flops | bytes accessed | tf_op | source)
XLA Modules:
  0.0 509.5 jit_solution(15896871813075331835)
XLA Ops:
  14.6 33.6 %collective-permute-done.7.w2 = bf16[192,768]{1,0:T(8,128)(2,1)} collective-permute-done((bf16[192,768]{1,0:T(8,128)(2,1)}, bf16[192,768]{1,0:T(8,128)(2,1)}, u32[]{:S(2)}, u32[]{:S(2)}) %collective-permute-start.7) | collective-permute-done | bytes 294944 | tf_op jit(solution)/shard_map/ppermute | solution.py:550
  60.2 5.7 %collective-permute-done.2.p3 = bf16[256,768]{1,0:T(8,128)(2,1)S(1)} collective-permute-done((bf16[256,768]{1,0:T(8,128)(2,1)S(1)}, bf16[256,768]{1,0:T(8,128)(2,1)S(1)}, u32[]{:S(2)}, u32[]{:S(2)}) %collective-permute-start.2) | collective-permute-done | bytes 393248 | tf_op jit(solution)/shard_map/ppermute | solution.py:550
  69.2 6.7 %project_first.1 = (bf16[1024,768]{1,0:T(8,128)(2,1)}, bf16[1024,768]{1,0:T(8,128)(2,1)}, bf16[3,128,1024]{2,1,0:T(8,128)(2,1)}, bf16[3,128,1024]{2,1,0:T(8,128)(2,1)}, bf16[3,128,1024]{2,1,0:T(8,128)(2,1)}) custom-call(s32[4]{0:T(128)} %pad_add_fusion.meta_ref.starts_ref.refs_5_, bf16[256,768]{1,0:T(8,128)(2,1)} %get-tuple-element.165.p0, ...), custom_call_target="tpu_custom_call" | custom-call | flops 1811939328 | bytes 9112592 | tf_op jit(solution)/shard_map/project_first/pallas_call | solution.py:31
  78.6 7.8 %collective-permute-done.18.refs_4_ = bf16[1,256,768]{2,1,0:T(8,128)(2,1)} collective-permute-done((bf16[1,256,768]{2,1,0:T(8,128)(2,1)}, bf16[1,256,768]{2,1,0:T(8,128)(2,1)}, u32[]{:S(2)}, u32[]{:S(2)}) %collective-permute-start.18) | collective-permute-done | bytes 393248 | tf_op jit(solution)/shard_map/ppermute | solution.py:550
  88.4 16.0 %attend.2 = (bf16[3,128,1024]{2,1,0:T(8,128)(2,1)}, bf16[1024,384]{1,0:T(8,128)(2,1)}, f32[3,2,1024]{2,1,0:T(2,128)}) custom-call(s32[4]{0:T(128)} %pad_add_fusion.meta_ref.starts_ref.refs_5_, bf16[3,128,1024]{2,1,0:T(8,128)(2,1)} %get-tuple-element.79.q_ref.refs_0_, bf16[3,128,1024]{2,1,0:T(8,128)(2,1)} %get-tuple-element.80.k_ref.refs_1_, ...), custom_call_target="tpu_custom_call" | custom-call | flops 4831838208 | bytes 3956752 | tf_op jit(solution)/shard_map/attend/pallas_call | solution.py:31
  104.5 6.4 %project_next.1 = (bf16[3,128,1024]{2,1,0:T(8,128)(2,1)}, bf16[3,128,1024]{2,1,0:T(8,128)(2,1)}, bf16[3,128,1024]{2,1,0:T(8,128)(2,1)}) custom-call(bf16[1024,768]{1,0:T(8,128)(2,1)} %get-tuple-element.83.n1_ref, bf16[3,192,768]{2,1,0:T(8,128)(2,1)} %copy-done.4, bf16[3,192,768]{2,1,0:T(8,128)(2,1)} %copy-done.6, f32[32,1024]{1,0:T(8,128)} %get-tuple-element.183.cos_ref, ...), custom_call_target="tpu_custom_call" | custom-call | flops 1811939328 | bytes 5963776 | tf_op jit(solution)/shard_map/project_next/pallas_call | solution.py:31
  111.6 15.8 %attend.3 = (bf16[3,128,1024]{2,1,0:T(8,128)(2,1)}, bf16[1024,384]{1,0:T(8,128)(2,1)}, f32[3,2,1024]{2,1,0:T(2,128)}) custom-call(s32[4]{0:T(128)} %pad_add_fusion.meta_ref.starts_ref.refs_5_, bf16[3,128,1024]{2,1,0:T(8,128)(2,1)} %get-tuple-element.84.q_ref.refs_5_, bf16[3,128,1024]{2,1,0:T(8,128)(2,1)} %get-tuple-element.85.k_ref.refs_6_, ...), custom_call_target="tpu_custom_call" | custom-call | flops 4831838208 | bytes 3956752 | tf_op jit(solution)/shard_map/attend/pallas_call | solution.py:31
  127.5 7.9 %after_attention.1 = (f32[1024,768]{1,0:T(8,128)}, bf16[1024,768]{1,0:T(8,128)(2,1)}, bf16[768,1024]{1,0:T(8,128)(2,1)}, bf16[1024,768]{1,0:T(8,128)(2,1)}, bf16[768,1024]{1,0:T(8,128)(2,1)}) custom-call(s32[4]{0:T(128)} %pad_add_fusion.meta_ref.starts_ref.refs_5_, bf16[1024,768]{1,0:T(8,128)(2,1)} %get-tuple-element.78.x_ref.refs_7_, ...), custom_call_target="tpu_custom_call" | custom-call | flops 1207959552 | bytes 15338512 | tf_op jit(solution)/shard_map/after_attention/pallas_call | solution.py:31
  135.9 26.6 %mlp.3 = (f32[1024,768]{1,0:T(8,128)}, f32[1024,768]{1,0:T(8,128)}, bf16[3,768,512]{2,1,0:T(8,128)(2,1)}, bf16[3,768,512]{2,1,0:T(8,128)(2,1)}) custom-call(s32[4]{0:T(128)} %pad_add_fusion.meta_ref.starts_ref.refs_5_, bf16[1024,768]{1,0:T(8,128)(2,1)} %get-tuple-element.89.n2_ref, bf16[768,1024]{1,0:T(8,128)(2,1)} %get-tuple-element.90.n2t_ref, ...), custom_call_target="tpu_custom_call" | custom-call | flops 14495514624 | bytes 22020112 | tf_op jit(solution)/shard_map/mlp/pallas_call | solution.py:31
  163.5 26.7 %mlp.2 = (f32[1024,768]{1,0:T(8,128)}, f32[1024,768]{1,0:T(8,128)}, bf16[3,768,512]{2,1,0:T(8,128)(2,1)}, bf16[3,768,512]{2,1,0:T(8,128)(2,1)}) custom-call(s32[4]{0:T(128)} %pad_add_fusion.meta_ref.starts_ref.refs_5_, bf16[1024,768]{1,0:T(8,128)(2,1)} %get-tuple-element.89.n2_ref, bf16[768,1024]{1,0:T(8,128)(2,1)} %get-tuple-element.90.n2t_ref, ...), custom_call_target="tpu_custom_call" | custom-call | flops 14495514624 | bytes 22020112 | tf_op jit(solution)/shard_map/mlp/pallas_call | solution.py:31
  190.6 13.9 %middle.1 = (bf16[256,768]{1,0:T(8,128)(2,1)}, bf16[256,768]{1,0:T(8,128)(2,1)}, bf16[256,768]{1,0:T(8,128)(2,1)}, bf16[256,768]{1,0:T(8,128)(2,1)}, f32[1024,76...) custom-call(s32[4]{0:T(128)} %pad_add_fusion.meta_ref.starts_ref.refs_5_, ...), custom_call_target="tpu_custom_call" | custom-call | flops 2415919104 | bytes 29104144 | tf_op jit(solution)/shard_map/middle/pallas_call | solution.py:31
  204.5 14.6 %attend_back.5 = (bf16[3,256,1024]{2,1,0:T(8,128)(2,1)}, bf16[4,3,64,768]{3,2,1,0:T(8,128)(2,1)}) custom-call(s32[4]{0:T(128)} %pad_add_fusion.meta_ref.starts_ref.refs_5_, f32[32,1024]{1,0:T(8,128)} %get-tuple-element.183.cos_ref, f32[32,1024]{1,0:T(8,128)} %get-tuple-element.182.sin_ref, bf16[1024,768]{1,0:T(8,128)(2,1)} %get-tuple-element.83.n1_ref, ...), custom_call_target="tpu_custom_call" | custom-call | flops 9261023232 | bytes 12501008 | tf_op jit(solution)/shard_map/attend_back/pallas_call | solution.py:31
  227.4 14.6 %attend_back.4 = (bf16[3,256,1024]{2,1,0:T(8,128)(2,1)}, bf16[4,3,64,768]{3,2,1,0:T(8,128)(2,1)}) custom-call(s32[4]{0:T(128)} %pad_add_fusion.meta_ref.starts_ref.refs_5_, f32[32,1024]{1,0:T(8,128)} %get-tuple-element.183.cos_ref, f32[32,1024]{1,0:T(8,128)} %get-tuple-element.182.sin_ref, bf16[1024,768]{1,0:T(8,128)(2,1)} %get-tuple-element.83.n1_ref, ...), custom_call_target="tpu_custom_call" | custom-call | flops 9261023232 | bytes 12501008 | tf_op jit(solution)/shard_map/attend_back/pallas_call | solution.py:31
  253.9 26.9 %collective-permute-done.58 = bf16[2304,512]{1,0:T(8,128)(2,1)} collective-permute-done((bf16[2304,512]{1,0:T(8,128)(2,1)}, bf16[2304,512]{1,0:T(8,128)(2,1)}, u32[]{:S(2)}, u32[]{:S(2)}) %collective-permute-start.58) | collective-permute-done | bytes 2359328 | tf_op jit(solution)/shard_map/ppermute | solution.py:550
  280.8 5.3 %sum_split.19 = (bf16[1152,512]{1,0:T(8,128)(2,1)}, bf16[1152,512]{1,0:T(8,128)(2,1)}) custom-call(s32[1]{0:T(128)} %bitcast.12.index_ref, bf16[2,1152,512]{2,1,0:T(8,128)(2,1)} %bitcast.87, bf16[2,1152,512]{2,1,0:T(8,128)(2,1)} %bitcast.88, bf16[2,1152,512]{2,1,0:T(8,128)(2,1)} %bitcast.60.refs_2_), custom_call_target="tpu_custom_call" | custom-call | flops 3538944 | bytes 9437188 | tf_op jit(solution)/shard_map/sum_split/pallas_call | solution.py:31
  286.6 14.6 %attend_back.3 = (bf16[3,256,1024]{2,1,0:T(8,128)(2,1)}, bf16[4,3,64,768]{3,2,1,0:T(8,128)(2,1)}) custom-call(s32[4]{0:T(128)} %pad_add_fusion.meta_ref.starts_ref.refs_5_, f32[32,1024]{1,0:T(8,128)} %get-tuple-element.183.cos_ref, f32[32,1024]{1,0:T(8,128)} %get-tuple-element.182.sin_ref, bf16[1024,768]{1,0:T(8,128)(2,1)} %get-tuple-element.83.n1_ref, ...), custom_call_target="tpu_custom_call" | custom-call | flops 9261023232 | bytes 12501008 | tf_op jit(solution)/shard_map/attend_back/pallas_call | solution.py:31
  301.2 7.1 %token_grad.2.refs_6_ = f32[1024,768]{1,0:T(8,128)} custom-call(bf16[3,256,1024]{2,1,0:T(8,128)(2,1)} %get-tuple-element.107.refs_0_, bf16[3,256,1024]{2,1,0:T(8,128)(2,1)} %get-tuple-element.108.refs_1_, bf16[3,192,768]{2,1,0:T(8,128)(2,1)} %copy-done.2, bf16[3,192,768]{2,1,0:T(8,128)(2,1)} %copy-done.5, bf16[3,192,768]{2,1,0:T(8,128)(2,1)} %copy-done.4, ...), custom_call_target="tpu_custom_call" | custom-call | flops 2415919104 | bytes 9830400 | tf_op jit(solution)/shard_map/token_grad/pallas_call | solution.py:31
  308.3 9.0 %token_grad.3 = (bf16[256,768]{1,0:T(8,128)(2,1)}, bf16[256,768]{1,0:T(8,128)(2,1)}, bf16[256,768]{1,0:T(8,128)(2,1)}, bf16[256,768]{1,0:T(8,128)(2,1)}, f32[1,768]{1,0:T(1,128)}) custom-call(bf16[3,256,1024]{2,1,0:T(8,128)(2,1)} %get-tuple-element.106.refs_0_, bf16[3,192,768]{2,1,0:T(8,128)(2,1)} %copy-done.2, bf16[3,192,768]{2,1,0:T(8,128)(2,1)} %copy-done.5, ...), custom_call_target="tpu_custom_call" | custom-call | flops 1207959552 | bytes 16128016 | tf_op jit(solution)/shard_map/token_grad/pallas_call | solution.py:31
  336.8 8.4 %collective-permute-done.60 = bf16[288,512]{1,0:T(8,128)(2,1)S(1)} collective-permute-done((bf16[288,512]{1,0:T(8,128)(2,1)}, bf16[288,512]{1,0:T(8,128)(2,1)S(1)}, u32[]{:S(2)}, u32[]{:S(2)}) %collective-permute-start.60) | collective-permute-done | bytes 294944 | tf_op jit(solution)/shard_map/ppermute | solution.py:550
  346.5 9.3 %collective-permute-done.61 = bf16[288,512]{1,0:T(8,128)(2,1)S(1)} collective-permute-done((bf16[288,512]{1,0:T(8,128)(2,1)}, bf16[288,512]{1,0:T(8,128)(2,1)S(1)}, u32[]{:S(2)}, u32[]{:S(2)}) %collective-permute-start.61) | collective-permute-done | bytes 294944 | tf_op jit(solution)/shard_map/ppermute | solution.py:550
  374.9 6.1 %collective-permute-done.63.refs_1_ = bf16[288,512]{1,0:T(8,128)(2,1)S(1)} collective-permute-done((bf16[288,512]{1,0:T(8,128)(2,1)}, bf16[288,512]{1,0:T(8,128)(2,1)S(1)}, u32[]{:S(2)}, u32[]{:S(2)}) %collective-permute-start.63) | collective-permute-done | bytes 294944 | tf_op jit(solution)/shard_map/ppermute | solution.py:550
  381.0 13.8 %collective-permute-done.64.refs_2_ = bf16[288,512]{1,0:T(8,128)(2,1)S(1)} collective-permute-done((bf16[288,512]{1,0:T(8,128)(2,1)}, bf16[288,512]{1,0:T(8,128)(2,1)S(1)}, u32[]{:S(2)}, u32[]{:S(2)}) %collective-permute-start.64) | collective-permute-done | bytes 294944 | tf_op jit(solution)/shard_map/ppermute | solution.py:550
  458.6 5.9 %collective-permute-done.27.p3 = bf16[256,768]{1,0:T(8,128)(2,1)} collective-permute-done((bf16[256,768]{1,0:T(8,128)(2,1)}, bf16[256,768]{1,0:T(8,128)(2,1)}, u32[]{:S(2)}, u32[]{:S(2)}) %collective-permute-start.27) | collective-permute-done | bytes 393248 | tf_op jit(solution)/shard_map/ppermute | solution.py:550
  503.6 5.8 %mlp_out.1 = (f32[1536,512]{1,0:T(8,128)}, f32[512,768]{1,0:T(8,128)}) custom-call(bf16[2304,512]{1,0:T(8,128)(2,1)} %bitcast.81, bf16[2304,512]{1,0:T(8,128)(2,1)} %bitcast.82), custom_call_target="tpu_custom_call" | custom-call | flops 1179648 | bytes 9437184 | tf_op jit(solution)/shard_map/mlp_out/pallas_call | solution.py:31
  (348 shorter events, 199.8 us)
Async XLA Ops:
  2.2 48.5 %collective-permute-start.4 = (bf16[3,192,768]{2,1,0:T(8,128)(2,1)S(1)}, bf16[3,192,768]{2,1,0:T(8,128)(2,1)S(1)}, u32[]{:S(2)}, u32[]{:S(2)}) collective-permute-start(bf16[3,192,768]{2,1,0:T(8,128)(2,1)S(1)} %convert_bitcast_fusion.w0.refs_2_.refs_1_), channel_id=1, source_target_pairs={{0,2},{1,3},{2,0},{3,1},{4,6},{5,7},{6,4},{7,5},{8,10},{9,11},{10,... | collective-permute-start | bytes 2654216 | tf_op jit(solution)/shard_map/ppermute | solution.py:550
  8.4 43.9 %collective-permute-start.14 = (bf16[1,768,512]{2,1,0:T(8,128)(2,1)}, bf16[1,768,512]{2,1,0:T(8,128)(2,1)}, u32[]{:S(2)}, u32[]{:S(2)}) collective-permute-start(bf16[1,768,512]{2,1,0:T(8,128)(2,1)} %constant_dynamic-slice_fusion.1), channel_id=1, source_target_pairs={{0,2},{1,3},{2,0},{3,1},{4,6},{5,7},{6,4},{7,5},{8,10},{9,11},{10,... | collective-permute-start | bytes 2359304 | tf_op jit(solution)/shard_map/ppermute | solution.py:550
  12.6 37.4 %collective-permute-start = (bf16[256,768]{1,0:T(8,128)(2,1)S(1)}, bf16[256,768]{1,0:T(8,128)(2,1)S(1)}, u32[]{:S(2)}, u32[]{:S(2)}) collective-permute-start(bf16[256,768]{1,0:T(8,128)(2,1)S(1)} %get-tuple-element.164), channel_id=1, source_target_pairs={{0,1},{1,0},{2,3},{3,2},{4,5},{5,4},{6,7},{7,6},{8,9},{9,8},{10,11... | collective-permute-start | bytes 1179656 | tf_op jit(solution)/shard_map/ppermute | solution.py:550
  13.1 53.4 %collective-permute-start.3 = (bf16[3,192,768]{2,1,0:T(8,128)(2,1)S(1)}, bf16[3,192,768]{2,1,0:T(8,128)(2,1)S(1)}, u32[]{:S(2)}, u32[]{:S(2)}) collective-permute-start(bf16[3,192,768]{2,1,0:T(8,128)(2,1)S(1)} %convert_bitcast_fusion.w0.refs_2_.refs_1_), channel_id=1, source_target_pairs={{0,1},{1,0},{2,3},{3,2},{4,5},{5,4},{6,7},{7,6},{8,9},{9,8},{10,11... | collective-permute-start | bytes 2654216 | tf_op jit(solution)/shard_map/ppermute | solution.py:550
  13.1 35.1 %collective-permute-start.7 = (bf16[192,768]{1,0:T(8,128)(2,1)}, bf16[192,768]{1,0:T(8,128)(2,1)}, u32[]{:S(2)}, u32[]{:S(2)}) collective-permute-start(bf16[192,768]{1,0:T(8,128)(2,1)} %convert_element_type.70.w0), channel_id=1, source_target_pairs={{0,2},{1,3},{2,0},{3,1},{4,6},{5,7},{6,4},{7,5},{8,10},{9,11},{10,... | collective-permute-start | bytes 884744 | tf_op jit(solution)/shard_map/ppermute | solution.py:550
  50.7 37.2 %collective-permute-start.5 = (bf16[3,192,768]{2,1,0:T(8,128)(2,1)S(1)}, bf16[3,192,768]{2,1,0:T(8,128)(2,1)S(1)}, u32[]{:S(2)}, u32[]{:S(2)}) collective-permute-start(bf16[3,192,768]{2,1,0:T(8,128)(2,1)S(1)} %collective-permute-done.4.w0.refs_4_.refs_3_), channel_id=1, source_target_pairs={{0,1},{1,0},{2,3},{3,2},{4,5},{5,4},{6,7},{7,6},{8,9},{9,8},{10,11... | collective-permute-start | bytes 2654216 | tf_op jit(solution)/shard_map/ppermute | solution.py:550
  52.3 35.6 %collective-permute-start.15 = (bf16[1,768,512]{2,1,0:T(8,128)(2,1)}, bf16[1,768,512]{2,1,0:T(8,128)(2,1)}, u32[]{:S(2)}, u32[]{:S(2)}) collective-permute-start(bf16[1,768,512]{2,1,0:T(8,128)(2,1)} %collective-permute-done.14.refs_0_), channel_id=1, source_target_pairs={{0,4},{4,0},{8,12},{12,8},{16,20},{20,16},{24,28},{28,24},{1,5},{5... | collective-permute-start | bytes 2359304 | tf_op jit(solution)/shard_map/ppermute | solution.py:550
  76.0 35.0 %collective-permute-start.11 = (bf16[256,768]{1,0:T(8,128)(2,1)S(1)}, bf16[256,768]{1,0:T(8,128)(2,1)S(1)}, u32[]{:S(2)}, u32[]{:S(2)}) collective-permute-start(bf16[256,768]{1,0:T(8,128)(2,1)S(1)} %copy-done.30), channel_id=1, source_target_pairs={{0,3},{1,2},{2,1},{3,0},{4,7},{5,6},{6,5},{7,4},{8,11},{9,10},{10,... | collective-permute-start | bytes 1179656 | tf_op jit(solution)/shard_map/ppermute | solution.py:550
  77.9 33.2 %collective-permute-start.8 = (bf16[192,768]{1,0:T(8,128)(2,1)}, bf16[192,768]{1,0:T(8,128)(2,1)S(1)}, u32[]{:S(2)}, u32[]{:S(2)}) collective-permute-start(bf16[192,768]{1,0:T(8,128)(2,1)} %collective-permute-done.7.w2), channel_id=1, source_target_pairs={{0,1},{1,0},{2,3},{3,2},{4,5},{5,4},{6,7},{7,6},{8,9},{9,8},{10,11... | collective-permute-start | bytes 884744 | tf_op jit(solution)/shard_map/ppermute | solution.py:550
  87.9 48.0 %collective-permute-start.16 = (bf16[1,768,512]{2,1,0:T(8,128)(2,1)}, bf16[1,768,512]{2,1,0:T(8,128)(2,1)}, u32[]{:S(2)}, u32[]{:S(2)}) collective-permute-start(bf16[1,768,512]{2,1,0:T(8,128)(2,1)} %collective-permute-done.14.refs_0_), channel_id=1, source_target_pairs={{0,1},{1,0},{2,3},{3,2},{4,5},{5,4},{6,7},{7,6},{8,9},{9,8},{10,11... | collective-permute-start | bytes 2359304 | tf_op jit(solution)/shard_map/ppermute | solution.py:550
  87.9 48.0 %collective-permute-start.17 = (bf16[1,768,512]{2,1,0:T(8,128)(2,1)}, bf16[1,768,512]{2,1,0:T(8,128)(2,1)}, u32[]{:S(2)}, u32[]{:S(2)}) collective-permute-start(bf16[1,768,512]{2,1,0:T(8,128)(2,1)} %collective-permute-done.15.refs_1_), channel_id=1, source_target_pairs={{0,1},{1,0},{2,3},{3,2},{4,5},{5,4},{6,7},{7,6},{8,9},{9,8},{10,11... | collective-permute-start | bytes 2359304 | tf_op jit(solution)/shard_map/ppermute | solution.py:550
  111.0 51.6 %collective-permute-start.12 = (bf16[2,768,512]{2,1,0:T(8,128)(2,1)S(1)}, bf16[2,768,512]{2,1,0:T(8,128)(2,1)}, u32[]{:S(2)}, u32[]{:S(2)}) collective-permute-start(bf16[2,768,512]{2,1,0:T(8,128)(2,1)S(1)} %copy-done.8), channel_id=1, source_target_pairs={{0,1},{1,0},{2,3},{3,2},{4,5},{5,4},{6,7},{7,6},{8,9},{9,8},{10,11... | collective-permute-start | bytes 4718600 | tf_op jit(solution)/shard_map/ppermute | solution.py:550
  135.4 27.1 %collective-permute-start.13 = (bf16[2,256,768]{2,1,0:T(8,128)(2,1)S(1)}, bf16[2,256,768]{2,1,0:T(8,128)(2,1)S(1)}, u32[]{:S(2)}, u32[]{:S(2)}) collective-permute-start(bf16[2,256,768]{2,1,0:T(8,128)(2,1)S(1)} %bitcast.92), channel_id=1, source_target_pairs={{0,1},{1,0},{2,3},{3,2},{4,5},{5,4},{6,7},{7,6},{8,9},{9,8},{10,11... | collective-permute-start | bytes 2359304 | tf_op jit(solution)/shard_map/ppermute | solution.py:550
  162.5 58.7 %collective-permute-start.57 = (bf16[3,768,512]{2,1,0:T(8,128)(2,1)}, bf16[3,768,512]{2,1,0:T(8,128)(2,1)}, u32[]{:S(2)}, u32[]{:S(2)}) collective-permute-start(bf16[3,768,512]{2,1,0:T(8,128)(2,1)} %get-tuple-element.137), channel_id=1, source_target_pairs={{0,1},{1,0},{2,3},{3,2},{4,5},{5,4},{6,7},{7,6},{8,9},{9,8},{10,11... | collective-permute-start | bytes 7077896 | tf_op jit(solution)/shard_map/ppermute | solution.py:550
  190.2 63.7 %collective-permute-start.56 = (bf16[3,768,512]{2,1,0:T(8,128)(2,1)}, bf16[3,768,512]{2,1,0:T(8,128)(2,1)S(1)}, u32[]{:S(2)}, u32[]{:S(2)}) collective-permute-start(bf16[3,768,512]{2,1,0:T(8,128)(2,1)} %get-tuple-element.135), channel_id=1, source_target_pairs={{0,1},{1,0},{2,3},{3,2},{4,5},{5,4},{6,7},{7,6},{8,9},{9,8},{10,11... | collective-permute-start | bytes 7077896 | tf_op jit(solution)/shard_map/ppermute | solution.py:550
  226.3 54.4 %collective-permute-start.58 = (bf16[2304,512]{1,0:T(8,128)(2,1)}, bf16[2304,512]{1,0:T(8,128)(2,1)}, u32[]{:S(2)}, u32[]{:S(2)}) collective-permute-start(bf16[2304,512]{1,0:T(8,128)(2,1)} %sum_split.18), channel_id=1, source_target_pairs={{0,2},{1,3},{2,0},{3,1},{4,6},{5,7},{6,4},{7,5},{8,10},{9,11},{10,... | collective-permute-start | bytes 7077896 | tf_op jit(solution)/shard_map/ppermute | solution.py:550
  248.4 86.4 %collective-permute-start.28 = (bf16[576,768]{1,0:T(8,128)(2,1)}, bf16[576,768]{1,0:T(8,128)(2,1)}, u32[]{:S(2)}, u32[]{:S(2)}) collective-permute-start(bf16[576,768]{1,0:T(8,128)(2,1)} %pad_maximum_fusion.1), channel_id=1, source_target_pairs={{0,1},{1,0},{2,3},{3,2},{4,5},{5,4},{6,7},{7,6},{8,9},{9,8},{10,11... | collective-permute-start | bytes 2654216 | tf_op jit(solution)/shard_map/ppermute | solution.py:550
  252.9 82.6 %collective-permute-start.30 = (bf16[576,768]{1,0:T(8,128)(2,1)}, bf16[576,768]{1,0:T(8,128)(2,1)}, u32[]{:S(2)}, u32[]{:S(2)}) collective-permute-start(bf16[576,768]{1,0:T(8,128)(2,1)} %sum_split.11), channel_id=1, source_target_pairs={{0,2},{1,3},{2,0},{3,1},{4,6},{5,7},{6,4},{7,5},{8,10},{9,11},{10,... | collective-permute-start | bytes 2654216 | tf_op jit(solution)/shard_map/ppermute | solution.py:550
  286.1 39.7 %collective-permute-start.59 = (bf16[1152,512]{1,0:T(8,128)(2,1)}, bf16[1152,512]{1,0:T(8,128)(2,1)S(1)}, u32[]{:S(2)}, u32[]{:S(2)}) collective-permute-start(bf16[1152,512]{1,0:T(8,128)(2,1)} %get-tuple-element.139), channel_id=1, source_target_pairs={{0,4},{4,0},{8,12},{12,8},{16,20},{20,16},{24,28},{28,24},{1,5},{5... | collective-permute-start | bytes 3538952 | tf_op jit(solution)/shard_map/ppermute | solution.py:550
  334.8 29.8 %collective-permute-start.71 = (f32[2,768]{1,0:T(2,128)S(1)}, f32[2,768]{1,0:T(2,128)S(1)}, u32[]{:S(2)}, u32[]{:S(2)}) collective-permute-start(f32[2,768]{1,0:T(2,128)S(1)} %copy-done.60), channel_id=1, source_target_pairs={{0,8},{4,12},{8,0},{12,4},{16,24},{20,28},{24,16},{28,20},{1,9},{5... | collective-permute-start | bytes 18440 | tf_op jit(solution)/shard_map/ppermute | solution.py:550
  335.5 30.9 %collective-permute-start.72 = (f32[2,768]{1,0:T(2,128)S(1)}, f32[2,768]{1,0:T(2,128)S(1)}, u32[]{:S(2)}, u32[]{:S(2)}) collective-permute-start(f32[2,768]{1,0:T(2,128)S(1)} %copy-done.60), channel_id=1, source_target_pairs={{0,12},{4,8},{8,4},{12,0},{16,28},{20,24},{24,20},{28,16},{1,13},{... | collective-permute-start | bytes 18440 | tf_op jit(solution)/shard_map/ppermute | solution.py:550
  366.4 36.5 %collective-permute-start.31 = (bf16[288,768]{1,0:T(8,128)(2,1)}, bf16[288,768]{1,0:T(8,128)(2,1)S(1)}, u32[]{:S(2)}, u32[]{:S(2)}) collective-permute-start(bf16[288,768]{1,0:T(8,128)(2,1)} %get-tuple-element.118), channel_id=1, source_target_pairs={{0,4},{4,0},{8,12},{12,8},{16,20},{20,16},{24,28},{28,24},{1,5},{5... | collective-permute-start | bytes 1327112 | tf_op jit(solution)/shard_map/ppermute | solution.py:550
  399.5 99.9 %collective-permute-start.66 = (bf16[1152,512]{1,0:T(8,128)(2,1)}, bf16[1152,512]{1,0:T(8,128)(2,1)S(1)}, u32[]{:S(2)}, u32[]{:S(2)}) collective-permute-start(bf16[1152,512]{1,0:T(8,128)(2,1)} %bitcast.83), channel_id=1, source_target_pairs={{0,4},{4,0},{8,12},{12,8},{16,20},{20,16},{24,28},{28,24},{1,5},{5... | collective-permute-start | bytes 3538952 | tf_op jit(solution)/shard_map/ppermute | solution.py:550
  454.9 35.6 %collective-permute-start.38 = (bf16[288,768]{1,0:T(8,128)(2,1)}, bf16[288,768]{1,0:T(8,128)(2,1)S(1)}, u32[]{:S(2)}, u32[]{:S(2)}) collective-permute-start(bf16[288,768]{1,0:T(8,128)(2,1)} %bitcast.93), channel_id=1, source_target_pairs={{0,4},{4,0},{8,12},{12,8},{16,20},{20,16},{24,28},{28,24},{1,5},{5... | collective-permute-start | bytes 1327112 | tf_op jit(solution)/shard_map/ppermute | solution.py:550
  (132 other events, 1862.5 us)

commit v2 on v1

v2 whole, which is shorter than its diff:
```python
import functools
import jax
import jax.numpy as jnp
import numpy as np
from jax import lax
from jax.experimental import pallas as pl
from jax.experimental.pallas import tpu as pltpu
from jax.sharding import PartitionSpec as P

HD = 64
LEN = 1024
PIECE = 256
HALF = 512
EPS = 1e-06
F32 = jnp.float32
BF16 = jnp.bfloat16
MIB = 1024 * 1024


def nn(a, b):
    return lax.dot_general(a, b, (((1,), (0,)), ((), ())), preferred_element_type=F32)


def nt(a, b):
    return lax.dot_general(a, b, (((1,), (1,)), ((), ())), preferred_element_type=F32)


def call(body, name, out_shape, args, vmem, cost=1e6, **kw):
    return pl.pallas_call(
        body,
        name=name,
        out_shape=out_shape,
        compiler_params=pltpu.CompilerParams(vmem_limit_bytes=vmem * MIB),
        cost_estimate=pl.CostEstimate(flops=int(cost), bytes_accessed=int(cost) // 100, transcendentals=0),
        **kw,
    )(*args)


def struct(shape, dtype):
    return jax.ShapeDtypeStruct(shape, dtype)


def project(n1_ref, weights, cos_ref, sin_ref, q_ref, k_ref, v_ref):
    step = 256
    for block in range(LEN // step):
        cols = slice(block * step, (block + 1) * step)
        rows = n1_ref[cols, :]
        cosine = cos_ref[:, cols]
        sine = sin_ref[:, cols]
        for slot, w_ref in enumerate(weights):
            for part, ref in ((0, q_ref), (1, k_ref), (2, v_ref)):
                made = nt(w_ref[part], rows)
                for head in range(3):
                    low = made[head * HD : head * HD + HD // 2]
                    high = made[head * HD + HD // 2 : (head + 1) * HD]
                    if part < 2:
                        low, high = low * cosine - high * sine, high * cosine + low * sine
                    if part == 0:
                        low, high = low * HD**-0.5, high * HD**-0.5
                    at = slot * HD
                    ref[head, at : at + HD // 2, cols] = low.astype(BF16)
                    ref[head, at + HD // 2 : at + HD, cols] = high.astype(BF16)


def in_order(here, pieces, ref):
    step = ref.shape[0] // 4
    for quarter in range(4):
        for slot, piece in enumerate(pieces):

            @pl.when((here ^ slot) == quarter)
            def _():
                ref[quarter * step : (quarter + 1) * step, :] = piece[...]


def project_first_body(meta_ref, p0, p1, p2, p3, gain_ref, w0, w1, cos_ref, sin_ref, x_ref, n1_ref, q_ref, k_ref, v_ref):
    step = 256
    gain = gain_ref[...]
    in_order(meta_ref[2], (p0, p1, p2, p3), x_ref)
    for block in range(LEN // step):
        rows = slice(block * step, (block + 1) * step)
        x = x_ref[rows, :].astype(F32)
        scale = lax.rsqrt(jnp.mean(x * x, axis=-1, keepdims=True) + EPS)
        n1_ref[rows, :] = (x * scale * gain).astype(BF16)
    project(n1_ref, (w0, w1), cos_ref, sin_ref, q_ref, k_ref, v_ref)


def project_next_body(
    meta_ref, n1_ref, d2, r2, d3, r3, cos_ref, sin_ref, q_ref, k_ref, v_ref, w2_ref, w3_ref
):
    bit = meta_ref[3]
    for direct, other, ref in ((d2, r2, w2_ref), (d3, r3, w3_ref)):
        for part in range(2):
            ref[2 * bit + part] = direct[part]
            ref[2 * (1 - bit) + part] = other[part]
    project(n1_ref, (w2_ref, w3_ref), cos_ref, sin_ref, q_ref, k_ref, v_ref)


HEADS3 = (3, 2 * HD, LEN)


VM = pl.BlockSpec(memory_space=pltpu.VMEM)
SM = pl.BlockSpec(memory_space=pltpu.SMEM)


def project_first(meta, pieces, gain, w0, w1, cosine, sine):
    width = gain.shape[1]
    out = [struct((LEN, width), BF16)] * 2 + [struct(HEADS3, BF16)] * 3
    args = (meta, *pieces, gain, w0, w1, cosine, sine)
    return call(
        project_first_body,
        "project_first",
        out,
        args,
        24,
        in_specs=[SM] + [VM] * (len(args) - 1),
        out_specs=[VM] * len(out),
    )


def project_next(meta, n1, far, cosine, sine):
    out = [struct(HEADS3, BF16)] * 3 + [struct((4,) + far[0].shape[1:], BF16)] * 2
    args = (meta, n1, *far, cosine, sine)
    return call(
        project_next_body,
        "project_next",
        out,
        args,
        24,
        in_specs=[SM] + [VM] * (len(args) - 1),
        out_specs=[VM] * len(out),
    )


def limits(starts_ref):
    pos = lax.broadcasted_iota(jnp.int32, (1, LEN), 1)
    lim = pos
    for piece in range(2):
        first = starts_ref[piece]
        lim = jnp.where((pos >= first) & (pos < first + PIECE), first + PIECE - 1, lim)
    return lim


def one_head(block, head):
    zero = jnp.zeros((HD, block.shape[1]), block.dtype)
    part = block[head * HD : (head + 1) * HD]
    return jnp.concatenate([part, zero] if head == 0 else [zero, part], axis=0)


NEG = -1e30


def attend_body(qb, starts_ref, q_ref, k_ref, v_ref, mt_ref, m_ref, lse_ref):
    lim = limits(starts_ref)
    k_rows = k_ref[0].T
    for head in range(2):
        q_one = one_head(q_ref[0], head)
        v_one = v_ref[0, head * HD : (head + 1) * HD, :]
        for block in range(LEN // qb):
            cols = slice(block * qb, (block + 1) * qb)
            keys = HALF if (block + 1) * qb <= HALF else LEN
            scores = nn(k_rows[:keys], q_one[:, cols])
            edge = scores[keys - HALF :]
            pos = lax.broadcasted_iota(jnp.int32, (HALF, qb), 0) + (keys - HALF)
            edge = jnp.where(pos <= lim[:, cols], edge, NEG)
            most = jnp.max(edge, axis=0, keepdims=True)
            if keys > HALF:
                body = scores[:HALF]
                most = jnp.maximum(most, jnp.max(body, axis=0, keepdims=True))
            soft = jnp.exp(edge - most)
            total = jnp.sum(soft, axis=0, keepdims=True)
            mixed = nn(v_one[:, keys - HALF : keys], soft.astype(BF16))
            if keys > HALF:
                soft = jnp.exp(body - most)
                total = total + jnp.sum(soft, axis=0, keepdims=True)
                mixed = mixed + nn(v_one[:, :HALF], soft.astype(BF16))
            mt_ref[0, head * HD : (head + 1) * HD, cols] = (mixed * (1.0 / total)).astype(BF16)
            lse_ref[0, head : head + 1, cols] = most + jnp.log(total)
    m_ref[...] = mt_ref[0].T


def attend(starts, q, k, v, qb=512):
    block = pl.BlockSpec((1, 2 * HD, LEN), lambda i: (i, 0, 0))
    out = [struct(HEADS3, BF16), struct((LEN, 6 * HD), BF16), struct((3, 2, LEN), F32)]
    return call(
        functools.partial(attend_body, qb),
        "attend",
        out,
        (starts, q, k, v),
        24,
        grid=(3,),
        in_specs=[pl.BlockSpec(memory_space=pltpu.SMEM), block, block, block],
        out_specs=[
            block,
            pl.BlockSpec((LEN, 2 * HD), lambda i: (0, i)),
            pl.BlockSpec((1, 2, LEN), lambda i: (i, 0, 0)),
        ],
    )


def attend_back_body(qb, starts_ref, cos_ref, sin_ref, n1_ref, *refs):
    sets = (refs[0:5], refs[5:10])
    do_ref = refs[10]
    dt_ref, even_ref, odd_ref, acc_ref = refs[11:]
    lim = limits(starts_ref)
    for which, (q_ref, k_ref, v_ref, mt_ref, lse_ref) in enumerate(sets):
        q = q_ref[0]
        k = k_ref[0]
        v = v_ref[0]
        do = do_ref[which * 2 * HD : (which + 1) * 2 * HD, :]
        k_rows = k.T
        v_rows = v.T
        both = do.astype(F32) * mt_ref[0].astype(F32)
        for head in range(2):
            mine = slice(head * HD, (head + 1) * HD)
            inner = jnp.sum(both[mine], axis=0, keepdims=True)
            q_one = one_head(q, head)
            do_one = one_head(do, head)
            lse = lse_ref[0, head : head + 1, :]
            for block in range(LEN // qb):
                cols = slice(block * qb, (block + 1) * qb)
                wide = (block + 1) * qb > HALF
                dq = None
                for part in range(2 if wide else 1):
                    keys = slice(part * HALF, (part + 1) * HALF)
                    scores = nn(k_rows[keys], q_one[:, cols])
                    if part == (1 if wide else 0):
                        pos = lax.broadcasted_iota(jnp.int32, (HALF, qb), 0) + part * HALF
                        scores = jnp.where(pos <= lim[:, cols], scores, NEG)
                    soft = jnp.exp(scores - lse[:, cols])
                    grad = nn(v_rows[keys], do_one[:, cols])
                    grad = (soft * (grad - inner[:, cols])).astype(BF16)
                    more = nn(k[mine, keys], grad)
                    dq = more if dq is None else dq + more
                    dk = nt(q[mine, cols], grad)
                    dv = nt(do[mine, cols], soft.astype(BF16))
                    fresh = block == (0 if part == 0 else HALF // qb)
                    if fresh:
                        acc_ref[1, mine, keys] = dk
                        acc_ref[2, mine, keys] = dv
                    else:
                        acc_ref[1, mine, keys] += dk
                        acc_ref[2, mine, keys] += dv
                acc_ref[0, mine, cols] = dq * HD**-0.5
        cosine = cos_ref[...]
        sine = sin_ref[...]
        for part in range(3):
            for head in range(2):
                at = head * HD
                low = acc_ref[part, at : at + HD // 2, :]
                high = acc_ref[part, at + HD // 2 : at + HD, :]
                if part < 2:
                    low, high = low * cosine + high * sine, high * cosine - low * sine
                to = which * 2 * HD + at
                dt_ref[part, to : to + HD // 2, :] = low.astype(BF16)
                dt_ref[part, to + HD // 2 : to + HD, :] = high.astype(BF16)
    for part in range(3):
        made = nn(dt_ref[part], n1_ref[...])
        for slot in range(4):
            ref = odd_ref if slot % 2 else even_ref
            ref[slot // 2, part * HD : (part + 1) * HD, :] = made[slot * HD : (slot + 1) * HD].astype(BF16)


def attend_back(turn, starts, cosine, sine, n1, sets, do, qb=512):
    width = n1.shape[1]
    head = pl.BlockSpec((1, 2 * HD, LEN), lambda i: (turn, 0, 0))
    full = lambda a: pl.BlockSpec(a.shape, lambda i, n=a.ndim: (0,) * n)
    lse = pl.BlockSpec((1, 2, LEN), lambda i: (turn, 0, 0))
    args = (starts, cosine, sine, n1, *sets[0], *sets[1], do)
    out = [struct((3, 4 * HD, LEN), BF16)] + [struct((2, 3 * HD, width), BF16)] * 2
    return call(
        functools.partial(attend_back_body, qb),
        "attend_back",
        out,
        args,
        40,
        grid=(1,),
        in_specs=[pl.BlockSpec(memory_space=pltpu.SMEM), full(cosine), full(sine), full(n1)]
        + [head, head, head, head, lse] * 2
        + [pl.BlockSpec((4 * HD, LEN), lambda i: (turn, 0))],
        out_specs=[full(o) for o in out],
        scratch_shapes=[pltpu.VMEM((3, 2 * HD, LEN), F32)],
    )


def turn_rows(w_refs):
    return jnp.concatenate(
        [w[3, turn * HD : (turn + 1) * HD, :] for turn in range(3) for w in w_refs], axis=0
    )


def after_body(
    meta_ref, x_ref, ma_ref, mb_ref, w0, w1, w2, w3, gain_ref, g0, g1, g2, g3,
    after_ref, n2_ref, n2t_ref, g_ref, gt_ref,
):
    slot = pl.program_id(0) ^ meta_ref[2]
    for which, piece in enumerate((g0, g1, g2, g3)):

        @pl.when(slot == which)
        def _():
            g_ref[...] = piece[...]

    first = turn_rows((w0, w1))
    second = turn_rows((w2, w3))
    after = x_ref[...].astype(F32) + nn(ma_ref[...], first) + nn(mb_ref[...], second)
    after_ref[...] = after
    scale = lax.rsqrt(jnp.mean(after * after, axis=-1, keepdims=True) + EPS)
    normed = (after * scale * gain_ref[...]).astype(BF16)
    n2_ref[...] = normed
    n2t_ref[...] = normed.T
    gt_ref[...] = g_ref[...].T


def after_attention(meta, x, mixed_a, mixed_b, wo, gain, g):
    width = x.shape[1]
    step = 256
    rows = lambda n: pl.BlockSpec((step, n), lambda i: (i, 0))
    cols = pl.BlockSpec((width, step), lambda i: (0, i))
    full = lambda a: pl.BlockSpec(a.shape, lambda i, n=a.ndim: (0,) * n)
    args = (meta, x, mixed_a, mixed_b, *wo, gain, *g)
    out = [
        struct((LEN, width), F32),
        struct((LEN, width), BF16),
        struct((width, LEN), BF16),
        struct((LEN, width), BF16),
        struct((width, LEN), BF16),
    ]
    return call(
        after_body,
        "after_attention",
        out,
        args,
        30,
        grid=(LEN // step,),
        in_specs=[SM, rows(width), rows(6 * HD), rows(6 * HD)]
        + [full(w) for w in wo]
        + [full(gain)]
        + [full(p) for p in g],
        out_specs=[rows(width), rows(width), cols, rows(width), cols],
    )


def mlp_body(layout, first, meta_ref, n2_ref, n2t_ref, g_ref, gt_ref, *refs):
    block = 256
    refs = list(refs)
    sources = [[refs.pop(0) for _ in range(kind)] for kind in layout]
    if not first:
        out_in, back_in = refs.pop(0), refs.pop(0)
    out_ref, back_ref = refs.pop(0), refs.pop(0)
    made = [refs.pop(0) for _ in layout]
    hid, dga, dup = refs[:3]
    if first:
        out_ref[...] = jnp.zeros_like(out_ref)
        back_ref[...] = jnp.zeros_like(back_ref)
    else:
        out_ref[...] = out_in[...]
        back_ref[...] = back_in[...]
    width = n2_ref.shape[1]
    half = 3 * width // 2
    for source, dw_ref in zip(sources, made):
        if len(source) == 2:
            hold = refs[3]
            hold[meta_ref[3]] = source[0][...]
            hold[1 - meta_ref[3]] = source[1][...]

            def take(part, cols, hold=hold):
                if part == 0:
                    return hold[0, :width, cols]
                if part == 2:
                    return hold[1, half - width :, cols]
                return jnp.concatenate([hold[0, width:, cols], hold[1, : half - width, cols]], axis=0)
        else:

            def take(part, cols, hold=source[0]):
                return hold[part, :, cols]

        for part in range(2):
            cols = slice(part * block, (part + 1) * block)
            wg = take(0, cols)
            wu = take(1, cols)
            wl = take(2, cols)
            n2 = n2_ref[...]
            gate = nn(n2, wg)
            up = nn(n2, wu)
            grad = nn(g_ref[...], wl)
            sigma = 1.0 / (1.0 + jnp.exp(-gate))
            silu = gate * sigma
            hid[...] = (silu * up).astype(BF16)
            dup[...] = (grad * silu).astype(BF16)
            dga[...] = (grad * up * (sigma * (1.0 + gate * (1.0 - sigma)))).astype(BF16)
            out_ref[...] += nt(hid[...], wl)
            back_ref[...] += nt(dga[...], wg) + nt(dup[...], wu)
            dw_ref[0, :, cols] = nn(n2t_ref[...], dga[...]).astype(BF16)
            dw_ref[1, :, cols] = nn(n2t_ref[...], dup[...]).astype(BF16)
            dw_ref[2, :, cols] = nn(gt_ref[...], hid[...]).astype(BF16)


def mlp(meta, n2, n2t, g, gt, weights, before=()):
    width = n2.shape[1]
    units = 512
    layout = tuple(len(w) for w in weights)
    out = [struct((LEN, width), F32)] * 2 + [struct((3, width, units), BF16)] * len(weights)
    args = (meta, n2, n2t, g, gt, *[a for w in weights for a in w], *before)
    scratch = [pltpu.VMEM((LEN, 256), BF16)] * 3
    if 2 in layout:
        scratch.append(pltpu.VMEM((2, 3 * width // 2, units), BF16))
    aliases = {len(args) - 2: 0, len(args) - 1: 1} if before else {}
    return call(
        functools.partial(mlp_body, layout, not before),
        "mlp",
        out,
        args,
        50,
        in_specs=[SM] + [VM] * (len(args) - 1),
        out_specs=[VM] * len(out),
        scratch_shapes=scratch,
        input_output_aliases=aliases,
    )


def norm_back(grad, value, gain):
    scale = lax.rsqrt(jnp.mean(value * value, axis=-1, keepdims=True) + EPS)
    unit = value * scale
    gain_grad = jnp.sum(grad * unit, axis=0, keepdims=True)
    e = grad * gain
    return scale * (e - unit * jnp.mean(e * unit, axis=-1, keepdims=True)), gain_grad


def give(meta_ref, value, refs):
    slot = pl.program_id(0) ^ meta_ref[2]
    for which, ref in enumerate(refs):

        @pl.when(slot == which)
        def _():
            ref[...] = value


def middle_body(
    meta_ref, x_ref, after_ref, sum_ref, back_ref, g_ref, gain_ref, mta_ref, mtb_ref,
    w0, w1, w2, w3, e0, e1, e2, e3, da_ref, do_ref, even_ref, odd_ref, gain_out, acc,
):
    step = pl.program_id(0)
    after = after_ref[...]
    delta = (after - x_ref[...].astype(F32) + sum_ref[...]).astype(BF16)
    give(meta_ref, delta, (e0, e1, e2, e3))
    back, gain_grad = norm_back(back_ref[...], after, gain_ref[...])
    grad_after = g_ref[...].astype(F32) + back
    da_ref[...] = grad_after
    low = grad_after.astype(BF16)

    @pl.when(step == 0)
    def _():
        gain_out[...] = jnp.zeros_like(gain_out)
        acc[...] = jnp.zeros_like(acc)

    gain_out[...] += gain_grad
    weights = turn_rows((w0, w1, w2, w3))
    do_ref[...] = nt(weights, low).astype(BF16)
    for turn in range(3):
        for which, mt in enumerate((mta_ref, mtb_ref)):
            acc[turn, which] += nn(mt[turn], low)

    @pl.when(step == pl.num_programs(0) - 1)
    def _():
        for turn in range(3):
            for slot in range(4):
                at = (slot % 2) * HD
                ref = odd_ref if slot % 2 else even_ref
                ref[slot // 2, turn * HD : (turn + 1) * HD, :] = acc[turn, slot // 2, at : at + HD, :].astype(BF16)


def middle(meta, x, after, total, back, g, gain, mts, wo):
    width = x.shape[1]
    step = 256
    rows = pl.BlockSpec((step, width), lambda i: (i, 0))
    full = lambda a: pl.BlockSpec(a.shape, lambda i, n=a.ndim: (0,) * n)
    heads = pl.BlockSpec((3, 2 * HD, step), lambda i: (0, 0, i))
    args = (meta, x, after, total, back, g, gain, *mts, *wo)
    out = [struct((step, width), BF16)] * 4 + [
        struct((LEN, width), F32),
        struct((12 * HD, LEN), BF16),
        struct((2, 3 * HD, width), BF16),
        struct((2, 3 * HD, width), BF16),
        struct((1, width), F32),
    ]
    return call(
        middle_body,
        "middle",
        out,
        args,
        40,
        grid=(LEN // step,),
        in_specs=[SM] + [rows] * 5 + [full(gain), heads, heads] + [full(w) for w in wo],
        out_specs=[full(o) for o in out[:4]]
        + [rows, pl.BlockSpec((12 * HD, step), lambda i: (0, i)), full(out[6]), full(out[7]), full(out[8])],
        scratch_shapes=[pltpu.VMEM((3, 2, 2 * HD, width), F32)],
    )


def token_grad_body(turns, last, meta_ref, *refs):
    dts = refs[: len(turns)]
    weights = refs[len(turns) : len(turns) + 4]
    rest = refs[len(turns) + 4 :]
    step = pl.program_id(0)
    total = None
    for turn, dt in zip(turns, dts):
        for part in range(3):
            w = jnp.concatenate([w[part, turn * HD : (turn + 1) * HD, :] for w in weights], axis=0)
            more = nn(dt[part].T, w)
            total = more if total is None else total + more
    if not last:
        rest[0][...] = total
        return
    before_ref, x_ref, da_ref, g_ref, gain_ref, e0, e1, e2, e3, gain_out = rest
    total = total + before_ref[...]
    back, gain_grad = norm_back(total, x_ref[...].astype(F32), gain_ref[...])
    give(meta_ref, (da_ref[...] - g_ref[...].astype(F32) + back).astype(BF16), (e0, e1, e2, e3))

    @pl.when(step == 0)
    def _():
        gain_out[...] = jnp.zeros_like(gain_out)

    gain_out[...] += gain_grad


def token_grad(meta, turns, dts, weights, rest=None):
    width = weights[0].shape[2]
    step = 256
    rows = pl.BlockSpec((step, width), lambda i: (i, 0))
    full = lambda a: pl.BlockSpec(a.shape, lambda i, n=a.ndim: (0,) * n)
    cols = pl.BlockSpec((3, 4 * HD, step), lambda i: (0, 0, i))
    specs = [SM] + [cols] * len(dts) + [full(w) for w in weights]
    args = (meta, *dts, *weights)
    if rest is None:
        out = [struct((LEN, width), F32)]
        out_specs = [rows]
    else:
        out = [struct((step, width), BF16)] * 4 + [struct((1, width), F32)]
        out_specs = [full(o) for o in out]
        specs = specs + [rows] * 4 + [full(rest[4])]
        args = args + tuple(rest)
    return call(
        functools.partial(token_grad_body, turns, rest is not None),
        "token_grad",
        out,
        args,
        30,
        grid=(LEN // step,),
        in_specs=specs,
        out_specs=out_specs,
    )


def rope_tables(length, width):
    halfway = width // 2
    inverse = 10000.0 ** (-jnp.arange(halfway, dtype=F32) * 2.0 / width)
    angles = inverse[:, None] * jnp.arange(length, dtype=F32)[None, :]
    return jnp.cos(angles), jnp.sin(angles)


def swap(value, axis, size, mask):
    return lax.ppermute(value, axis, [(i, i ^ mask) for i in range(size)])


def added(*refs):
    total = refs[0].astype(F32)
    for ref in refs[1:]:
        total = total + ref.astype(F32)
    return total.astype(BF16)


def put(cond, ref, at, value):
    @pl.when(cond)
    def _():
        if at is None:
            ref[...] = value
        else:
            ref[at] = value


def start_body(meta_ref, a0, b0, a2, b2, keep_p, send_p, keep_q, send_q):
    step = pl.program_id(0)
    bit = meta_ref[3]
    two = meta_ref[4]
    for slot, (a, b) in enumerate(((a0, b0), (a2, b2))):
        value = added(a[0], b[0])
        put(step == bit, keep_p, slot, value)
        put(step == 1 - bit, send_p, slot, value)
        put(step == 2 + two, keep_q, slot, value)
        put(step == 3 - two, send_q, slot, value)


def start_sums(meta, dw0, in1, dw2, in3):
    rows = dw0.shape[0] * dw0.shape[1] // 4
    cols = dw0.shape[2]
    parts = [a.reshape(4, rows, cols) for a in (dw0, in1, dw2, in3)]
    out = [struct((2, rows, cols), BF16)] * 4
    return call(
        start_body,
        "start_sums",
        out,
        (meta, *parts),
        16,
        grid=(4,),
        in_specs=[SM] + [pl.BlockSpec((1, rows, cols), lambda i: (i, 0, 0))] * 4,
        out_specs=[pl.BlockSpec((2, rows, cols), lambda i: (0, 0, 0))] * 4,
    )


def second_body(meta_ref, kp, rp, kq, rq, keep, send):
    for which, (k, r) in enumerate(((kp, rp), (kq, rq))):
        keep[which] = added(k[0], r[0])
        send[which] = added(k[1], r[1])


def second_sums(meta, kp, rp, kq, rq):
    _, rows, cols = kp.shape
    block = pl.BlockSpec((2, rows // 2, cols), lambda i: (0, i, 0))
    return call(
        second_body,
        "second_sums",
        [struct((2, rows, cols), BF16)] * 2,
        (meta, kp, rp, kq, rq),
        16,
        grid=(2,),
        in_specs=[SM] + [block] * 4,
        out_specs=[block] * 2,
    )


def third_body(meta_ref, a, b, keep, send_p, send_q):
    step = pl.program_id(0)
    two = meta_ref[4]
    bit = meta_ref[3]
    value = added(a[0, 0], b[0, 0])
    put(step == two, keep, 0, value)
    put(step == 1 - two, send_p, None, value)
    value = added(a[1, 0], b[1, 0])
    put(step == bit, keep, 1, value)
    put(step == 1 - bit, send_q, None, value)


def third_sums(meta, a, b):
    _, rows, cols = a.shape
    half = rows // 2
    views = [v.reshape(2, 2, half, cols) for v in (a, b)]
    return call(
        third_body,
        "third_sums",
        [struct((2, half, cols), BF16)] + [struct((half, cols), BF16)] * 2,
        (meta, *views),
        12,
        grid=(2,),
        in_specs=[SM] + [pl.BlockSpec((2, 1, half, cols), lambda i: (0, i, 0, 0))] * 2,
        out_specs=[pl.BlockSpec((2, half, cols), lambda i: (0, 0, 0))]
        + [pl.BlockSpec((half, cols), lambda i: (0, 0))] * 2,
    )


def halve_body(bit_ref, a, b0, b1, keep, send):
    bit = bit_ref[0]
    step = pl.program_id(0)
    for which, b in enumerate((b0, b1)):
        value = added(a[which, 0], b[0])
        put(step == bit, keep, which, value)
        put(step != bit, send, which, value)


def halve_sums(bit, a, b0, b1):
    _, rows, cols = a.shape
    half = rows // 2
    return call(
        halve_body,
        "halve_sums",
        [struct((2, half, cols), BF16)] * 2,
        (bit.reshape(1), a.reshape(2, 2, half, cols), b0.reshape(2, half, cols), b1.reshape(2, half, cols)),
        12,
        grid=(2,),
        in_specs=[SM, pl.BlockSpec((2, 1, half, cols), lambda i: (0, i, 0, 0))]
        + [pl.BlockSpec((1, half, cols), lambda i: (i, 0, 0))] * 2,
        out_specs=[pl.BlockSpec((2, half, cols), lambda i: (0, 0, 0))] * 2,
    )


def plain_body(tie_ref, a, b, out):
    out[...] = added(a[...], b[...])


def plain_sum(tie, a, b):
    return call(plain_body, "plain_sum", [struct(a.shape, BF16)], (tie, a, b), 12, in_specs=[SM, VM, VM], out_specs=[VM])[0]


def pair_body(bit_ref, a, b, out):
    bit = bit_ref[0]
    for which in range(2):
        out[which, bit] = a[which]
        out[which, 1 - bit] = b[which]


def pair_join(bit, a, b):
    _, rows, cols = a.shape
    made = call(
        pair_body,
        "pair_join",
        [struct((2, 2, rows, cols), BF16)],
        (bit.reshape(1), a, b),
        12,
        in_specs=[SM, VM, VM],
        out_specs=[VM],
    )[0]
    return made.reshape(2, 2 * rows, cols)


def cross_body(meta_ref, a, bp, bq, out_p, out_q):
    two = meta_ref[4]
    bit = meta_ref[3]
    out_p[two] = a[0]
    out_p[1 - two] = bp[...]
    out_q[bit] = a[1]
    out_q[1 - bit] = bq[...]


def cross_join(meta, a, bp, bq):
    _, rows, cols = a.shape
    made = call(
        cross_body,
        "cross_join",
        [struct((2, rows, cols), BF16)] * 2,
        (meta, a, bp, bq),
        12,
        in_specs=[SM, VM, VM, VM],
        out_specs=[VM, VM],
    )
    return [m.reshape(2 * rows, cols) for m in made]


def mlp_out_body(meta_ref, p, rp, q, rq, gu_ref, wd_ref, hold):
    bit = meta_ref[3]
    two = meta_ref[4]
    hold[bit] = p[...]
    hold[1 - bit] = rp[...]
    hold[2 + two] = q[...]
    hold[3 - two] = rq[...]
    rows = hold.shape[1]
    pair = gu_ref.shape[0]
    for which in range(2):
        gu_ref[which * rows : (which + 1) * rows, :] = hold[which].astype(F32)
    rest = pair - 2 * rows
    gu_ref[2 * rows :, :] = hold[2, :rest, :].astype(F32)
    wd_ref[:, : rows - rest] = hold[2, rest:, :].astype(F32).T
    wd_ref[:, rows - rest :] = hold[3].astype(F32).T


def mlp_out(meta, p, rp, q, rq, width):
    rows, units = p.shape
    return call(
        mlp_out_body,
        "mlp_out",
        [struct((2 * width, units), F32), struct((units, width), F32)],
        (meta, p, rp, q, rq),
        24,
        in_specs=[SM] + [VM] * 4,
        out_specs=[VM] * 2,
        scratch_shapes=[pltpu.VMEM((4, rows, units), BF16)],
    )


def core_body(count, meta_ref, *refs):
    evens, ins = refs[:count], refs[count : 2 * count]
    keep, send = refs[2 * count :]
    rows = evens[0].shape[1]
    for which, (a, b) in enumerate(zip(evens, ins)):
        keep[which * rows : (which + 1) * rows, :] = added(a[0], b[0])
        send[which * rows : (which + 1) * rows, :] = added(a[1], b[1])


def core_sums(meta, evens, ins):
    count = len(evens)
    _, rows, cols = evens[0].shape
    args = (meta, *evens, *ins)
    return call(
        functools.partial(core_body, count),
        "core_sums",
        [struct((count * rows, cols), BF16)] * 2,
        args,
        16,
        in_specs=[SM] + [VM] * (2 * count),
        out_specs=[VM] * 2,
    )


def spread_body(tie_ref, in_ref, out_ref):
    total = in_ref[0].astype(F32)
    for which in range(1, in_ref.shape[0]):
        total = total + in_ref[which].astype(F32)
    total = total.astype(BF16)
    for which in range(in_ref.shape[0]):
        out_ref[which] = total


def spread_sum(tie, pieces):
    return call(spread_body, "spread_sum", [struct(pieces.shape, BF16)], (tie, pieces), 16, in_specs=[SM, VM], out_specs=[VM])[0]


def exchange(value):
    return lax.all_to_all(value, "dp", 0, 0)


def attn_out_body(tie_ref, early_ref, late_ref, qkv_ref, wo_ref):
    wo_ref[...] = early_ref[: 3 * HD, :].astype(F32)
    for part in range(3):
        at = part * HD
        parts = [early_ref[3 * HD + at : 3 * HD + at + HD, :], early_ref[6 * HD + at : 6 * HD + at + HD, :]]
        parts.append(late_ref[at : at + HD, :])
        qkv_ref[part] = jnp.concatenate(parts, axis=0).astype(F32).T


def attn_out(tie, early, late):
    width = early.shape[1]
    return call(
        attn_out_body,
        "attn_out",
        [struct((3, width, 3 * HD), F32), struct((3 * HD, width), F32)],
        (tie, early, late),
        20,
        in_specs=[SM, VM, VM],
        out_specs=[VM, VM],
    )


def add_home_body(meta_ref, in_ref, p0, p1, p2, p3, out_ref):
    slot = pl.program_id(0) ^ meta_ref[2]
    for which, piece in enumerate((p0, p1, p2, p3)):

        @pl.when(slot == which)
        def _():
            out_ref[0] = in_ref[0] + piece[...].astype(F32)


def add_home(meta, base, pieces):
    count, rows, width = base.shape
    block = pl.BlockSpec((1, rows, width), lambda i: (i, 0, 0))
    full = pl.BlockSpec((rows, width), lambda i: (0, 0))
    return call(
        add_home_body,
        "add_home",
        [struct(base.shape, F32)],
        (meta, base, *pieces),
        16,
        grid=(count,),
        in_specs=[SM, block] + [full] * 4,
        out_specs=[block],
    )[0]


def tie(value, *after):
    return lax.optimization_barrier((value, *after))[0]


def local(n_dp, inputs, w_qkv, w_out, w_gate_up, w_down, gain_attn, gain_mlp, piece_starts, out_grad):
    width = inputs.shape[2]
    units = w_down.shape[0]
    here = lax.axis_index("tensor").astype(jnp.int32)
    row = lax.axis_index("dp").astype(jnp.int32)
    bit = row & 1
    bits = [(row >> s) & 1 for s in range(n_dp.bit_length() - 1)]
    mine = lax.dynamic_index_in_dim(piece_starts, here, 0, keepdims=False)[0]
    meta = jnp.concatenate([mine, jnp.stack([here, bits[0], bits[1]])])
    one = gain_attn[None]
    two = gain_mlp[None]
    cosine, sine = rope_tables(LEN, HD)
    tensor = functools.partial(swap, axis="tensor", size=4)
    dp = functools.partial(swap, axis="dp", size=n_dp)

    def picks(whole):
        return [lax.dynamic_index_in_dim(whole, here ^ k, 0, keepdims=False).astype(BF16) for k in range(4)]

    def around(pieces):
        return [pieces[0]] + [tensor(pieces[k], mask=k) for k in range(1, 4)]

    def far(half):
        direct = tensor(half, mask=2)
        other = dp(direct, mask=1)
        return direct, other, tensor(direct, mask=1), tensor(other, mask=1)

    x_mine = picks(inputs)
    xs = around(x_mine)
    wa0 = jnp.concatenate([jnp.swapaxes(w_qkv, 1, 2), w_out[None]]).astype(BF16)
    wa1 = tensor(wa0, mask=1)
    wa_far = far(lax.dynamic_slice_in_dim(wa0, 2 * bit, 2, 0))
    wm0 = jnp.concatenate([w_gate_up, w_down.T[None]]).astype(BF16)
    wm1 = tensor(wm0, mask=1)
    wm_far = far(lax.dynamic_slice_in_dim(wm0.reshape(3 * width, units), 3 * width // 2 * bit, 3 * width // 2, 0))
    gs = around(picks(out_grad))

    last = [meta]

    def run(kernel, first, *args, **kw):
        out = kernel(tie(first, last[0]), *args, **kw)
        last[0] = out[0] if isinstance(out, (list, tuple)) else out
        return out

    x, n1, qa, ka, va = run(project_first, meta, xs, one, wa0, wa1, cosine, sine)
    mta, ma, la = run(attend, meta, qa, ka, va)
    qb, kb, vb, wa2, wa3 = run(project_next, meta, n1, wa_far, cosine, sine)
    wa = (wa0, wa1, wa2, wa3)
    mtb, mb, lb = run(attend, meta, qb, kb, vb)
    after, n2, n2t, g, gt = run(after_attention, meta, x, ma, mb, wa, two, gs)
    acc_out, acc_back, dw1, dw0 = run(mlp, meta, n2, n2t, g, gt, ((wm1,), (wm0,)))
    in1 = tensor(dw1, mask=1)
    acc_out, acc_back, dw3 = run(mlp, meta, n2, n2t, g, gt, (wm_far[2:],), (acc_out, acc_back))
    in3 = tensor(dw3, mask=1)
    acc_out, acc_back, dw2 = run(mlp, meta, n2, n2t, g, gt, (wm_far[:2],), (acc_out, acc_back))
    keep_p, send_p, keep_q, send_q = run(start_sums, meta, dw0, in1, dw2, in3)
    recv_p = dp(send_p, mask=1)
    recv_q = dp(send_q, mask=2)
    middle_out = run(middle, meta, x, after, acc_out, acc_back, g, two, (mta, mtb), wa)
    home = around(middle_out[:4])
    da, do, even_o, odd_o, gain_two = middle_out[4:]
    in_o = tensor(odd_o, mask=1)
    sets = ((qa, ka, va, mta, la), (qb, kb, vb, mtb, lb))
    back = lambda turn: run(lambda m: attend_back(turn, m, cosine, sine, n1, sets, do), meta)
    dt0, even0, odd0 = back(0)
    in0 = tensor(odd0, mask=1)
    keep, send = run(second_sums, meta, keep_p, recv_p, keep_q, recv_q)
    recv = tensor(send, mask=2)
    dt1, even1, odd1 = back(1)
    in1_ = tensor(odd1, mask=1)
    outputs = run(add_home, meta, inputs, home)
    early, early_send = run(core_sums, meta, (even_o, even0, even1), (in_o, in0, in1_))
    early_recv = tensor(early_send, mask=2)
    keep, send_p, send_q = run(third_sums, meta, keep, recv)
    recv_p = dp(send_p, mask=2)
    recv_q = dp(send_q, mask=1)
    (before,) = run(lambda m: token_grad(m, (0, 1), (dt0, dt1), wa), meta)
    pieces = (recv_p, recv_q)
    for shift in range(2, len(bits)):
        keep, send = run(halve_sums, bits[shift], keep, *pieces)
        pieces = dp(send, mask=1 << shift)
    dt2, even2, odd2 = back(2)
    in2 = tensor(odd2, mask=1)
    piece = run(plain_sum, meta, keep, pieces)
    other = dp(piece, mask=1 << (len(bits) - 1))
    early = run(plain_sum, meta, early, early_recv)
    early = exchange(early.reshape(n_dp, -1, width))
    late, late_send = run(core_sums, meta, (even2,), (in2,))
    late_recv = tensor(late_send, mask=2)
    *grads, gain_one = run(lambda m: token_grad(m, (2,), (dt2,), wa, (before, x, da, g, one)), meta)
    grads = around(grads)
    late = run(plain_sum, meta, late, late_recv)
    late = exchange(late.reshape(n_dp, -1, width))
    for shift in reversed(range(2, len(bits))):
        piece = run(pair_join, bits[shift], piece, other)
        if shift > 2:
            other = dp(piece, mask=1 << (shift - 1))
    recv_p = dp(piece[0], mask=2)
    recv_q = dp(piece[1], mask=1)
    early = exchange(run(spread_sum, meta, early))
    p, q = run(cross_join, meta, piece, recv_p, recv_q)
    recv_p = dp(p, mask=1)
    recv_q = dp(q, mask=2)
    gains = jnp.concatenate([gain_one, gain_two])
    gains = gains + tensor(gains, mask=1)
    gains = gains + tensor(gains, mask=2)
    for shift in range(len(bits)):
        gains = gains + dp(gains, mask=1 << shift)
    late = exchange(run(spread_sum, meta, late))
    input_grad = run(add_home, meta, out_grad, grads)
    grad_pair, grad_down = run(mlp_out, meta, p, recv_p, q, recv_q, width)
    grad_qkv, grad_out = run(attn_out, meta, early.reshape(9 * HD, width), late.reshape(3 * HD, width))
    return (
        outputs,
        input_grad,
        grad_qkv,
        grad_out,
        grad_pair.reshape(2, width, units),
        grad_down,
        gains[0],
        gains[1],
    )


def solution(mesh):
    rows = P(None, ("dp", "tensor"), None)
    weights = (P(None, None, "tensor"), P("tensor", None), P(None, None, "tensor"), P("tensor", None))
    return jax.shard_map(
        functools.partial(local, mesh.shape["dp"]),
        mesh=mesh,
        in_specs=(rows, *weights, P(), P(), P(None, "dp", None), rows),
        out_specs=(rows, rows, *weights, P(), P()),
        check_vma=False,
    )
```

time: 516 us -> 476 us (0.922)
  Pallas kernels: 250 us -> 171 us
  local copies, waits for them, and re-layouts: 25.5 us -> 62 us
  starting transfers between devices: 78.5 us -> 56.3 us
  waiting for transfers between devices: 142 us -> 160 us
  blocking collectives: 0 us -> 14.5 us
  other arithmetic: 12.2 us -> 6.33 us
    pallas_call x35 -> x31, Pallas kernels: 250 us -> 171 us  [call(): pl.pallas_call(body, name=name, out_shape=out_shape, compiler_params=pltp...]
    unnamed x159 -> x230, local copies, waits for them, and re-layouts: 10.9 us -> 57.3 us
    ppermute x77 -> x46, starting transfers between devices: 78.5 us -> 44.2 us  [swap(): return lax.ppermute(value, axis, [(i, i ^ mask) for i in range(size)])]
    ppermute x77 -> x46, waiting for transfers between devices: 142 us -> 160 us  [swap(): return lax.ppermute(value, axis, [(i, i ^ mask) for i in range(size)])]
    all_to_all x0 -> x1, blocking collectives: none -> 14.5 us  [exchange(): return lax.all_to_all(value, 'dp', 0, 0)]
    all_to_all x0 -> x3, starting transfers between devices: none -> 12.1 us  [exchange(): return lax.all_to_all(value, 'dp', 0, 0)]
    slice x4 -> x1, local copies, waits for them, and re-layouts: 6.05 us -> 0.04 us  [local(): recv_q = dp(piece[1], mask=1)]
  transfers between devices with their start and end apart: 77 -> 49, of which waited for: 22 -> 20; matrix products, arithmetic and copies ran while one was open for 6% -> 2% of each run, Pallas kernels for 47% -> 34%
where the time goes in v2:
time: 476 us; the launch traced here: 472 us
  Pallas kernels  171 us (36%)
  waiting for transfers between devices  160 us (34%)
  local copies, waits for them, and re-layouts  62 us (13%)
  starting transfers between devices  56.3 us (12%)
  blocking collectives  14.5 us (3%)
  other arithmetic  6.33 us (1%)
    pallas_call x31, Pallas kernels, call(): pl.pallas_call(body, name=name, out_shape=out_shape, compiler_params=pltp...  171 us
    ppermute x46, waiting for transfers between devices, swap(): return lax.ppermute(value, axis, [(i, i ^ mask) for i in range(size)])  160 us
    unnamed x230, local copies, waits for them, and re-layouts  57.3 us
    ppermute x46, starting transfers between devices, swap(): return lax.ppermute(value, axis, [(i, i ^ mask) for i in range(size)])  44.2 us
    all_to_all x1, blocking collectives, exchange(): return lax.all_to_all(value, 'dp', 0, 0)  14.5 us
    all_to_all x3, starting transfers between devices, exchange(): return lax.all_to_all(value, 'dp', 0, 0)  12.1 us
  transfers between devices with their start and end apart: 49, of which 20 were waited for; matrix products, arithmetic and copies ran while one was open for 2% of the time, Pallas kernels for 34%

profile of v2, /device:TPU:0, one launch (start us, length us, event | category | flops | bytes accessed | tf_op | source)
XLA Modules:
  0.0 471.6 jit_solution(1397833577584407248)
XLA Ops:
  17.4 20.9 %collective-permute-done.12.refs_0_ = bf16[1152,512]{1,0:T(8,128)(2,1)} collective-permute-done((bf16[1152,512]{1,0:T(8,128)(2,1)}, bf16[1152,512]{1,0:T(8,128)(2,1)}, u32[]{:S(2)}, u32[]{:S(2)}) %collective-permute-start.12) | collective-permute-done | bytes 1179680 | tf_op jit(solution)/shard_map/ppermute | solution.py:561
  41.4 4.9 %collective-permute-done.2.p3 = bf16[256,768]{1,0:T(8,128)(2,1)S(1)} collective-permute-done((bf16[256,768]{1,0:T(8,128)(2,1)}, bf16[256,768]{1,0:T(8,128)(2,1)S(1)}, u32[]{:S(2)}, u32[]{:S(2)}) %collective-permute-start.2) | collective-permute-done | bytes 393248 | tf_op jit(solution)/shard_map/ppermute | solution.py:561
  47.7 7.5 %collective-permute-done.1.p2 = bf16[256,768]{1,0:T(8,128)(2,1)S(1)} collective-permute-done((bf16[256,768]{1,0:T(8,128)(2,1)}, bf16[256,768]{1,0:T(8,128)(2,1)S(1)}, u32[]{:S(2)}, u32[]{:S(2)}) %collective-permute-start.1) | collective-permute-done | bytes 393248 | tf_op jit(solution)/shard_map/ppermute | solution.py:561
  55.9 11.9 %collective-permute-done.4.d2 = bf16[2,192,768]{2,1,0:T(8,128)(2,1)S(1)} collective-permute-done((bf16[2,192,768]{2,1,0:T(8,128)(2,1)S(1)}, bf16[2,192,768]{2,1,0:T(8,128)(2,1)S(1)}, u32[]{:S(2)}, u32[]{:S(2)}) %collective-permute-start.4) | collective-permute-done | bytes 589856 | tf_op jit(solution)/shard_map/ppermute | solution.py:561
  69.2 5.5 %collective-permute-done.10.g3 = bf16[256,768]{1,0:T(8,128)(2,1)S(1)} collective-permute-done((bf16[256,768]{1,0:T(8,128)(2,1)S(1)}, bf16[256,768]{1,0:T(8,128)(2,1)S(1)}, u32[]{:S(2)}, u32[]{:S(2)}) %collective-permute-start.10) | collective-permute-done | bytes 393248 | tf_op jit(solution)/shard_map/ppermute | solution.py:561
  78.2 13.1 %collective-permute-done.5.r2 = bf16[2,192,768]{2,1,0:T(8,128)(2,1)} collective-permute-done((bf16[2,192,768]{2,1,0:T(8,128)(2,1)S(1)}, bf16[2,192,768]{2,1,0:T(8,128)(2,1)}, u32[]{:S(2)}, u32[]{:S(2)}) %collective-permute-start.5) | collective-permute-done | bytes 589856 | tf_op jit(solution)/shard_map/ppermute | solution.py:561
  102.8 10.3 %attend.2 = (bf16[3,128,1024]{2,1,0:T(8,128)(2,1)S(1)}, bf16[1024,384]{1,0:T(8,128)(2,1)S(1)}, f32[3,2,1024]{2,1,0:T(2,128)S(1)}) custom-call(s32[5]{0:T(128)S(1)} %pad_add_fusion.meta_ref.starts_ref.tie_ref, bf16[3,128,1024]{2,1,0:T(8,128)(2,1)S(1)} %get-tuple-element.117.q_ref.refs_0_, bf16[3,128,1024]{2,1,0:T(8,128)(2,1)S(1)} %get-tuple-element.118.k_ref.refs_1_, ...), custom_call_target="tpu_custom_call" | custom-call | flops 1000000 | bytes 10000 | tf_op jit(solution)/shard_map/attend/pallas_call | solution.py:29
  120.4 10.3 %attend.3 = (bf16[3,128,1024]{2,1,0:T(8,128)(2,1)S(1)}, bf16[1024,384]{1,0:T(8,128)(2,1)S(1)}, f32[3,2,1024]{2,1,0:T(2,128)S(1)}) custom-call(s32[5]{0:T(128)S(1)} %pad_add_fusion.meta_ref.starts_ref.tie_ref, bf16[3,128,1024]{2,1,0:T(8,128)(2,1)S(1)} %get-tuple-element.123.q_ref.refs_5_, bf16[3,128,1024]{2,1,0:T(8,128)(2,1)S(1)} %get-tuple-element.125.k_ref.refs_6_, ...), custom_call_target="tpu_custom_call" | custom-call | flops 1000000 | bytes 10000 | tf_op jit(solution)/shard_map/attend/pallas_call | solution.py:29
  143.0 22.3 %mlp.3 = (f32[1024,768]{1,0:T(8,128)}, f32[1024,768]{1,0:T(8,128)}, bf16[3,768,512]{2,1,0:T(8,128)(2,1)}, bf16[3,768,512]{2,1,0:T(8,128)(2,1)}) custom-call(s32[5]{0:T(128)S(1)} %pad_add_fusion.meta_ref.starts_ref.tie_ref, bf16[1024,768]{1,0:T(8,128)(2,1)S(1)} %get-tuple-element.135.n2_ref, bf16[768,1024]{1,0:T(8,128)(2,1)S(1)} %get-tuple-element.136.n2t_ref, ...), custom_call_target="tpu_custom_call" | custom-call | flops 1000000 | bytes 10000 | tf_op jit(solution)/shard_map/mlp/pallas_call | solution.py:29
  165.7 14.6 %mlp.4 = (f32[1024,768]{1,0:T(8,128)}, f32[1024,768]{1,0:T(8,128)}, bf16[3,768,512]{2,1,0:T(8,128)(2,1)}) custom-call(s32[5]{0:T(128)S(1)} %pad_add_fusion.meta_ref.starts_ref.tie_ref, bf16[1024,768]{1,0:T(8,128)(2,1)S(1)} %get-tuple-element.135.n2_ref, bf16[768,1024]{1,0:T(8,128)(2,1)} %copy-done.20, ...), custom_call_target="tpu_custom_call", output_to_operand_aliasing={{0}: (7, {}), {1}: (8, {})} | custom-call | flops 1000000 | bytes 10000 | tf_op jit(solution)/shard_map/mlp/pallas_call | solution.py:29
  180.4 15.0 %mlp.5 = (f32[1024,768]{1,0:T(8,128)}, f32[1024,768]{1,0:T(8,128)}, bf16[3,768,512]{2,1,0:T(8,128)(2,1)}) custom-call(s32[5]{0:T(128)S(1)} %pad_add_fusion.meta_ref.starts_ref.tie_ref, bf16[1024,768]{1,0:T(8,128)(2,1)S(1)} %get-tuple-element.135.n2_ref, bf16[768,1024]{1,0:T(8,128)(2,1)} %copy-done.20, ...), custom_call_target="tpu_custom_call", output_to_operand_aliasing={{0}: (7, {}), {1}: (8, {})} | custom-call | flops 1000000 | bytes 10000 | tf_op jit(solution)/shard_map/mlp/pallas_call | solution.py:29
  198.8 6.2 %start_sums.1 = (bf16[2,576,512]{2,1,0:T(8,128)(2,1)S(1)}, bf16[2,576,512]{2,1,0:T(8,128)(2,1)}, bf16[2,576,512]{2,1,0:T(8,128)(2,1)S(1)}, bf16[2,576,512]{2,1,0:T(8,128)(2,1)}) custom-call(s32[5]{0:T(128)S(1)} %pad_add_fusion.meta_ref.starts_ref.tie_ref, bf16[4,576,512]{2,1,0:T(8,128)(2,1)S(1)} %bitcast.50, bf16[4,576,512]{2,1,0:T(8,128)(2,1)} %bitcast.17.b0, ...), custom_call_target="tpu_custom_call" | custom-call | flops 1000000 | bytes 10000 | tf_op jit(solution)/shard_map/start_sums/pallas_call | solution.py:29
  209.4 10.1 %middle.1 = (bf16[256,768]{1,0:T(8,128)(2,1)S(1)}, bf16[256,768]{1,0:T(8,128)(2,1)}, bf16[256,768]{1,0:T(8,128)(2,1)}, bf16[256,768]{1,0:T(8,128)(2,1)S(1)}, f32...) custom-call(s32[5]{0:T(128)S(1)} %pad_add_fusion.meta_ref.starts_ref, ...), custom_call_target="tpu_custom_call" | custom-call | flops 1000000 | bytes 10000 | tf_op jit(solution)/shard_map/middle/pallas_call | solution.py:29
  219.7 12.0 %attend_back.3 = (bf16[3,256,1024]{2,1,0:T(8,128)(2,1)S(1)}, bf16[2,192,768]{2,1,0:T(8,128)(2,1)S(1)}, bf16[2,192,768]{2,1,0:T(8,128)(2,1)}) custom-call(s32[5]{0:T(128)S(1)} %pad_add_fusion.meta_ref.starts_ref.tie_ref, f32[32,1024]{1,0:T(8,128)S(1)} %copy-done.55, f32[32,1024]{1,0:T(8,128)S(1)} %copy-done.52, ...), custom_call_target="tpu_custom_call" | custom-call | flops 1000000 | bytes 10000 | tf_op jit(solution)/shard_map/attend_back/pallas_call | solution.py:29
  241.7 11.1 %attend_back.4 = (bf16[3,256,1024]{2,1,0:T(8,128)(2,1)S(1)}, bf16[2,192,768]{2,1,0:T(8,128)(2,1)S(1)}, bf16[2,192,768]{2,1,0:T(8,128)(2,1)S(1)}) custom-call(s32[5]{0:T(128)S(1)} %pad_add_fusion.meta_ref.starts_ref.tie_ref, f32[32,1024]{1,0:T(8,128)S(1)} %copy-done.55, f32[32,1024]{1,0:T(8,128)S(1)} %copy-done.52, ...), custom_call_target="tpu_custom_call" | custom-call | flops 1000000 | bytes 10000 | tf_op jit(solution)/shard_map/attend_back/pallas_call | solution.py:29
  252.9 21.8 %collective-permute-done.21.p2 = bf16[256,768]{1,0:T(8,128)(2,1)S(1)} collective-permute-done((bf16[256,768]{1,0:T(8,128)(2,1)}, bf16[256,768]{1,0:T(8,128)(2,1)S(1)}, u32[]{:S(2)}, u32[]{:S(2)}) %collective-permute-start.21) | collective-permute-done | bytes 393248 | tf_op jit(solution)/shard_map/ppermute | solution.py:561
  274.7 11.6 %collective-permute-done.22.p3 = bf16[256,768]{1,0:T(8,128)(2,1)S(1)} collective-permute-done((bf16[256,768]{1,0:T(8,128)(2,1)}, bf16[256,768]{1,0:T(8,128)(2,1)S(1)}, u32[]{:S(2)}, u32[]{:S(2)}) %collective-permute-start.22) | collective-permute-done | bytes 393248 | tf_op jit(solution)/shard_map/ppermute | solution.py:561
  314.6 11.1 %attend_back.5 = (bf16[3,256,1024]{2,1,0:T(8,128)(2,1)S(1)}, bf16[2,192,768]{2,1,0:T(8,128)(2,1)S(1)}, bf16[2,192,768]{2,1,0:T(8,128)(2,1)S(1)}) custom-call(s32[5]{0:T(128)S(1)} %pad_add_fusion.meta_ref.starts_ref.tie_ref, f32[32,1024]{1,0:T(8,128)S(1)} %copy-done.56, f32[32,1024]{1,0:T(8,128)S(1)} %copy-done.53, bf16[1024,768]{1,0:T(8,128)(2,1)S(1)} %copy-done.9, ...), custom_call_target="tpu_custom_call" | custom-call | flops 1000000 | bytes 10000 | tf_op jit(solution)/shard_map/attend_back/pallas_call | solution.py:29
  359.2 11.1 %collective-permute-done.33.b = bf16[2,144,512]{2,1,0:T(8,128)(2,1)S(1)} collective-permute-done((bf16[2,144,512]{2,1,0:T(8,128)(2,1)}, bf16[2,144,512]{2,1,0:T(8,128)(2,1)S(1)}, u32[]{:S(2)}, u32[]{:S(2)}) %collective-permute-start.33) | collective-permute-done | bytes 294944 | tf_op jit(solution)/shard_map/ppermute | solution.py:561
  378.8 8.7 %collective-permute-done.34.bp = bf16[288,512]{1,0:T(8,128)(2,1)S(1)} collective-permute-done((bf16[288,512]{1,0:T(8,128)(2,1)S(1)}, bf16[288,512]{1,0:T(8,128)(2,1)S(1)}, u32[]{:S(2)}, u32[]{:S(2)}) %collective-permute-start.34) | collective-permute-done | bytes 294944 | tf_op jit(solution)/shard_map/ppermute | solution.py:561
  391.4 14.5 %all_to_all.20 = bf16[8,24,768]{2,1,0:T(8,128)(2,1)S(1)} all-to-all(bf16[8,24,768]{2,1,0:T(8,128)(2,1)S(1)} %spread_sum.3), channel_id=1, replica_groups=mesh['dp'=8,'tensor'=4] {'dp'}, dimensions={0} | all-to-all | bytes 589824 | tf_op jit(solution)/shard_map/all_to_all | solution.py:805
  417.4 16.5 %collective-permute-done.43 = f32[2,768]{1,0:T(2,128)S(1)} collective-permute-done((f32[2,768]{1,0:T(2,128)S(1)}, f32[2,768]{1,0:T(2,128)S(1)}, u32[]{:S(2)}, u32[]{:S(2)}) %collective-permute-start.43) | collective-permute-done | bytes 6176 | tf_op jit(solution)/shard_map/ppermute | solution.py:561
  443.7 8.9 %collective-permute-done.37.p2 = bf16[256,768]{1,0:T(8,128)(2,1)S(1)} collective-permute-done((bf16[256,768]{1,0:T(8,128)(2,1)}, bf16[256,768]{1,0:T(8,128)(2,1)S(1)}, u32[]{:S(2)}, u32[]{:S(2)}) %collective-permute-start.37) | collective-permute-done | bytes 393248 | tf_op jit(solution)/shard_map/ppermute | solution.py:561
  452.6 7.5 %collective-permute-done.38.p3 = bf16[256,768]{1,0:T(8,128)(2,1)S(1)} collective-permute-done((bf16[256,768]{1,0:T(8,128)(2,1)}, bf16[256,768]{1,0:T(8,128)(2,1)S(1)}, u32[]{:S(2)}, u32[]{:S(2)}) %collective-permute-start.38) | collective-permute-done | bytes 393248 | tf_op jit(solution)/shard_map/ppermute | solution.py:561
  (358 shorter events, 182.5 us)
Async XLA Ops:
  8.3 30.1 %collective-permute-start.12 = (bf16[1152,512]{1,0:T(8,128)(2,1)}, bf16[1152,512]{1,0:T(8,128)(2,1)}, u32[]{:S(2)}, u32[]{:S(2)}) collective-permute-start(bf16[1152,512]{1,0:T(8,128)(2,1)} %constant_dynamic-slice_fusion), channel_id=1, source_target_pairs={{0,2},{1,3},{2,0},{3,1},{4,6},{5,7},{6,4},{7,5},{8,10},{9,11},{10,... | collective-permute-start | bytes 3538952 | tf_op jit(solution)/shard_map/ppermute | solution.py:561
  12.3 34.1 %collective-permute-start.2 = (bf16[256,768]{1,0:T(8,128)(2,1)}, bf16[256,768]{1,0:T(8,128)(2,1)S(1)}, u32[]{:S(2)}, u32[]{:S(2)}) collective-permute-start(bf16[256,768]{1,0:T(8,128)(2,1)} %get-tuple-element.234), channel_id=1, source_target_pairs={{0,3},{1,2},{2,1},{3,0},{4,7},{5,6},{6,5},{7,4},{8,11},{9,10},{10,... | collective-permute-start | bytes 1179656 | tf_op jit(solution)/shard_map/ppermute | solution.py:561
  12.3 42.8 %collective-permute-start.1 = (bf16[256,768]{1,0:T(8,128)(2,1)}, bf16[256,768]{1,0:T(8,128)(2,1)S(1)}, u32[]{:S(2)}, u32[]{:S(2)}) collective-permute-start(bf16[256,768]{1,0:T(8,128)(2,1)} %get-tuple-element.235), channel_id=1, source_target_pairs={{0,2},{1,3},{2,0},{3,1},{4,6},{5,7},{6,4},{7,5},{8,10},{9,11},{10,... | collective-permute-start | bytes 1179656 | tf_op jit(solution)/shard_map/ppermute | solution.py:561
  16.5 51.2 %collective-permute-start.4 = (bf16[2,192,768]{2,1,0:T(8,128)(2,1)S(1)}, bf16[2,192,768]{2,1,0:T(8,128)(2,1)S(1)}, u32[]{:S(2)}, u32[]{:S(2)}) collective-permute-start(bf16[2,192,768]{2,1,0:T(8,128)(2,1)S(1)} %fusion), channel_id=1, source_target_pairs={{0,2},{1,3},{2,0},{3,1},{4,6},{5,7},{6,4},{7,5},{8,10},{9,11},{10,... | collective-permute-start | bytes 1769480 | tf_op jit(solution)/shard_map/ppermute | solution.py:561
  17.4 125.5 %collective-permute-start.11 = (bf16[3,768,512]{2,1,0:T(8,128)(2,1)}, bf16[3,768,512]{2,1,0:T(8,128)(2,1)}, u32[]{:S(2)}, u32[]{:S(2)}) collective-permute-start(bf16[3,768,512]{2,1,0:T(8,128)(2,1)} %copy-done.112), channel_id=1, source_target_pairs={{0,1},{1,0},{2,3},{3,2},{4,5},{5,4},{6,7},{7,6},{8,9},{9,8},{10,11... | collective-permute-start | bytes 7077896 | tf_op jit(solution)/shard_map/ppermute | solution.py:561
  38.4 39.8 %collective-permute-start.14 = (bf16[1152,512]{1,0:T(8,128)(2,1)}, bf16[1152,512]{1,0:T(8,128)(2,1)}, u32[]{:S(2)}, u32[]{:S(2)}) collective-permute-start(bf16[1152,512]{1,0:T(8,128)(2,1)} %collective-permute-done.12.refs_0_), channel_id=1, source_target_pairs={{0,4},{4,0},{8,12},{12,8},{16,20},{20,16},{24,28},{28,24},{1,5},{5... | collective-permute-start | bytes 3538952 | tf_op jit(solution)/shard_map/ppermute | solution.py:561
  77.7 88.0 %collective-permute-start.13 = (bf16[1152,512]{1,0:T(8,128)(2,1)}, bf16[1152,512]{1,0:T(8,128)(2,1)}, u32[]{:S(2)}, u32[]{:S(2)}) collective-permute-start(bf16[1152,512]{1,0:T(8,128)(2,1)} %collective-permute-done.12.refs_0_), channel_id=1, source_target_pairs={{0,1},{1,0},{2,3},{3,2},{4,5},{5,4},{6,7},{7,6},{8,9},{9,8},{10,11... | collective-permute-start | bytes 3538952 | tf_op jit(solution)/shard_map/ppermute | solution.py:561
  78.2 87.5 %collective-permute-start.15 = (bf16[1152,512]{1,0:T(8,128)(2,1)}, bf16[1152,512]{1,0:T(8,128)(2,1)}, u32[]{:S(2)}, u32[]{:S(2)}) collective-permute-start(bf16[1152,512]{1,0:T(8,128)(2,1)} %collective-permute-done.14.refs_1_), channel_id=1, source_target_pairs={{0,1},{1,0},{2,3},{3,2},{4,5},{5,4},{6,7},{7,6},{8,9},{9,8},{10,11... | collective-permute-start | bytes 3538952 | tf_op jit(solution)/shard_map/ppermute | solution.py:561
  91.5 42.8 %collective-permute-start.9 = (bf16[256,768]{1,0:T(8,128)(2,1)}, bf16[256,768]{1,0:T(8,128)(2,1)S(1)}, u32[]{:S(2)}, u32[]{:S(2)}) collective-permute-start(bf16[256,768]{1,0:T(8,128)(2,1)} %get-tuple-element.231), channel_id=1, source_target_pairs={{0,2},{1,3},{2,0},{3,1},{4,6},{5,7},{6,4},{7,5},{8,10},{9,11},{10,... | collective-permute-start | bytes 1179656 | tf_op jit(solution)/shard_map/ppermute | solution.py:561
  93.6 40.7 %collective-permute-start.8 = (bf16[256,768]{1,0:T(8,128)(2,1)}, bf16[256,768]{1,0:T(8,128)(2,1)S(1)}, u32[]{:S(2)}, u32[]{:S(2)}) collective-permute-start(bf16[256,768]{1,0:T(8,128)(2,1)} %get-tuple-element.232), channel_id=1, source_target_pairs={{0,1},{1,0},{2,3},{3,2},{4,5},{5,4},{6,7},{7,6},{8,9},{9,8},{10,11... | collective-permute-start | bytes 1179656 | tf_op jit(solution)/shard_map/ppermute | solution.py:561
  165.3 30.1 %collective-permute-start.16 = (bf16[3,768,512]{2,1,0:T(8,128)(2,1)}, bf16[3,768,512]{2,1,0:T(8,128)(2,1)}, u32[]{:S(2)}, u32[]{:S(2)}) collective-permute-start(bf16[3,768,512]{2,1,0:T(8,128)(2,1)} %get-tuple-element.148), channel_id=1, source_target_pairs={{0,1},{1,0},{2,3},{3,2},{4,5},{5,4},{6,7},{7,6},{8,9},{9,8},{10,11... | collective-permute-start | bytes 7077896 | tf_op jit(solution)/shard_map/ppermute | solution.py:561
  206.0 28.5 %collective-permute-start.18 = (bf16[2,576,512]{2,1,0:T(8,128)(2,1)}, bf16[2,576,512]{2,1,0:T(8,128)(2,1)S(1)}, u32[]{:S(2)}, u32[]{:S(2)}) collective-permute-start(bf16[2,576,512]{2,1,0:T(8,128)(2,1)} %get-tuple-element.161), channel_id=1, source_target_pairs={{0,4},{4,0},{8,12},{12,8},{16,20},{20,16},{24,28},{28,24},{1,5},{5... | collective-permute-start | bytes 3538952 | tf_op jit(solution)/shard_map/ppermute | solution.py:561
  219.6 33.3 %collective-permute-start.20 = (bf16[256,768]{1,0:T(8,128)(2,1)}, bf16[256,768]{1,0:T(8,128)(2,1)S(1)}, u32[]{:S(2)}, u32[]{:S(2)}) collective-permute-start(bf16[256,768]{1,0:T(8,128)(2,1)} %get-tuple-element.168), channel_id=1, source_target_pairs={{0,1},{1,0},{2,3},{3,2},{4,5},{5,4},{6,7},{7,6},{8,9},{9,8},{10,11... | collective-permute-start | bytes 1179656 | tf_op jit(solution)/shard_map/ppermute | solution.py:561
  239.2 53.2 %collective-permute-start.26 = (bf16[2,576,512]{2,1,0:T(8,128)(2,1)S(1)}, bf16[2,576,512]{2,1,0:T(8,128)(2,1)S(1)}, u32[]{:S(2)}, u32[]{:S(2)}) collective-permute-start(bf16[2,576,512]{2,1,0:T(8,128)(2,1)S(1)} %get-tuple-element.180), channel_id=1, source_target_pairs={{0,2},{1,3},{2,0},{3,1},{4,6},{5,7},{6,4},{7,5},{8,10},{9,11},{10,... | collective-permute-start | bytes 3538952 | tf_op jit(solution)/shard_map/ppermute | solution.py:561
  240.7 34.0 %collective-permute-start.21 = (bf16[256,768]{1,0:T(8,128)(2,1)}, bf16[256,768]{1,0:T(8,128)(2,1)S(1)}, u32[]{:S(2)}, u32[]{:S(2)}) collective-permute-start(bf16[256,768]{1,0:T(8,128)(2,1)} %get-tuple-element.169), channel_id=1, source_target_pairs={{0,2},{1,3},{2,0},{3,1},{4,6},{5,7},{6,4},{7,5},{8,10},{9,11},{10,... | collective-permute-start | bytes 1179656 | tf_op jit(solution)/shard_map/ppermute | solution.py:561
  241.2 47.8 %collective-permute-start.23 = (bf16[2,192,768]{2,1,0:T(8,128)(2,1)}, bf16[2,192,768]{2,1,0:T(8,128)(2,1)S(1)}, u32[]{:S(2)}, u32[]{:S(2)}) collective-permute-start(bf16[2,192,768]{2,1,0:T(8,128)(2,1)} %get-tuple-element.175), channel_id=1, source_target_pairs={{0,1},{1,0},{2,3},{3,2},{4,5},{5,4},{6,7},{7,6},{8,9},{9,8},{10,11... | collective-permute-start | bytes 1769480 | tf_op jit(solution)/shard_map/ppermute | solution.py:561
  241.2 47.8 %collective-permute-start.24 = (bf16[2,192,768]{2,1,0:T(8,128)(2,1)}, bf16[2,192,768]{2,1,0:T(8,128)(2,1)S(1)}, u32[]{:S(2)}, u32[]{:S(2)}) collective-permute-start(bf16[2,192,768]{2,1,0:T(8,128)(2,1)} %get-tuple-element.176), channel_id=1, source_target_pairs={{0,1},{1,0},{2,3},{3,2},{4,5},{5,4},{6,7},{7,6},{8,9},{9,8},{10,11... | collective-permute-start | bytes 1769480 | tf_op jit(solution)/shard_map/ppermute | solution.py:561
  252.9 36.2 %collective-permute-start.25 = (bf16[2,192,768]{2,1,0:T(8,128)(2,1)S(1)}, bf16[2,192,768]{2,1,0:T(8,128)(2,1)S(1)}, u32[]{:S(2)}, u32[]{:S(2)}) collective-permute-start(bf16[2,192,768]{2,1,0:T(8,128)(2,1)S(1)} %get-tuple-element.177), channel_id=1, source_target_pairs={{0,1},{1,0},{2,3},{3,2},{4,5},{5,4},{6,7},{7,6},{8,9},{9,8},{10,11... | collective-permute-start | bytes 1769480 | tf_op jit(solution)/shard_map/ppermute | solution.py:561
  291.8 36.9 %collective-permute-start.30 = (bf16[576,768]{1,0:T(8,128)(2,1)}, bf16[576,768]{1,0:T(8,128)(2,1)}, u32[]{:S(2)}, u32[]{:S(2)}) collective-permute-start(bf16[576,768]{1,0:T(8,128)(2,1)} %get-tuple-element.192), channel_id=1, source_target_pairs={{0,2},{1,3},{2,0},{3,1},{4,6},{5,7},{6,4},{7,5},{8,10},{9,11},{10,... | collective-permute-start | bytes 2654216 | tf_op jit(solution)/shard_map/ppermute | solution.py:561
  331.1 39.2 %all-to-all-start = ((bf16[8,72,768]{2,1,0:T(8,128)(2,1)}), bf16[8,72,768]{2,1,0:T(8,128)(2,1)}, u32[]{:S(2)}, u32[]{:S(2)}) async-start(bf16[8,72,768]{2,1,0:T(8,128)(2,1)} %bitcast.49), calls=%async_computation | async-start | bytes 1769472 | tf_op jit(solution)/shard_map/all_to_all | solution.py:805
  340.2 30.1 %collective-permute-start.33 = (bf16[2,144,512]{2,1,0:T(8,128)(2,1)}, bf16[2,144,512]{2,1,0:T(8,128)(2,1)S(1)}, u32[]{:S(2)}, u32[]{:S(2)}) collective-permute-start(bf16[2,144,512]{2,1,0:T(8,128)(2,1)} %copy-done.74), channel_id=1, source_target_pairs={{0,16},{4,20},{8,24},{12,28},{16,0},{20,4},{24,8},{28,12},{1,17},{... | collective-permute-start | bytes 884744 | tf_op jit(solution)/shard_map/ppermute | solution.py:561
  405.9 61.4 %all-to-all-start.2 = ((bf16[8,72,768]{2,1,0:T(8,128)(2,1)}), bf16[8,72,768]{2,1,0:T(8,128)(2,1)}, u32[]{:S(2)}, u32[]{:S(2)}) async-start(bf16[8,72,768]{2,1,0:T(8,128)(2,1)} %copy-done.58), calls=%async_computation.2 | async-start | bytes 1769472 | tf_op jit(solution)/shard_map/all_to_all | solution.py:805
  413.4 50.5 %collective-permute-start.39 = (bf16[576,512]{1,0:T(8,128)(2,1)}, bf16[576,512]{1,0:T(8,128)(2,1)S(1)}, u32[]{:S(2)}, u32[]{:S(2)}) collective-permute-start(bf16[576,512]{1,0:T(8,128)(2,1)} %bitcast.55), channel_id=1, source_target_pairs={{0,4},{4,0},{8,12},{12,8},{16,20},{20,16},{24,28},{28,24},{1,5},{5... | collective-permute-start | bytes 1769480 | tf_op jit(solution)/shard_map/ppermute | solution.py:561
  415.2 48.6 %collective-permute-start.40 = (bf16[576,512]{1,0:T(8,128)(2,1)}, bf16[576,512]{1,0:T(8,128)(2,1)S(1)}, u32[]{:S(2)}, u32[]{:S(2)}) collective-permute-start(bf16[576,512]{1,0:T(8,128)(2,1)} %bitcast.57), channel_id=1, source_target_pairs={{0,8},{4,12},{8,0},{12,4},{16,24},{20,28},{24,16},{28,20},{1,9},{5... | collective-permute-start | bytes 1769480 | tf_op jit(solution)/shard_map/ppermute | solution.py:561
  (139 other events, 1932.0 us)

commit v3 on v2

--- a/solution.py
+++ b/solution.py
@@ -25,13 +25,29 @@
     return lax.dot_general(a, b, (((1,), (1,)), ((), ())), preferred_element_type=F32)
 
 
-def call(body, name, out_shape, args, vmem, cost=1e6, **kw):
+COST = {
+    "project_first": 5,
+    "project_next": 5,
+    "attend": 10,
+    "after_attention": 5,
+    "mlp": 15,
+    "middle": 10,
+    "attend_back": 4,
+    "token_grad": 1,
+    "start_sums": 1,
+    "add_home": 0.2,
+    "mlp_out": 0.5,
+}
+RATE = 1e9
+
+
+def call(body, name, out_shape, args, vmem, **kw):
     return pl.pallas_call(
         body,
         name=name,
         out_shape=out_shape,
         compiler_params=pltpu.CompilerParams(vmem_limit_bytes=vmem * MIB),
-        cost_estimate=pl.CostEstimate(flops=int(cost), bytes_accessed=int(cost) // 100, transcendentals=0),
+        cost_estimate=pl.CostEstimate(flops=int(COST.get(name, 0.3) * RATE), bytes_accessed=0, transcendentals=0),
         **kw,
     )(*args)
 
@@ -427,21 +443,27 @@
 
 def give(meta_ref, value, refs):
     slot = pl.program_id(0) ^ meta_ref[2]
-    for which, ref in enumerate(refs):
+    for which, ref in enumerate(refs[:2]):
 
         @pl.when(slot == which)
         def _():
             ref[...] = value
 
+    for which in range(2):
+
+        @pl.when(slot == 2 + which)
+        def _():
+            refs[2][which] = value
+
 
 def middle_body(
     meta_ref, x_ref, after_ref, sum_ref, back_ref, g_ref, gain_ref, mta_ref, mtb_ref,
-    w0, w1, w2, w3, e0, e1, e2, e3, da_ref, do_ref, even_ref, odd_ref, gain_out, acc,
+    w0, w1, w2, w3, e0, e1, e23, da_ref, do_ref, even_ref, odd_ref, gain_out, acc,
 ):
     step = pl.program_id(0)
     after = after_ref[...]
     delta = (after - x_ref[...].astype(F32) + sum_ref[...]).astype(BF16)
-    give(meta_ref, delta, (e0, e1, e2, e3))
+    give(meta_ref, delta, (e0, e1, e23))
     back, gain_grad = norm_back(back_ref[...], after, gain_ref[...])
     grad_after = g_ref[...].astype(F32) + back
     da_ref[...] = grad_after
@@ -475,7 +497,8 @@
     full = lambda a: pl.BlockSpec(a.shape, lambda i, n=a.ndim: (0,) * n)
     heads = pl.BlockSpec((3, 2 * HD, step), lambda i: (0, 0, i))
     args = (meta, x, after, total, back, g, gain, *mts, *wo)
-    out = [struct((step, width), BF16)] * 4 + [
+    out = [struct((step, width), BF16)] * 2 + [
+        struct((2, step, width), BF16),
         struct((LEN, width), F32),
         struct((12 * HD, LEN), BF16),
         struct((2, 3 * HD, width), BF16),
@@ -490,8 +513,8 @@
         40,
         grid=(LEN // step,),
         in_specs=[SM] + [rows] * 5 + [full(gain), heads, heads] + [full(w) for w in wo],
-        out_specs=[full(o) for o in out[:4]]
-        + [rows, pl.BlockSpec((12 * HD, step), lambda i: (0, i)), full(out[6]), full(out[7]), full(out[8])],
+        out_specs=[full(o) for o in out[:3]]
+        + [rows, pl.BlockSpec((12 * HD, step), lambda i: (0, i)), full(out[5]), full(out[6]), full(out[7])],
         scratch_shapes=[pltpu.VMEM((3, 2, 2 * HD, width), F32)],
     )
 
@@ -510,10 +533,10 @@
     if not last:
         rest[0][...] = total
         return
-    before_ref, x_ref, da_ref, g_ref, gain_ref, e0, e1, e2, e3, gain_out = rest
+    before_ref, x_ref, da_ref, g_ref, gain_ref, e0, e1, e23, gain_out = rest
     total = total + before_ref[...]
     back, gain_grad = norm_back(total, x_ref[...].astype(F32), gain_ref[...])
-    give(meta_ref, (da_ref[...] - g_ref[...].astype(F32) + back).astype(BF16), (e0, e1, e2, e3))
+    give(meta_ref, (da_ref[...] - g_ref[...].astype(F32) + back).astype(BF16), (e0, e1, e23))
 
     @pl.when(step == 0)
     def _():
@@ -534,7 +557,7 @@
         out = [struct((LEN, width), F32)]
         out_specs = [rows]
     else:
-        out = [struct((step, width), BF16)] * 4 + [struct((1, width), F32)]
+        out = [struct((step, width), BF16)] * 2 + [struct((2, step, width), BF16), struct((1, width), F32)]
         out_specs = [full(o) for o in out]
         specs = specs + [rows] * 4 + [full(rest[4])]
         args = args + tuple(rest)
@@ -606,87 +629,130 @@
     )
 
 
-def second_body(meta_ref, kp, rp, kq, rq, keep, send):
-    for which, (k, r) in enumerate(((kp, rp), (kq, rq))):
-        keep[which] = added(k[0], r[0])
-        send[which] = added(k[1], r[1])
-
-
-def second_sums(meta, kp, rp, kq, rq):
-    _, rows, cols = kp.shape
-    block = pl.BlockSpec((2, rows // 2, cols), lambda i: (0, i, 0))
+def second_body(meta_ref, kp, rp, kq, rq, keep, send_p, send_q):
+    step = pl.program_id(0)
+    for which, (k, r, send, bit) in enumerate(((kp, rp, send_p, meta_ref[4]), (kq, rq, send_q, meta_ref[3]))):
+        for slot in range(2):
+            value = added(k[slot, 0], r[slot, 0])
+            put(step == bit, keep, (which, slot), value)
+            put(step == 1 - bit, send, slot, value)
+
+
+def second_sums(meta, *pieces):
+    _, rows, cols = pieces[0].shape
+    half = rows // 2
+    full = lambda n: pl.BlockSpec((2,) * n + (half, cols), lambda i: (0,) * (n + 2))
     return call(
         second_body,
         "second_sums",
+        [struct((2, 2, half, cols), BF16)] + [struct((2, half, cols), BF16)] * 2,
+        (meta, *[p.reshape(2, 2, half, cols) for p in pieces]),
+        20,
+        grid=(2,),
+        in_specs=[SM] + [pl.BlockSpec((2, 1, half, cols), lambda i: (0, i, 0, 0))] * 4,
+        out_specs=[full(2), full(1), full(1)],
+    )
+
+
+def third_body(meta_ref, a, bp, bq, keep, send):
+    which = pl.program_id(0)
+    for part, b in enumerate((bp, bq)):
+
+        @pl.when(which == part)
+        def _():
+            keep[0] = added(a[0, 0], b[0])
+            send[0] = added(a[0, 1], b[1])
+
+
+def third_sums(meta, a, bp, bq):
+    _, _, rows, cols = a.shape
+    whole = pl.BlockSpec((2, rows, cols), lambda i: (0, 0, 0))
+    block = pl.BlockSpec((1, rows, cols), lambda i: (i, 0, 0))
+    return call(
+        third_body,
+        "third_sums",
         [struct((2, rows, cols), BF16)] * 2,
-        (meta, kp, rp, kq, rq),
-        16,
+        (meta, a, bp, bq),
+        12,
         grid=(2,),
-        in_specs=[SM] + [block] * 4,
-        out_specs=[block] * 2,
-    )
-
-
-def third_body(meta_ref, a, b, keep, send_p, send_q):
+        in_specs=[SM, pl.BlockSpec((1, 2, rows, cols), lambda i: (i, 0, 0, 0)), whole, whole],
+        out_specs=[block, block],
+    )
+
+
+def halve_body(bit_ref, a, b, keep, send):
+    bit = bit_ref[0]
     step = pl.program_id(0)
-    two = meta_ref[4]
-    bit = meta_ref[3]
-    value = added(a[0, 0], b[0, 0])
-    put(step == two, keep, 0, value)
-    put(step == 1 - two, send_p, None, value)
-    value = added(a[1, 0], b[1, 0])
-    put(step == bit, keep, 1, value)
-    put(step == 1 - bit, send_q, None, value)
-
-
-def third_sums(meta, a, b):
+    for which in range(2):
+        value = added(a[which, 0], b[which, 0])
+        put(step == bit, keep, which, value)
+        put(step != bit, send, which, value)
+
+
+def halve_sums(bit, a, b):
     _, rows, cols = a.shape
     half = rows // 2
-    views = [v.reshape(2, 2, half, cols) for v in (a, b)]
-    return call(
-        third_body,
-        "third_sums",
-        [struct((2, half, cols), BF16)] + [struct((half, cols), BF16)] * 2,
-        (meta, *views),
+    return call(
+        halve_body,
+        "halve_sums",
+        [struct((2, half, cols), BF16)] * 2,
+        (bit.reshape(1), a.reshape(2, 2, half, cols), b.reshape(2, 2, half, cols)),
         12,
         grid=(2,),
         in_specs=[SM] + [pl.BlockSpec((2, 1, half, cols), lambda i: (0, i, 0, 0))] * 2,
-        out_specs=[pl.BlockSpec((2, half, cols), lambda i: (0, 0, 0))]
-        + [pl.BlockSpec((half, cols), lambda i: (0, 0))] * 2,
-    )
-
-
-def halve_body(bit_ref, a, b0, b1, keep, send):
+        out_specs=[pl.BlockSpec((2, half, cols), lambda i: (0, 0, 0))] * 2,
+    )
+
+
+def plain_body(tie_ref, a, b, out):
+    out[...] = added(a[...], b[...])
+
+
+def plain_sum(tie, a, b):
+    return call(plain_body, "plain_sum", [struct(a.shape, BF16)], (tie, a, b), 12, in_specs=[SM, VM, VM], out_specs=[VM])[0]
+
+
+def split_body(bit_ref, a, b, keep, send):
     bit = bit_ref[0]
     step = pl.program_id(0)
-    for which, b in enumerate((b0, b1)):
-        value = added(a[which, 0], b[0])
-        put(step == bit, keep, which, value)
-        put(step != bit, send, which, value)
-
-
-def halve_sums(bit, a, b0, b1):
-    _, rows, cols = a.shape
+    value = added(a[0], b[0])
+    put(step == bit, keep, None, value)
+    put(step != bit, send, None, value)
+
+
+def split_sums(bit, a, b):
+    rows, cols = a.shape
     half = rows // 2
     return call(
-        halve_body,
-        "halve_sums",
-        [struct((2, half, cols), BF16)] * 2,
-        (bit.reshape(1), a.reshape(2, 2, half, cols), b0.reshape(2, half, cols), b1.reshape(2, half, cols)),
+        split_body,
+        "split_sums",
+        [struct((half, cols), BF16)] * 2,
+        (bit.reshape(1), a.reshape(2, half, cols), b.reshape(2, half, cols)),
         12,
         grid=(2,),
-        in_specs=[SM, pl.BlockSpec((2, 1, half, cols), lambda i: (0, i, 0, 0))]
-        + [pl.BlockSpec((1, half, cols), lambda i: (i, 0, 0))] * 2,
-        out_specs=[pl.BlockSpec((2, half, cols), lambda i: (0, 0, 0))] * 2,
-    )
-
-
-def plain_body(tie_ref, a, b, out):
-    out[...] = added(a[...], b[...])
-
-
-def plain_sum(tie, a, b):
-    return call(plain_body, "plain_sum", [struct(a.shape, BF16)], (tie, a, b), 12, in_specs=[SM, VM, VM], out_specs=[VM])[0]
+        in_specs=[SM] + [pl.BlockSpec((1, half, cols), lambda i: (i, 0, 0))] * 2,
+        out_specs=[pl.BlockSpec((half, cols), lambda i: (0, 0))] * 2,
+    )
+
+
+def merge_body(bit_ref, a, b, out):
+    bit = bit_ref[0]
+    out[bit] = a[...]
+    out[1 - bit] = b[...]
+
+
+def merge(bit, a, b):
+    rows, cols = a.shape
+    made = call(
+        merge_body,
+        "merge",
+        [struct((2, rows, cols), BF16)],
+        (bit.reshape(1), a, b),
+        12,
+        in_specs=[SM, VM, VM],
+        out_specs=[VM],
+    )[0]
+    return made.reshape(2 * rows, cols)
 
 
 def pair_body(bit_ref, a, b, out):
@@ -801,35 +867,79 @@
     return call(spread_body, "spread_sum", [struct(pieces.shape, BF16)], (tie, pieces), 16, in_specs=[SM, VM], out_specs=[VM])[0]
 
 
+GAIN_ROWS = 8
+
+
+def spread_gain_body(tie_ref, in_ref, gain_ref, out_ref):
+    count, rows, width = in_ref.shape
+    total = in_ref[0].astype(F32)
+    for which in range(1, count):
+        total = total + in_ref[which].astype(F32)
+    total = total.astype(BF16)
+    gains = gain_ref[...]
+    high = gains.astype(BF16)
+    low = (gains - high.astype(F32)).astype(BF16)
+    head = jnp.concatenate([high, low, jnp.zeros((GAIN_ROWS - 4, width), BF16)], axis=0)
+    for which in range(count):
+        out_ref[which, :GAIN_ROWS, :] = head
+        out_ref[which, GAIN_ROWS:, :] = total
+
+
+def spread_gain_sum(tie, pieces, gains):
+    count, rows, width = pieces.shape
+    return call(
+        spread_gain_body,
+        "spread_sum",
+        [struct((count, rows + GAIN_ROWS, width), BF16)],
+        (tie, pieces, gains),
+        16,
+        in_specs=[SM, VM, VM],
+        out_specs=[VM],
+    )[0]
+
+
 def exchange(value):
     return lax.all_to_all(value, "dp", 0, 0)
 
 
-def attn_out_body(tie_ref, early_ref, late_ref, qkv_ref, wo_ref):
-    wo_ref[...] = early_ref[: 3 * HD, :].astype(F32)
+def attn_out_body(meta_ref, own_ref, other_ref, late_ref, qkv_ref, wo_ref, gain_ref, hold, hold_early):
+    bit = meta_ref[3]
+    hold_early[bit] = own_ref[...]
+    hold_early[1 - bit] = other_ref[...]
+    early = hold_early[...].reshape(9 * HD, hold.shape[1])
+    wo_ref[...] = early[: 3 * HD, :].astype(F32)
+    count = late_ref.shape[0]
+    rows = late_ref.shape[1] - GAIN_ROWS
+    gains = None
+    for which in range(count):
+        head = late_ref[which, :GAIN_ROWS, :].astype(F32)
+        gains = head if gains is None else gains + head
+        hold[which * rows : (which + 1) * rows, :] = late_ref[which, GAIN_ROWS:, :].astype(F32)
+    gain_ref[...] = gains[0:2] + gains[2:4]
     for part in range(3):
         at = part * HD
-        parts = [early_ref[3 * HD + at : 3 * HD + at + HD, :], early_ref[6 * HD + at : 6 * HD + at + HD, :]]
-        parts.append(late_ref[at : at + HD, :])
-        qkv_ref[part] = jnp.concatenate(parts, axis=0).astype(F32).T
-
-
-def attn_out(tie, early, late):
-    width = early.shape[1]
+        parts = [early[3 * HD + at : 3 * HD + at + HD, :], early[6 * HD + at : 6 * HD + at + HD, :]]
+        parts = [p.astype(F32) for p in parts] + [hold[at : at + HD, :]]
+        qkv_ref[part] = jnp.concatenate(parts, axis=0).T
+
+
+def attn_out(meta, own, other, late):
+    width = own.shape[1]
     return call(
         attn_out_body,
         "attn_out",
-        [struct((3, width, 3 * HD), F32), struct((3 * HD, width), F32)],
-        (tie, early, late),
+        [struct((3, width, 3 * HD), F32), struct((3 * HD, width), F32), struct((2, width), F32)],
+        (meta, own, other, late),
         20,
-        in_specs=[SM, VM, VM],
-        out_specs=[VM, VM],
-    )
-
-
-def add_home_body(meta_ref, in_ref, p0, p1, p2, p3, out_ref):
+        in_specs=[SM, VM, VM, VM],
+        out_specs=[VM, VM, VM],
+        scratch_shapes=[pltpu.VMEM((3 * HD, width), F32), pltpu.VMEM((2,) + own.shape, BF16)],
+    )
+
+
+def add_home_body(meta_ref, in_ref, p0, p1, p23, p3, out_ref):
     slot = pl.program_id(0) ^ meta_ref[2]
-    for which, piece in enumerate((p0, p1, p2, p3)):
+    for which, piece in enumerate((p0, p1, p23.at[0], p3)):
 
         @pl.when(slot == which)
         def _():
@@ -839,7 +949,7 @@
 def add_home(meta, base, pieces):
     count, rows, width = base.shape
     block = pl.BlockSpec((1, rows, width), lambda i: (i, 0, 0))
-    full = pl.BlockSpec((rows, width), lambda i: (0, 0))
+    full = lambda a: pl.BlockSpec(a.shape, lambda i, n=a.ndim: (0,) * n)
     return call(
         add_home_body,
         "add_home",
@@ -847,7 +957,7 @@
         (meta, base, *pieces),
         16,
         grid=(count,),
-        in_specs=[SM, block] + [full] * 4,
+        in_specs=[SM, block] + [full(p) for p in pieces],
         out_specs=[block],
     )[0]
 
@@ -877,6 +987,10 @@
     def around(pieces):
         return [pieces[0]] + [tensor(pieces[k], mask=k) for k in range(1, 4)]
 
+    def homeward(own, core, far):
+        received = tensor(far, mask=2)
+        return own, tensor(core, mask=1), received, tensor(received[1], mask=1)
+
     def far(half):
         direct = tensor(half, mask=2)
         other = dp(direct, mask=1)
@@ -886,7 +1000,7 @@
     xs = around(x_mine)
     wa0 = jnp.concatenate([jnp.swapaxes(w_qkv, 1, 2), w_out[None]]).astype(BF16)
     wa1 = tensor(wa0, mask=1)
-    wa_far = far(lax.dynamic_slice_in_dim(wa0, 2 * bit, 2, 0))
+    wa_far = far(tie(lax.dynamic_slice_in_dim(wa0, 2 * bit, 2, 0), xs[1]))
     wm0 = jnp.concatenate([w_gate_up, w_down.T[None]]).astype(BF16)
     wm1 = tensor(wm0, mask=1)
     wm_far = far(lax.dynamic_slice_in_dim(wm0.reshape(3 * width, units), 3 * width // 2 * bit, 3 * width // 2, 0))
@@ -907,66 +1021,72 @@
     after, n2, n2t, g, gt = run(after_attention, meta, x, ma, mb, wa, two, gs)
     acc_out, acc_back, dw1, dw0 = run(mlp, meta, n2, n2t, g, gt, ((wm1,), (wm0,)))
     in1 = tensor(dw1, mask=1)
-    acc_out, acc_back, dw3 = run(mlp, meta, n2, n2t, g, gt, (wm_far[2:],), (acc_out, acc_back))
+    acc_out, acc_back, dw3, dw2 = run(mlp, meta, n2, n2t, g, gt, (wm_far[2:], wm_far[:2]), (acc_out, acc_back))
     in3 = tensor(dw3, mask=1)
-    acc_out, acc_back, dw2 = run(mlp, meta, n2, n2t, g, gt, (wm_far[:2],), (acc_out, acc_back))
+    middle_out = run(middle, meta, x, after, acc_out, acc_back, g, two, (mta, mtb), wa)
+    home = homeward(*middle_out[:3])
+    da, do, even_o, odd_o, gain_two = middle_out[3:]
+    in_o = tensor(odd_o, mask=1)
     keep_p, send_p, keep_q, send_q = run(start_sums, meta, dw0, in1, dw2, in3)
     recv_p = dp(send_p, mask=1)
     recv_q = dp(send_q, mask=2)
-    middle_out = run(middle, meta, x, after, acc_out, acc_back, g, two, (mta, mtb), wa)
-    home = around(middle_out[:4])
-    da, do, even_o, odd_o, gain_two = middle_out[4:]
-    in_o = tensor(odd_o, mask=1)
     sets = ((qa, ka, va, mta, la), (qb, kb, vb, mtb, lb))
     back = lambda turn: run(lambda m: attend_back(turn, m, cosine, sine, n1, sets, do), meta)
     dt0, even0, odd0 = back(0)
     in0 = tensor(odd0, mask=1)
-    keep, send = run(second_sums, meta, keep_p, recv_p, keep_q, recv_q)
-    recv = tensor(send, mask=2)
     dt1, even1, odd1 = back(1)
     in1_ = tensor(odd1, mask=1)
-    outputs = run(add_home, meta, inputs, home)
+    keep, send_p, send_q = run(second_sums, tie(meta, home[2]), keep_p, recv_p, keep_q, recv_q)
+    recv_p = dp(send_p, mask=2)
+    recv_q = dp(send_q, mask=1)
     early, early_send = run(core_sums, meta, (even_o, even0, even1), (in_o, in0, in1_))
     early_recv = tensor(early_send, mask=2)
-    keep, send_p, send_q = run(third_sums, meta, keep, recv)
-    recv_p = dp(send_p, mask=2)
-    recv_q = dp(send_q, mask=1)
-    (before,) = run(lambda m: token_grad(m, (0, 1), (dt0, dt1), wa), meta)
-    pieces = (recv_p, recv_q)
-    for shift in range(2, len(bits)):
-        keep, send = run(halve_sums, bits[shift], keep, *pieces)
-        pieces = dp(send, mask=1 << shift)
     dt2, even2, odd2 = back(2)
     in2 = tensor(odd2, mask=1)
+    keep, send = run(third_sums, tie(meta, home[3]), keep, recv_p, recv_q)
+    pieces = tensor(send, mask=2)
+    late, late_send = run(core_sums, meta, (even2,), (in2,))
+    late_recv = tensor(late_send, mask=2)
+    (before,) = run(lambda m: token_grad(m, (0, 1), (dt0, dt1), wa), meta)
+    early, early_send = run(split_sums, bits[0], early, early_recv)
+    early_recv = dp(early_send, mask=1)
+    *grads, gain_one = run(lambda m: token_grad(m, (2,), (dt2,), wa, (before, x, da, g, one)), meta)
+    for shift in range(2, len(bits)):
+        keep, send = run(halve_sums, bits[shift], keep, pieces)
+        pieces = dp(send, mask=1 << shift)
+    late = run(plain_sum, meta, late, late_recv)
+    late = exchange(late.reshape(n_dp, -1, width))
+    grads = homeward(grads[0], grads[1], tie(grads[2], late_recv))
+    early, early_send = run(split_sums, bits[1], early, early_recv)
+    early_recv = dp(early_send, mask=2)
+    outputs = run(add_home, meta, inputs, home)
+    gains = jnp.concatenate([gain_one, gain_two])
+    gains = gains + tensor(gains, mask=1)
+    gains = gains + tensor(gains, mask=2)
+    for shift in range(2, len(bits)):
+        early, early_send = run(split_sums, bits[shift], early, early_recv)
+        early_recv = dp(early_send, mask=1 << shift)
     piece = run(plain_sum, meta, keep, pieces)
     other = dp(piece, mask=1 << (len(bits) - 1))
     early = run(plain_sum, meta, early, early_recv)
-    early = exchange(early.reshape(n_dp, -1, width))
-    late, late_send = run(core_sums, meta, (even2,), (in2,))
-    late_recv = tensor(late_send, mask=2)
-    *grads, gain_one = run(lambda m: token_grad(m, (2,), (dt2,), wa, (before, x, da, g, one)), meta)
-    grads = around(grads)
-    late = run(plain_sum, meta, late, late_recv)
-    late = exchange(late.reshape(n_dp, -1, width))
+    early_recv = dp(early, mask=1 << (len(bits) - 1))
+    late = exchange(run(spread_gain_sum, meta, late, gains))
     for shift in reversed(range(2, len(bits))):
         piece = run(pair_join, bits[shift], piece, other)
         if shift > 2:
             other = dp(piece, mask=1 << (shift - 1))
     recv_p = dp(piece[0], mask=2)
     recv_q = dp(piece[1], mask=1)
-    early = exchange(run(spread_sum, meta, early))
-    p, q = run(cross_join, meta, piece, recv_p, recv_q)
-    recv_p = dp(p, mask=1)
-    recv_q = dp(q, mask=2)
-    gains = jnp.concatenate([gain_one, gain_two])
-    gains = gains + tensor(gains, mask=1)
-    gains = gains + tensor(gains, mask=2)
-    for shift in range(len(bits)):
-        gains = gains + dp(gains, mask=1 << shift)
-    late = exchange(run(spread_sum, meta, late))
-    input_grad = run(add_home, meta, out_grad, grads)
+    for shift in reversed(range(1, len(bits))):
+        early = run(merge, bits[shift], early, early_recv)
+        early_recv = dp(early, mask=1 << (shift - 1))
+        if shift == 2:
+            input_grad = run(add_home, meta, out_grad, grads)
+            p, q = run(cross_join, meta, piece, recv_p, recv_q)
+            recv_p = dp(p, mask=1)
+            recv_q = dp(q, mask=2)
+    grad_qkv, grad_out, gains = run(attn_out, meta, early, early_recv, late)
     grad_pair, grad_down = run(mlp_out, meta, p, recv_p, q, recv_q, width)
-    grad_qkv, grad_out = run(attn_out, meta, early.reshape(9 * HD, width), late.reshape(3 * HD, width))
     return (
         outputs,
         input_grad,

time: 476 us -> 365 us (0.77)
  waiting for transfers between devices: 160 us -> 76.2 us
  local copies, waits for them, and re-layouts: 62 us -> 45.5 us
  blocking collectives: 14.5 us -> 0 us
  starting transfers between devices: 56.3 us -> 47.9 us
  Pallas kernels: 171 us -> 178 us
  other arithmetic: 6.33 us -> 11.3 us
    ppermute x46 -> x49, waiting for transfers between devices: 160 us -> 76.2 us  [swap(): return lax.ppermute(value, axis, [(i, i ^ mask) for i in range(size)])]
    unnamed x230 -> x166, local copies, waits for them, and re-layouts: 57.3 us -> 37.7 us
    all_to_all x1 -> x0, blocking collectives: 14.5 us -> none  [exchange(): return lax.all_to_all(value, 'dp', 0, 0)]
    pallas_call x31 -> x34, Pallas kernels: 171 us -> 178 us  [call(): pl.pallas_call(body, name=name, out_shape=out_shape, compiler_params=pltp...]
    all_to_all x3 -> x2, starting transfers between devices: 12.1 us -> 7.85 us  [exchange(): return lax.all_to_all(value, 'dp', 0, 0)]
    ppermute x46 -> x49, starting transfers between devices: 44.2 us -> 40 us  [swap(): return lax.ppermute(value, axis, [(i, i ^ mask) for i in range(size)])]
  transfers between devices with their start and end apart: 49 -> 51, of which waited for: 20 -> 10; matrix products, arithmetic and copies ran while one was open for 2% -> 5% of each run, Pallas kernels for 34% -> 48%
where the time goes in v3:
time: 365 us; the launch traced here: 361 us
  Pallas kernels  178 us (49%)
  waiting for transfers between devices  76.2 us (21%)
  starting transfers between devices  47.9 us (13%)
  local copies, waits for them, and re-layouts  45.5 us (12%)
  other arithmetic  11.3 us (3%)
    pallas_call x34, Pallas kernels, call(): pl.pallas_call(body, name=name, out_shape=out_shape, compiler_params=pltp...  178 us
    ppermute x49, waiting for transfers between devices, swap(): return lax.ppermute(value, axis, [(i, i ^ mask) for i in range(size)])  76.2 us
    ppermute x49, starting transfers between devices, swap(): return lax.ppermute(value, axis, [(i, i ^ mask) for i in range(size)])  40 us
    unnamed x166, local copies, waits for them, and re-layouts  37.7 us
    all_to_all x2, starting transfers between devices, exchange(): return lax.all_to_all(value, 'dp', 0, 0)  7.85 us
  transfers between devices with their start and end apart: 51, of which 10 were waited for; matrix products, arithmetic and copies ran while one was open for 5% of the time, Pallas kernels for 48%

profile of v3, /device:TPU:0, one launch (start us, length us, event | category | flops | bytes accessed | tf_op | source)
XLA Modules:
  0.0 360.8 jit_solution(10502900991580983940)
XLA Ops:
  24.2 18.3 %collective-permute-done.4.d2 = bf16[2,192,768]{2,1,0:T(8,128)(2,1)S(1)} collective-permute-done((bf16[2,192,768]{2,1,0:T(8,128)(2,1)S(1)}, bf16[2,192,768]{2,1,0:T(8,128)(2,1)S(1)}, u32[]{:S(2)}, u32[]{:S(2)}) %collective-permute-start.4) | collective-permute-done | bytes 589856 | tf_op jit(solution)/shard_map/ppermute | solution.py:584
  46.6 4.8 %project_first.1 = (bf16[1024,768]{1,0:T(8,128)(2,1)S(1)}, bf16[1024,768]{1,0:T(8,128)(2,1)S(1)}, bf16[3,128,1024]{2,1,0:T(8,128)(2,1)S(1)}, bf16[3,128,1024]{2,1,0:T(8,128)(2,1)S(1)}, bf16[3,128,1024]{2,1,0:T(8,128)(2,1)S(1)}) custom-call(s32[5]{0:T(128)S(1)} %pad_add_fusion.meta_ref.starts_ref.tie_ref, bf16[256,768]{1,0:T(8,128)(2,1)S(1)} %get-tuple-element.257.p0, ...), custom_call_target="tpu_custom_call" | custom-call | flops 5000000000 | tf_op jit(solution)/shard_map/project_first/pallas_call | solution.py:45
  51.4 6.2 %collective-permute-done.5.r2 = bf16[2,192,768]{2,1,0:T(8,128)(2,1)S(1)} collective-permute-done((bf16[2,192,768]{2,1,0:T(8,128)(2,1)S(1)}, bf16[2,192,768]{2,1,0:T(8,128)(2,1)S(1)}, u32[]{:S(2)}, u32[]{:S(2)}) %collective-permute-start.5) | collective-permute-done | bytes 589856 | tf_op jit(solution)/shard_map/ppermute | solution.py:584
  57.6 10.3 %attend.2 = (bf16[3,128,1024]{2,1,0:T(8,128)(2,1)S(1)}, bf16[1024,384]{1,0:T(8,128)(2,1)S(1)}, f32[3,2,1024]{2,1,0:T(2,128)S(1)}) custom-call(s32[5]{0:T(128)S(1)} %pad_add_fusion.meta_ref.starts_ref.tie_ref, bf16[3,128,1024]{2,1,0:T(8,128)(2,1)S(1)} %get-tuple-element.127.q_ref.refs_0_, bf16[3,128,1024]{2,1,0:T(8,128)(2,1)S(1)} %get-tuple-element.128.k_ref.refs_1_, ...), custom_call_target="tpu_custom_call" | custom-call | flops 10000000000 | tf_op jit(solution)/shard_map/attend/pallas_call | solution.py:45
  68.0 5.3 %collective-permute-done.12.refs_2_ = bf16[1152,512]{1,0:T(8,128)(2,1)S(1)} collective-permute-done((bf16[1152,512]{1,0:T(8,128)(2,1)S(1)}, bf16[1152,512]{1,0:T(8,128)(2,1)S(1)}, u32[]{:S(2)}, u32[]{:S(2)}) %collective-permute-start.12) | collective-permute-done | bytes 1179680 | tf_op jit(solution)/shard_map/ppermute | solution.py:584
  79.2 10.3 %attend.3 = (bf16[3,128,1024]{2,1,0:T(8,128)(2,1)S(1)}, bf16[1024,384]{1,0:T(8,128)(2,1)S(1)}, f32[3,2,1024]{2,1,0:T(2,128)S(1)}) custom-call(s32[5]{0:T(128)S(1)} %pad_add_fusion.meta_ref.starts_ref.tie_ref, bf16[3,128,1024]{2,1,0:T(8,128)(2,1)S(1)} %get-tuple-element.134.q_ref.refs_5_, bf16[3,128,1024]{2,1,0:T(8,128)(2,1)S(1)} %get-tuple-element.136.k_ref.refs_6_, ...), custom_call_target="tpu_custom_call" | custom-call | flops 10000000000 | tf_op jit(solution)/shard_map/attend/pallas_call | solution.py:45
  90.6 4.7 %after_attention.1 = (f32[1024,768]{1,0:T(8,128)S(1)}, bf16[1024,768]{1,0:T(8,128)(2,1)S(1)}, bf16[768,1024]{1,0:T(8,128)(2,1)S(1)}, bf16[1024,768]{1,0:T(8,128)(2,1)S(1)}, bf16[768,1024]{1,0:T(8,128)(2,1)S(1)}) custom-call(s32[5]{0:T(128)S(1)} %pad_add_fusion.meta_ref.starts_ref.tie_ref, bf16[1024,768]{1,0:T(8,128)(2,1)S(1)} %get-tuple-element.125.x_ref.refs_6_, ...), custom_call_target="tpu_custom_call" | custom-call | flops 5000000000 | tf_op jit(solution)/shard_map/after_attention/pallas_call | solution.py:45
  99.4 3.9 %collective-permute-done.14.refs_3_ = bf16[1152,512]{1,0:T(8,128)(2,1)} collective-permute-done((bf16[1152,512]{1,0:T(8,128)(2,1)S(1)}, bf16[1152,512]{1,0:T(8,128)(2,1)}, u32[]{:S(2)}, u32[]{:S(2)}) %collective-permute-start.14) | collective-permute-done | bytes 1179680 | tf_op jit(solution)/shard_map/ppermute | solution.py:584
  103.3 22.0 %mlp.2 = (f32[1024,768]{1,0:T(8,128)}, f32[1024,768]{1,0:T(8,128)}, bf16[3,768,512]{2,1,0:T(8,128)(2,1)}, bf16[3,768,512]{2,1,0:T(8,128)(2,1)}) custom-call(s32[5]{0:T(128)S(1)} %pad_add_fusion.meta_ref.starts_ref.tie_ref, bf16[1024,768]{1,0:T(8,128)(2,1)S(1)} %get-tuple-element.146.n2_ref, bf16[768,1024]{1,0:T(8,128)(2,1)S(1)} %get-tuple-element.147.n2t_ref, ...), custom_call_target="tpu_custom_call" | custom-call | flops 15000000512 | tf_op jit(solution)/shard_map/mlp/pallas_call | solution.py:45
  125.8 23.4 %mlp.3 = (f32[1024,768]{1,0:T(8,128)}, f32[1024,768]{1,0:T(8,128)}, bf16[3,768,512]{2,1,0:T(8,128)(2,1)}, bf16[3,768,512]{2,1,0:T(8,128)(2,1)}) custom-call(s32[5]{0:T(128)S(1)} %pad_add_fusion.meta_ref.starts_ref.tie_ref, bf16[1024,768]{1,0:T(8,128)(2,1)} %copy-done.75, ...), custom_call_target="tpu_custom_call", output_to_operand_aliasing={{0}: (9, {}), {1}: (10, {})} | custom-call | flops 15000000512 | tf_op jit(solution)/shard_map/mlp/pallas_call | solution.py:45
  153.3 10.0 %middle.1 = (bf16[256,768]{1,0:T(8,128)(2,1)S(1)}, bf16[256,768]{1,0:T(8,128)(2,1)}, bf16[2,256,768]{2,1,0:T(8,128)(2,1)}, f32[1024,768]{1,0:T(8,128)}, bf16[768...) custom-call(s32[5]{0:T(128)S(1)} %pad_add_fusion.meta_ref.starts_ref, ...), custom_call_target="tpu_custom_call" | custom-call | flops 10000000000 | tf_op jit(solution)/shard_map/middle/pallas_call | solution.py:45
  165.5 6.3 %start_sums.1 = (bf16[2,576,512]{2,1,0:T(8,128)(2,1)S(1)}, bf16[2,576,512]{2,1,0:T(8,128)(2,1)}, bf16[2,576,512]{2,1,0:T(8,128)(2,1)S(1)}, bf16[2,576,512]{2,1,0:T(8,128)(2,1)}) custom-call(s32[5]{0:T(128)S(1)} %pad_add_fusion.meta_ref.starts_ref.tie_ref, bf16[4,576,512]{2,1,0:T(8,128)(2,1)S(1)} %bitcast.64, bf16[4,576,512]{2,1,0:T(8,128)(2,1)S(1)} %bitcast.65, ...), custom_call_target="tpu_custom_call" | custom-call | flops 1000000000 | tf_op jit(solution)/shard_map/start_sums/pallas_call | solution.py:45
  178.6 11.9 %attend_back.3 = (bf16[3,256,1024]{2,1,0:T(8,128)(2,1)S(1)}, bf16[2,192,768]{2,1,0:T(8,128)(2,1)S(1)}, bf16[2,192,768]{2,1,0:T(8,128)(2,1)}) custom-call(s32[5]{0:T(128)S(1)} %pad_add_fusion.meta_ref.starts_ref.tie_ref, f32[32,1024]{1,0:T(8,128)S(1)} %get-tuple-element.261.cos_ref, f32[32,1024]{1,0:T(8,128)S(1)} %get-tuple-element.260.sin_ref, ...), custom_call_target="tpu_custom_call" | custom-call | flops 4000000000 | tf_op jit(solution)/shard_map/attend_back/pallas_call | solution.py:45
  191.3 12.1 %attend_back.4 = (bf16[3,256,1024]{2,1,0:T(8,128)(2,1)S(1)}, bf16[2,192,768]{2,1,0:T(8,128)(2,1)S(1)}, bf16[2,192,768]{2,1,0:T(8,128)(2,1)}) custom-call(s32[5]{0:T(128)S(1)} %pad_add_fusion.meta_ref.starts_ref.tie_ref, f32[32,1024]{1,0:T(8,128)S(1)} %get-tuple-element.261.cos_ref, f32[32,1024]{1,0:T(8,128)S(1)} %get-tuple-element.260.sin_ref, ...), custom_call_target="tpu_custom_call" | custom-call | flops 4000000000 | tf_op jit(solution)/shard_map/attend_back/pallas_call | solution.py:45
  213.4 11.1 %attend_back.5 = (bf16[3,256,1024]{2,1,0:T(8,128)(2,1)S(1)}, bf16[2,192,768]{2,1,0:T(8,128)(2,1)S(1)}, bf16[2,192,768]{2,1,0:T(8,128)(2,1)S(1)}) custom-call(s32[5]{0:T(128)S(1)} %pad_add_fusion.meta_ref.starts_ref.tie_ref, f32[32,1024]{1,0:T(8,128)S(1)} %get-tuple-element.261.cos_ref, f32[32,1024]{1,0:T(8,128)S(1)} %get-tuple-element.260.sin_ref, ...), custom_call_target="tpu_custom_call" | custom-call | flops 4000000000 | tf_op jit(solution)/shard_map/attend_back/pallas_call | solution.py:45
  233.1 4.2 %token_grad.2.refs_5_ = f32[1024,768]{1,0:T(8,128)S(1)} custom-call(s32[5]{0:T(128)S(1)} %pad_add_fusion.meta_ref.starts_ref.tie_ref, bf16[3,256,1024]{2,1,0:T(8,128)(2,1)S(1)} %get-tuple-element.170.refs_0_, bf16[3,256,1024]{2,1,0:T(8,128)(2,1)S(1)} %get-tuple-element.172.refs_1_, bf16[4,192,768]{2,1,0:T(8,128)(2,1)S(1)} %pad_maximum_fusion.w0.refs_2_.refs_1_, ...), custom_call_target="tpu_custom_call" | custom-call | flops 1000000000 | tf_op jit(solution)/shard_map/token_grad/pallas_call | solution.py:45
  241.0 5.4 %token_grad.3 = (bf16[256,768]{1,0:T(8,128)(2,1)S(1)}, bf16[256,768]{1,0:T(8,128)(2,1)}, bf16[2,256,768]{2,1,0:T(8,128)(2,1)}, f32[1,768]{1,0:T(1,128)S(1)}) custom-call(s32[5]{0:T(128)S(1)} %pad_add_fusion.meta_ref.starts_ref.tie_ref, bf16[3,256,1024]{2,1,0:T(8,128)(2,1)S(1)} %get-tuple-element.187.refs_0_, ...), custom_call_target="tpu_custom_call" | custom-call | flops 1000000000 | tf_op jit(solution)/shard_map/token_grad/pallas_call | solution.py:45
  247.2 5.1 %collective-permute-done.30.b = bf16[192,768]{1,0:T(8,128)(2,1)S(1)} collective-permute-done((bf16[192,768]{1,0:T(8,128)(2,1)S(1)}, bf16[192,768]{1,0:T(8,128)(2,1)S(1)}, u32[]{:S(2)}, u32[]{:S(2)}) %collective-permute-start.30) | collective-permute-done | bytes 294944 | tf_op jit(solution)/shard_map/ppermute | solution.py:584
  270.1 4.1 %all-to-all-start = ((bf16[8,24,768]{2,1,0:T(8,128)(2,1)}), bf16[8,24,768]{2,1,0:T(8,128)(2,1)}, u32[]{:S(2)}, u32[]{:S(2)}) async-start(bf16[8,24,768]{2,1,0:T(8,128)(2,1)} %bitcast.76), calls=%async_computation | async-start | bytes 589824 | tf_op jit(solution)/shard_map/all_to_all | solution.py:902
  288.9 9.4 %collective-permute-done.35.b = bf16[72,768]{1,0:T(8,128)(2,1)S(1)} collective-permute-done((bf16[72,768]{1,0:T(8,128)(2,1)S(1)}, bf16[72,768]{1,0:T(8,128)(2,1)S(1)}, u32[]{:S(2)}, u32[]{:S(2)}) %collective-permute-start.35) | collective-permute-done | bytes 110624 | tf_op jit(solution)/shard_map/ppermute | solution.py:584
  302.3 4.4 %collective-permute-done.38.b = bf16[2,144,512]{2,1,0:T(8,128)(2,1)S(1)} collective-permute-done((bf16[2,144,512]{2,1,0:T(8,128)(2,1)S(1)}, bf16[2,144,512]{2,1,0:T(8,128)(2,1)S(1)}, u32[]{:S(2)}, u32[]{:S(2)}) %collective-permute-start.38) | collective-permute-done | bytes 294944 | tf_op jit(solution)/shard_map/ppermute | solution.py:584
  314.8 3.8 %all-to-all-start.1 = ((bf16[8,32,768]{2,1,0:T(8,128)(2,1)}), bf16[8,32,768]{2,1,0:T(8,128)(2,1)S(1)}, u32[]{:S(2)}, u32[]{:S(2)}) async-start(bf16[8,32,768]{2,1,0:T(8,128)(2,1)} %copy-done.36), calls=%async_computation.1 | async-start | bytes 786432 | tf_op jit(solution)/shard_map/all_to_all | solution.py:902
  331.2 18.0 %collective-permute-done.46.other_ref = bf16[288,768]{1,0:T(8,128)(2,1)S(1)} collective-permute-done((bf16[288,768]{1,0:T(8,128)(2,1)S(1)}, bf16[288,768]{1,0:T(8,128)(2,1)S(1)}, u32[]{:S(2)}, u32[]{:S(2)}) %collective-permute-start.46) | collective-permute-done | bytes 442400 | tf_op jit(solution)/shard_map/ppermute | solution.py:584
  356.2 4.3 %mlp_out.1 = (f32[1536,512]{1,0:T(8,128)}, f32[512,768]{1,0:T(8,128)}) custom-call(s32[5]{0:T(128)S(1)} %pad_add_fusion.meta_ref.starts_ref.tie_ref, bf16[576,512]{1,0:T(8,128)(2,1)S(1)} %bitcast.72, bf16[576,512]{1,0:T(8,128)(2,1)} %collective-permute-done.47.rp, bf16[576,512]{1,0:T(8,128)(2,1)} %bitcast.48.q, bf16[576,512]{1,0:T(8,128)(2,1)} %collective-permute-done.48.rq), custom_call_target="tpu_custom_call" | custom-call | flops 500000000 | tf_op jit(solution)/shard_map/mlp_out/pallas_call | solution.py:45
  (299 shorter events, 139.7 us)
Async XLA Ops:
  5.5 40.4 %collective-permute-start.3 = (bf16[4,192,768]{2,1,0:T(8,128)(2,1)S(1)}, bf16[4,192,768]{2,1,0:T(8,128)(2,1)S(1)}, u32[]{:S(2)}, u32[]{:S(2)}) collective-permute-start(bf16[4,192,768]{2,1,0:T(8,128)(2,1)S(1)} %pad_maximum_fusion.w0.refs_2_.refs_1_), channel_id=1, source_target_pairs={{0,1},{1,0},{2,3},{3,2},{4,5},{5,4},{6,7},{7,6},{8,9},{9,8},{10,11... | collective-permute-start | bytes 3538952 | tf_op jit(solution)/shard_map/ppermute | solution.py:584
  9.0 35.4 %collective-permute-start.2 = (bf16[256,768]{1,0:T(8,128)(2,1)}, bf16[256,768]{1,0:T(8,128)(2,1)}, u32[]{:S(2)}, u32[]{:S(2)}) collective-permute-start(bf16[256,768]{1,0:T(8,128)(2,1)} %get-tuple-element.254), channel_id=1, source_target_pairs={{0,3},{1,2},{2,1},{3,0},{4,7},{5,6},{6,5},{7,4},{8,11},{9,10},{10,... | collective-permute-start | bytes 1179656 | tf_op jit(solution)/shard_map/ppermute | solution.py:584
  11.6 34.4 %collective-permute-start.1 = (bf16[256,768]{1,0:T(8,128)(2,1)}, bf16[256,768]{1,0:T(8,128)(2,1)}, u32[]{:S(2)}, u32[]{:S(2)}) collective-permute-start(bf16[256,768]{1,0:T(8,128)(2,1)} %get-tuple-element.255), channel_id=1, source_target_pairs={{0,2},{1,3},{2,0},{3,1},{4,6},{5,7},{6,4},{7,5},{8,10},{9,11},{10,... | collective-permute-start | bytes 1179656 | tf_op jit(solution)/shard_map/ppermute | solution.py:584
  18.0 85.2 %collective-permute-start.11 = (bf16[3,768,512]{2,1,0:T(8,128)(2,1)}, bf16[3,768,512]{2,1,0:T(8,128)(2,1)}, u32[]{:S(2)}, u32[]{:S(2)}) collective-permute-start(bf16[3,768,512]{2,1,0:T(8,128)(2,1)} %maximum_convert_fusion.refs_1_), channel_id=1, source_target_pairs={{0,1},{1,0},{2,3},{3,2},{4,5},{5,4},{6,7},{7,6},{8,9},{9,8},{10,11... | collective-permute-start | bytes 7077896 | tf_op jit(solution)/shard_map/ppermute | solution.py:584
  20.1 22.4 %collective-permute-start.4 = (bf16[2,192,768]{2,1,0:T(8,128)(2,1)S(1)}, bf16[2,192,768]{2,1,0:T(8,128)(2,1)S(1)}, u32[]{:S(2)}, u32[]{:S(2)}) collective-permute-start(bf16[2,192,768]{2,1,0:T(8,128)(2,1)S(1)} %fusion), channel_id=1, source_target_pairs={{0,2},{1,3},{2,0},{3,1},{4,6},{5,7},{6,4},{7,5},{8,10},{9,11},{10,... | collective-permute-start | bytes 1769480 | tf_op jit(solution)/shard_map/ppermute | solution.py:584
  44.3 28.9 %collective-permute-start.12 = (bf16[1152,512]{1,0:T(8,128)(2,1)S(1)}, bf16[1152,512]{1,0:T(8,128)(2,1)S(1)}, u32[]{:S(2)}, u32[]{:S(2)}) collective-permute-start(bf16[1152,512]{1,0:T(8,128)(2,1)S(1)} %constant_dynamic-slice_fusion), channel_id=1, source_target_pairs={{0,2},{1,3},{2,0},{3,1},{4,6},{5,7},{6,4},{7,5},{8,10},{9,11},{10,... | collective-permute-start | bytes 3538952 | tf_op jit(solution)/shard_map/ppermute | solution.py:584
  45.9 44.5 %collective-permute-start.10 = (bf16[256,768]{1,0:T(8,128)(2,1)S(1)}, bf16[256,768]{1,0:T(8,128)(2,1)S(1)}, u32[]{:S(2)}, u32[]{:S(2)}) collective-permute-start(bf16[256,768]{1,0:T(8,128)(2,1)S(1)} %get-tuple-element.250), channel_id=1, source_target_pairs={{0,3},{1,2},{2,1},{3,0},{4,7},{5,6},{6,5},{7,4},{8,11},{9,10},{10,... | collective-permute-start | bytes 1179656 | tf_op jit(solution)/shard_map/ppermute | solution.py:584
  45.9 28.8 %collective-permute-start.6 = (bf16[2,192,768]{2,1,0:T(8,128)(2,1)S(1)}, bf16[2,192,768]{2,1,0:T(8,128)(2,1)S(1)}, u32[]{:S(2)}, u32[]{:S(2)}) collective-permute-start(bf16[2,192,768]{2,1,0:T(8,128)(2,1)S(1)} %collective-permute-done.4.d2), channel_id=1, source_target_pairs={{0,1},{1,0},{2,3},{3,2},{4,5},{5,4},{6,7},{7,6},{8,9},{9,8},{10,11... | collective-permute-start | bytes 1769480 | tf_op jit(solution)/shard_map/ppermute | solution.py:584
  74.8 28.5 %collective-permute-start.14 = (bf16[1152,512]{1,0:T(8,128)(2,1)S(1)}, bf16[1152,512]{1,0:T(8,128)(2,1)}, u32[]{:S(2)}, u32[]{:S(2)}) collective-permute-start(bf16[1152,512]{1,0:T(8,128)(2,1)S(1)} %collective-permute-done.12.refs_2_), channel_id=1, source_target_pairs={{0,4},{4,0},{8,12},{12,8},{16,20},{20,16},{24,28},{28,24},{1,5},{5... | collective-permute-start | bytes 3538952 | tf_op jit(solution)/shard_map/ppermute | solution.py:584
  90.4 35.4 %collective-permute-start.13 = (bf16[1152,512]{1,0:T(8,128)(2,1)S(1)}, bf16[1152,512]{1,0:T(8,128)(2,1)S(1)}, u32[]{:S(2)}, u32[]{:S(2)}) collective-permute-start(bf16[1152,512]{1,0:T(8,128)(2,1)S(1)} %collective-permute-done.12.refs_2_), channel_id=1, source_target_pairs={{0,1},{1,0},{2,3},{3,2},{4,5},{5,4},{6,7},{7,6},{8,9},{9,8},{10,11... | collective-permute-start | bytes 3538952 | tf_op jit(solution)/shard_map/ppermute | solution.py:584
  103.3 22.6 %collective-permute-start.15 = (bf16[1152,512]{1,0:T(8,128)(2,1)}, bf16[1152,512]{1,0:T(8,128)(2,1)S(1)}, u32[]{:S(2)}, u32[]{:S(2)}) collective-permute-start(bf16[1152,512]{1,0:T(8,128)(2,1)} %collective-permute-done.14.refs_3_), channel_id=1, source_target_pairs={{0,1},{1,0},{2,3},{3,2},{4,5},{5,4},{6,7},{7,6},{8,9},{9,8},{10,11... | collective-permute-start | bytes 3538952 | tf_op jit(solution)/shard_map/ppermute | solution.py:584
  125.3 40.2 %collective-permute-start.18 = (bf16[3,768,512]{2,1,0:T(8,128)(2,1)}, bf16[3,768,512]{2,1,0:T(8,128)(2,1)S(1)}, u32[]{:S(2)}, u32[]{:S(2)}) collective-permute-start(bf16[3,768,512]{2,1,0:T(8,128)(2,1)} %get-tuple-element.162), channel_id=1, source_target_pairs={{0,1},{1,0},{2,3},{3,2},{4,5},{5,4},{6,7},{7,6},{8,9},{9,8},{10,11... | collective-permute-start | bytes 7077896 | tf_op jit(solution)/shard_map/ppermute | solution.py:584
  164.4 45.0 %collective-permute-start.22 = (bf16[2,192,768]{2,1,0:T(8,128)(2,1)}, bf16[2,192,768]{2,1,0:T(8,128)(2,1)}, u32[]{:S(2)}, u32[]{:S(2)}) collective-permute-start(bf16[2,192,768]{2,1,0:T(8,128)(2,1)} %get-tuple-element.182), channel_id=1, source_target_pairs={{0,1},{1,0},{2,3},{3,2},{4,5},{5,4},{6,7},{7,6},{8,9},{9,8},{10,11... | collective-permute-start | bytes 1769480 | tf_op jit(solution)/shard_map/ppermute | solution.py:584
  164.9 38.5 %collective-permute-start.16 = (bf16[2,256,768]{2,1,0:T(8,128)(2,1)}, bf16[2,256,768]{2,1,0:T(8,128)(2,1)S(1)}, u32[]{:S(2)}, u32[]{:S(2)}) collective-permute-start(bf16[2,256,768]{2,1,0:T(8,128)(2,1)} %get-tuple-element.156), channel_id=1, source_target_pairs={{0,2},{1,3},{2,0},{3,1},{4,6},{5,7},{6,4},{7,5},{8,10},{9,11},{10,... | collective-permute-start | bytes 2359304 | tf_op jit(solution)/shard_map/ppermute | solution.py:584
  171.8 32.1 %collective-permute-start.20 = (bf16[2,576,512]{2,1,0:T(8,128)(2,1)}, bf16[2,576,512]{2,1,0:T(8,128)(2,1)S(1)}, u32[]{:S(2)}, u32[]{:S(2)}) collective-permute-start(bf16[2,576,512]{2,1,0:T(8,128)(2,1)} %get-tuple-element.174), channel_id=1, source_target_pairs={{0,4},{4,0},{8,12},{12,8},{16,20},{20,16},{24,28},{28,24},{1,5},{5... | collective-permute-start | bytes 3538952 | tf_op jit(solution)/shard_map/ppermute | solution.py:584
  172.3 31.7 %collective-permute-start.21 = (bf16[2,576,512]{2,1,0:T(8,128)(2,1)}, bf16[2,576,512]{2,1,0:T(8,128)(2,1)}, u32[]{:S(2)}, u32[]{:S(2)}) collective-permute-start(bf16[2,576,512]{2,1,0:T(8,128)(2,1)} %get-tuple-element.176), channel_id=1, source_target_pairs={{0,8},{4,12},{8,0},{12,4},{16,24},{20,28},{24,16},{28,20},{1,9},{5... | collective-permute-start | bytes 3538952 | tf_op jit(solution)/shard_map/ppermute | solution.py:584
  211.9 25.4 %collective-permute-start.28 = (bf16[576,768]{1,0:T(8,128)(2,1)}, bf16[576,768]{1,0:T(8,128)(2,1)}, u32[]{:S(2)}, u32[]{:S(2)}) collective-permute-start(bf16[576,768]{1,0:T(8,128)(2,1)} %get-tuple-element.198), channel_id=1, source_target_pairs={{0,2},{1,3},{2,0},{3,1},{4,6},{5,7},{6,4},{7,5},{8,10},{9,11},{10,... | collective-permute-start | bytes 2654216 | tf_op jit(solution)/shard_map/ppermute | solution.py:584
  230.3 24.8 %collective-permute-start.29 = (bf16[2,288,512]{2,1,0:T(8,128)(2,1)}, bf16[2,288,512]{2,1,0:T(8,128)(2,1)}, u32[]{:S(2)}, u32[]{:S(2)}) collective-permute-start(bf16[2,288,512]{2,1,0:T(8,128)(2,1)} %get-tuple-element.204), channel_id=1, source_target_pairs={{0,2},{1,3},{2,0},{3,1},{4,6},{5,7},{6,4},{7,5},{8,10},{9,11},{10,... | collective-permute-start | bytes 1769480 | tf_op jit(solution)/shard_map/ppermute | solution.py:584
  253.0 46.4 %collective-permute-start.41 = (bf16[2,256,768]{2,1,0:T(8,128)(2,1)}, bf16[2,256,768]{2,1,0:T(8,128)(2,1)}, u32[]{:S(2)}, u32[]{:S(2)}) collective-permute-start(bf16[2,256,768]{2,1,0:T(8,128)(2,1)} %get-tuple-element.228), channel_id=1, source_target_pairs={{0,2},{1,3},{2,0},{3,1},{4,6},{5,7},{6,4},{7,5},{8,10},{9,11},{10,... | collective-permute-start | bytes 2359304 | tf_op jit(solution)/shard_map/ppermute | solution.py:584
  255.1 63.5 %collective-permute-start.40 = (bf16[256,768]{1,0:T(8,128)(2,1)}, bf16[256,768]{1,0:T(8,128)(2,1)}, u32[]{:S(2)}, u32[]{:S(2)}) collective-permute-start(bf16[256,768]{1,0:T(8,128)(2,1)} %get-tuple-element.226), channel_id=1, source_target_pairs={{0,1},{1,0},{2,3},{3,2},{4,5},{5,4},{6,7},{7,6},{8,9},{9,8},{10,11... | collective-permute-start | bytes 1179656 | tf_op jit(solution)/shard_map/ppermute | solution.py:584
  261.8 23.1 %collective-permute-start.34 = (bf16[2,144,512]{2,1,0:T(8,128)(2,1)}, bf16[2,144,512]{2,1,0:T(8,128)(2,1)}, u32[]{:S(2)}, u32[]{:S(2)}) collective-permute-start(bf16[2,144,512]{2,1,0:T(8,128)(2,1)} %get-tuple-element.217), channel_id=1, source_target_pairs={{0,16},{4,20},{8,24},{12,28},{16,0},{20,4},{24,8},{28,12},{1,17},{... | collective-permute-start | bytes 884744 | tf_op jit(solution)/shard_map/ppermute | solution.py:584
  270.1 31.1 %all-to-all-start = ((bf16[8,24,768]{2,1,0:T(8,128)(2,1)}), bf16[8,24,768]{2,1,0:T(8,128)(2,1)}, u32[]{:S(2)}, u32[]{:S(2)}) async-start(bf16[8,24,768]{2,1,0:T(8,128)(2,1)} %bitcast.76), calls=%async_computation | async-start | bytes 589824 | tf_op jit(solution)/shard_map/all_to_all | solution.py:902
  325.2 31.0 %collective-permute-start.47 = (bf16[576,512]{1,0:T(8,128)(2,1)S(1)}, bf16[576,512]{1,0:T(8,128)(2,1)}, u32[]{:S(2)}, u32[]{:S(2)}) collective-permute-start(bf16[576,512]{1,0:T(8,128)(2,1)S(1)} %bitcast.71), channel_id=1, source_target_pairs={{0,4},{4,0},{8,12},{12,8},{16,20},{20,16},{24,28},{28,24},{1,5},{5... | collective-permute-start | bytes 1769480 | tf_op jit(solution)/shard_map/ppermute | solution.py:584
  327.3 29.0 %collective-permute-start.48 = (bf16[576,512]{1,0:T(8,128)(2,1)}, bf16[576,512]{1,0:T(8,128)(2,1)}, u32[]{:S(2)}, u32[]{:S(2)}) collective-permute-start(bf16[576,512]{1,0:T(8,128)(2,1)} %bitcast.48.q), channel_id=1, source_target_pairs={{0,8},{4,12},{8,0},{12,4},{16,24},{20,28},{24,16},{28,20},{1,9},{5... | collective-permute-start | bytes 1769480 | tf_op jit(solution)/shard_map/ppermute | solution.py:584
  (109 other events, 994.8 us)

commit v4 on v3

--- a/solution.py
+++ b/solution.py
@@ -31,12 +31,12 @@
     "attend": 10,
     "after_attention": 5,
     "mlp": 15,
-    "middle": 10,
-    "attend_back": 4,
-    "token_grad": 1,
+    "middle": 3,
+    "attend_back": 2,
+    "token_grad": 0.5,
     "start_sums": 1,
-    "add_home": 0.2,
-    "mlp_out": 0.5,
+    "add_home": 0.1,
+    "mlp_out": 0.1,
 }
 RATE = 1e9
 
@@ -127,7 +127,7 @@
         "project_first",
         out,
         args,
-        24,
+        10,
         in_specs=[SM] + [VM] * (len(args) - 1),
         out_specs=[VM] * len(out),
     )
@@ -141,7 +141,7 @@
         "project_next",
         out,
         args,
-        24,
+        10,
         in_specs=[SM] + [VM] * (len(args) - 1),
         out_specs=[VM] * len(out),
     )
@@ -202,7 +202,7 @@
         "attend",
         out,
         (starts, q, k, v),
-        24,
+        10,
         grid=(3,),
         in_specs=[pl.BlockSpec(memory_space=pltpu.SMEM), block, block, block],
         out_specs=[
@@ -288,7 +288,7 @@
         "attend_back",
         out,
         args,
-        40,
+        16,
         grid=(1,),
         in_specs=[pl.BlockSpec(memory_space=pltpu.SMEM), full(cosine), full(sine), full(n1)]
         + [head, head, head, head, lse] * 2
@@ -345,7 +345,7 @@
         "after_attention",
         out,
         args,
-        30,
+        12,
         grid=(LEN // step,),
         in_specs=[SM, rows(width), rows(6 * HD), rows(6 * HD)]
         + [full(w) for w in wo]
@@ -425,7 +425,7 @@
         "mlp",
         out,
         args,
-        50,
+        24,
         in_specs=[SM] + [VM] * (len(args) - 1),
         out_specs=[VM] * len(out),
         scratch_shapes=scratch,
@@ -510,7 +510,7 @@
         "middle",
         out,
         args,
-        40,
+        14,
         grid=(LEN // step,),
         in_specs=[SM] + [rows] * 5 + [full(gain), heads, heads] + [full(w) for w in wo],
         out_specs=[full(o) for o in out[:3]]
@@ -566,7 +566,7 @@
         "token_grad",
         out,
         args,
-        30,
+        12,
         grid=(LEN // step,),
         in_specs=specs,
         out_specs=out_specs,
@@ -1059,7 +1059,6 @@
     grads = homeward(grads[0], grads[1], tie(grads[2], late_recv))
     early, early_send = run(split_sums, bits[1], early, early_recv)
     early_recv = dp(early_send, mask=2)
-    outputs = run(add_home, meta, inputs, home)
     gains = jnp.concatenate([gain_one, gain_two])
     gains = gains + tensor(gains, mask=1)
     gains = gains + tensor(gains, mask=2)
@@ -1077,14 +1076,16 @@
             other = dp(piece, mask=1 << (shift - 1))
     recv_p = dp(piece[0], mask=2)
     recv_q = dp(piece[1], mask=1)
-    for shift in reversed(range(1, len(bits))):
+    for shift in reversed(range(2, len(bits))):
         early = run(merge, bits[shift], early, early_recv)
         early_recv = dp(early, mask=1 << (shift - 1))
-        if shift == 2:
-            input_grad = run(add_home, meta, out_grad, grads)
-            p, q = run(cross_join, meta, piece, recv_p, recv_q)
-            recv_p = dp(p, mask=1)
-            recv_q = dp(q, mask=2)
+    early = run(merge, bits[1], early, early_recv)
+    early_recv = dp(early, mask=1)
+    p, q = run(cross_join, meta, piece, recv_p, recv_q)
+    recv_p = dp(p, mask=1)
+    recv_q = dp(q, mask=2)
+    outputs = run(add_home, meta, inputs, home)
+    input_grad = run(add_home, meta, out_grad, grads)
     grad_qkv, grad_out, gains = run(attn_out, meta, early, early_recv, late)
     grad_pair, grad_down = run(mlp_out, meta, p, recv_p, q, recv_q, width)
     return (

time: 365 us -> 342 us (0.937)
  Pallas kernels: 178 us -> 159 us
  local copies, waits for them, and re-layouts: 45.5 us -> 38.5 us
    pallas_call x34, Pallas kernels: 178 us -> 159 us  [call(): pl.pallas_call(body, name=name, out_shape=out_shape, compiler_params=pltp...]
    unnamed x166 -> x102, local copies, waits for them, and re-layouts: 37.7 us -> 31.3 us
  transfers between devices with their start and end apart: 51 -> 51, of which waited for: 10 -> 13; matrix products, arithmetic and copies ran while one was open for 5% -> 5% of each run, Pallas kernels for 48% -> 46%
where the time goes in v4:
time: 342 us; the launch traced here: 338 us
  Pallas kernels  159 us (46%)
  waiting for transfers between devices  78.7 us (23%)
  starting transfers between devices  49.1 us (14%)
  local copies, waits for them, and re-layouts  38.5 us (11%)
  other arithmetic  10.9 us (3%)
    pallas_call x34, Pallas kernels, call(): pl.pallas_call(body, name=name, out_shape=out_shape, compiler_params=pltp...  159 us
    ppermute x49, waiting for transfers between devices, swap(): return lax.ppermute(value, axis, [(i, i ^ mask) for i in range(size)])  78.7 us
    ppermute x49, starting transfers between devices, swap(): return lax.ppermute(value, axis, [(i, i ^ mask) for i in range(size)])  39.8 us
    unnamed x102, local copies, waits for them, and re-layouts  31.3 us
    all_to_all x2, starting transfers between devices, exchange(): return lax.all_to_all(value, 'dp', 0, 0)  9.35 us
  transfers between devices with their start and end apart: 51, of which 13 were waited for; matrix products, arithmetic and copies ran while one was open for 5% of the time, Pallas kernels for 46%

profile of v4, /device:TPU:0, one launch (start us, length us, event | category | flops | bytes accessed | tf_op | source)
XLA Modules:
  0.0 337.5 jit_solution(11784296495404836229)
XLA Ops:
  24.4 18.3 %collective-permute-done.4.d2 = bf16[2,192,768]{2,1,0:T(8,128)(2,1)S(1)} collective-permute-done((bf16[2,192,768]{2,1,0:T(8,128)(2,1)S(1)}, bf16[2,192,768]{2,1,0:T(8,128)(2,1)S(1)}, u32[]{:S(2)}, u32[]{:S(2)}) %collective-permute-start.4) | collective-permute-done | bytes 589856 | tf_op jit(solution)/shard_map/ppermute | solution.py:584
  46.7 4.8 %project_first.1 = (bf16[1024,768]{1,0:T(8,128)(2,1)S(1)}, bf16[1024,768]{1,0:T(8,128)(2,1)S(1)}, bf16[3,128,1024]{2,1,0:T(8,128)(2,1)S(1)}, bf16[3,128,1024]{2,1,0:T(8,128)(2,1)S(1)}, bf16[3,128,1024]{2,1,0:T(8,128)(2,1)S(1)}) custom-call(s32[5]{0:T(128)S(1)} %pad_add_fusion.meta_ref.starts_ref.tie_ref, bf16[256,768]{1,0:T(8,128)(2,1)S(1)} %get-tuple-element.257.p0, ...), custom_call_target="tpu_custom_call" | custom-call | flops 5000000000 | tf_op jit(solution)/shard_map/project_first/pallas_call | solution.py:45
  51.5 6.3 %collective-permute-done.5.r2 = bf16[2,192,768]{2,1,0:T(8,128)(2,1)S(1)} collective-permute-done((bf16[2,192,768]{2,1,0:T(8,128)(2,1)S(1)}, bf16[2,192,768]{2,1,0:T(8,128)(2,1)S(1)}, u32[]{:S(2)}, u32[]{:S(2)}) %collective-permute-start.5) | collective-permute-done | bytes 589856 | tf_op jit(solution)/shard_map/ppermute | solution.py:584
  57.8 10.3 %attend.2 = (bf16[3,128,1024]{2,1,0:T(8,128)(2,1)S(1)}, bf16[1024,384]{1,0:T(8,128)(2,1)S(1)}, f32[3,2,1024]{2,1,0:T(2,128)S(1)}) custom-call(s32[5]{0:T(128)S(1)} %pad_add_fusion.meta_ref.starts_ref.tie_ref, bf16[3,128,1024]{2,1,0:T(8,128)(2,1)S(1)} %get-tuple-element.127.q_ref.refs_0_, bf16[3,128,1024]{2,1,0:T(8,128)(2,1)S(1)} %get-tuple-element.128.k_ref.refs_1_, ...), custom_call_target="tpu_custom_call" | custom-call | flops 10000000000 | tf_op jit(solution)/shard_map/attend/pallas_call | solution.py:45
  68.1 5.3 %collective-permute-done.12.refs_2_ = bf16[1152,512]{1,0:T(8,128)(2,1)S(1)} collective-permute-done((bf16[1152,512]{1,0:T(8,128)(2,1)S(1)}, bf16[1152,512]{1,0:T(8,128)(2,1)S(1)}, u32[]{:S(2)}, u32[]{:S(2)}) %collective-permute-start.12) | collective-permute-done | bytes 1179680 | tf_op jit(solution)/shard_map/ppermute | solution.py:584
  79.3 10.3 %attend.3 = (bf16[3,128,1024]{2,1,0:T(8,128)(2,1)S(1)}, bf16[1024,384]{1,0:T(8,128)(2,1)S(1)}, f32[3,2,1024]{2,1,0:T(2,128)S(1)}) custom-call(s32[5]{0:T(128)S(1)} %pad_add_fusion.meta_ref.starts_ref.tie_ref, bf16[3,128,1024]{2,1,0:T(8,128)(2,1)S(1)} %get-tuple-element.134.q_ref.refs_5_, bf16[3,128,1024]{2,1,0:T(8,128)(2,1)S(1)} %get-tuple-element.136.k_ref.refs_6_, ...), custom_call_target="tpu_custom_call" | custom-call | flops 10000000000 | tf_op jit(solution)/shard_map/attend/pallas_call | solution.py:45
  89.8 4.9 %after_attention.1 = (f32[1024,768]{1,0:T(8,128)S(1)}, bf16[1024,768]{1,0:T(8,128)(2,1)S(1)}, bf16[768,1024]{1,0:T(8,128)(2,1)S(1)}, bf16[1024,768]{1,0:T(8,128)(2,1)S(1)}, bf16[768,1024]{1,0:T(8,128)(2,1)S(1)}) custom-call(s32[5]{0:T(128)S(1)} %pad_add_fusion.meta_ref.starts_ref.tie_ref, bf16[1024,768]{1,0:T(8,128)(2,1)S(1)} %get-tuple-element.125.x_ref.refs_6_, ...), custom_call_target="tpu_custom_call" | custom-call | flops 5000000000 | tf_op jit(solution)/shard_map/after_attention/pallas_call | solution.py:45
  94.7 8.7 %collective-permute-done.14.refs_3_ = bf16[1152,512]{1,0:T(8,128)(2,1)} collective-permute-done((bf16[1152,512]{1,0:T(8,128)(2,1)S(1)}, bf16[1152,512]{1,0:T(8,128)(2,1)}, u32[]{:S(2)}, u32[]{:S(2)}) %collective-permute-start.14) | collective-permute-done | bytes 1179680 | tf_op jit(solution)/shard_map/ppermute | solution.py:584
  103.4 18.5 %mlp.2 = (f32[1024,768]{1,0:T(8,128)S(1)}, f32[1024,768]{1,0:T(8,128)S(1)}, bf16[3,768,512]{2,1,0:T(8,128)(2,1)}, bf16[3,768,512]{2,1,0:T(8,128)(2,1)S(1)}) custom-call(s32[5]{0:T(128)S(1)} %pad_add_fusion.meta_ref.starts_ref.tie_ref, bf16[1024,768]{1,0:T(8,128)(2,1)S(1)} %get-tuple-element.146.n2_ref, bf16[768,1024]{1,0:T(8,128)(2,1)S(1)} %get-tuple-element.147.n2t_ref, ...), custom_call_target="tpu_custom_call" | custom-call | flops 15000000512 | tf_op jit(solution)/shard_map/mlp/pallas_call | solution.py:45
  125.3 18.8 %mlp.3 = (f32[1024,768]{1,0:T(8,128)S(1)}, f32[1024,768]{1,0:T(8,128)S(1)}, bf16[3,768,512]{2,1,0:T(8,128)(2,1)S(1)}, bf16[3,768,512]{2,1,0:T(8,128)(2,1)S(1)}) custom-call(s32[5]{0:T(128)S(1)} %pad_add_fusion.meta_ref.starts_ref.tie_ref, bf16[1024,768]{1,0:T(8,128)(2,1)S(1)} %copy-done.46, ...), custom_call_target="tpu_custom_call", output_to_operand_aliasing={{0}: (9, {}), {1}: (10, {})} | custom-call | flops 15000000512 | tf_op jit(solution)/shard_map/mlp/pallas_call | solution.py:45
  151.1 8.1 %middle.1 = (bf16[256,768]{1,0:T(8,128)(2,1)S(1)}, bf16[256,768]{1,0:T(8,128)(2,1)}, bf16[2,256,768]{2,1,0:T(8,128)(2,1)S(1)}, f32[1024,768]{1,0:T(8,128)S(1)}, ...) custom-call(s32[5]{0:T(128)S(1)} %pad_add_fusion.meta_ref.starts_ref, ...), custom_call_target="tpu_custom_call" | custom-call | flops 3000000000 | tf_op jit(solution)/shard_map/middle/pallas_call | solution.py:45
  159.8 5.0 %start_sums.1 = (bf16[2,576,512]{2,1,0:T(8,128)(2,1)S(1)}, bf16[2,576,512]{2,1,0:T(8,128)(2,1)S(1)}, bf16[2,576,512]{2,1,0:T(8,128)(2,1)S(1)}, bf16[2,576,512]{2,1,0:T(8,128)(2,1)S(1)}) custom-call(s32[5]{0:T(128)S(1)} %pad_add_fusion.meta_ref.starts_ref.tie_ref, bf16[4,576,512]{2,1,0:T(8,128)(2,1)S(1)} %bitcast.64, bf16[4,576,512]{2,1,0:T(8,128)(2,1)} %bitcast.18.b0, ...), custom_call_target="tpu_custom_call" | custom-call | flops 1000000000 | tf_op jit(solution)/shard_map/start_sums/pallas_call | solution.py:45
  166.9 11.1 %attend_back.3 = (bf16[3,256,1024]{2,1,0:T(8,128)(2,1)S(1)}, bf16[2,192,768]{2,1,0:T(8,128)(2,1)S(1)}, bf16[2,192,768]{2,1,0:T(8,128)(2,1)S(1)}) custom-call(s32[5]{0:T(128)S(1)} %pad_add_fusion.meta_ref.starts_ref.tie_ref, f32[32,1024]{1,0:T(8,128)S(1)} %get-tuple-element.261.cos_ref, f32[32,1024]{1,0:T(8,128)S(1)} %get-tuple-element.260.sin_ref, ...), custom_call_target="tpu_custom_call" | custom-call | flops 2000000000 | tf_op jit(solution)/shard_map/attend_back/pallas_call | solution.py:45
  178.5 11.2 %attend_back.4 = (bf16[3,256,1024]{2,1,0:T(8,128)(2,1)S(1)}, bf16[2,192,768]{2,1,0:T(8,128)(2,1)S(1)}, bf16[2,192,768]{2,1,0:T(8,128)(2,1)S(1)}) custom-call(s32[5]{0:T(128)S(1)} %pad_add_fusion.meta_ref.starts_ref.tie_ref, f32[32,1024]{1,0:T(8,128)S(1)} %get-tuple-element.261.cos_ref, f32[32,1024]{1,0:T(8,128)S(1)} %get-tuple-element.260.sin_ref, ...), custom_call_target="tpu_custom_call" | custom-call | flops 2000000000 | tf_op jit(solution)/shard_map/attend_back/pallas_call | solution.py:45
  200.3 11.1 %attend_back.5 = (bf16[3,256,1024]{2,1,0:T(8,128)(2,1)S(1)}, bf16[2,192,768]{2,1,0:T(8,128)(2,1)S(1)}, bf16[2,192,768]{2,1,0:T(8,128)(2,1)S(1)}) custom-call(s32[5]{0:T(128)S(1)} %pad_add_fusion.meta_ref.starts_ref.tie_ref, f32[32,1024]{1,0:T(8,128)S(1)} %get-tuple-element.261.cos_ref, f32[32,1024]{1,0:T(8,128)S(1)} %get-tuple-element.260.sin_ref, ...), custom_call_target="tpu_custom_call" | custom-call | flops 2000000000 | tf_op jit(solution)/shard_map/attend_back/pallas_call | solution.py:45
  218.6 4.2 %token_grad.2.refs_5_ = f32[1024,768]{1,0:T(8,128)S(1)} custom-call(s32[5]{0:T(128)S(1)} %pad_add_fusion.meta_ref.starts_ref.tie_ref, bf16[3,256,1024]{2,1,0:T(8,128)(2,1)S(1)} %get-tuple-element.170.refs_0_, bf16[3,256,1024]{2,1,0:T(8,128)(2,1)S(1)} %get-tuple-element.172.refs_1_, bf16[4,192,768]{2,1,0:T(8,128)(2,1)S(1)} %pad_maximum_fusion.w0.refs_2_.refs_1_, ...), custom_call_target="tpu_custom_call" | custom-call | flops 500000000 | tf_op jit(solution)/shard_map/token_grad/pallas_call | solution.py:45
  238.1 5.2 %token_grad.3 = (bf16[256,768]{1,0:T(8,128)(2,1)S(1)}, bf16[256,768]{1,0:T(8,128)(2,1)S(1)}, bf16[2,256,768]{2,1,0:T(8,128)(2,1)}, f32[1,768]{1,0:T(1,128)S(1)}) custom-call(s32[5]{0:T(128)S(1)} %pad_add_fusion.meta_ref.starts_ref.tie_ref, bf16[3,256,1024]{2,1,0:T(8,128)(2,1)S(1)} %copy-done.28, bf16[4,192,768]{2,1,0:T(8,128)(2,1)S(1)} %pad_maximum_fusion.w0.refs_2_.refs_1_, ...), custom_call_target="tpu_custom_call" | custom-call | flops 500000000 | tf_op jit(solution)/shard_map/token_grad/pallas_call | solution.py:45
  251.7 3.8 %all-to-all-start = ((bf16[8,24,768]{2,1,0:T(8,128)(2,1)}), bf16[8,24,768]{2,1,0:T(8,128)(2,1)S(1)}, u32[]{:S(2)}, u32[]{:S(2)}) async-start(bf16[8,24,768]{2,1,0:T(8,128)(2,1)} %bitcast.37), calls=%async_computation | async-start | bytes 589824 | tf_op jit(solution)/shard_map/all_to_all | solution.py:902
  255.5 12.1 %collective-permute-done.32 = bf16[144,768]{1,0:T(8,128)(2,1)S(1)} collective-permute-done((bf16[144,768]{1,0:T(8,128)(2,1)S(1)}, bf16[144,768]{1,0:T(8,128)(2,1)S(1)}, u32[]{:S(2)}, u32[]{:S(2)}) %collective-permute-start.32) | collective-permute-done | bytes 221216 | tf_op jit(solution)/shard_map/ppermute | solution.py:584
  273.5 11.1 %collective-permute-done.34.b = bf16[72,768]{1,0:T(8,128)(2,1)S(1)} collective-permute-done((bf16[72,768]{1,0:T(8,128)(2,1)S(1)}, bf16[72,768]{1,0:T(8,128)(2,1)S(1)}, u32[]{:S(2)}, u32[]{:S(2)}) %collective-permute-start.34) | collective-permute-done | bytes 110624 | tf_op jit(solution)/shard_map/ppermute | solution.py:584
  293.3 5.5 %all-to-all-start.1 = ((bf16[8,32,768]{2,1,0:T(8,128)(2,1)}), bf16[8,32,768]{2,1,0:T(8,128)(2,1)S(1)}, u32[]{:S(2)}, u32[]{:S(2)}) async-start(bf16[8,32,768]{2,1,0:T(8,128)(2,1)} %copy-done.37), calls=%async_computation.1 | async-start | bytes 786432 | tf_op jit(solution)/shard_map/all_to_all | solution.py:902
  298.9 4.6 %collective-permute-done.39.b = bf16[144,768]{1,0:T(8,128)(2,1)} collective-permute-done((bf16[144,768]{1,0:T(8,128)(2,1)}, bf16[144,768]{1,0:T(8,128)(2,1)}, u32[]{:S(2)}, u32[]{:S(2)}) %collective-permute-start.39) | collective-permute-done | bytes 221216 | tf_op jit(solution)/shard_map/ppermute | solution.py:584
  327.4 5.4 %collective-permute-done.47.rp = bf16[576,512]{1,0:T(8,128)(2,1)} collective-permute-done((bf16[576,512]{1,0:T(8,128)(2,1)}, bf16[576,512]{1,0:T(8,128)(2,1)}, u32[]{:S(2)}, u32[]{:S(2)}) %collective-permute-start.47) | collective-permute-done | bytes 589856 | tf_op jit(solution)/shard_map/ppermute | solution.py:584
  332.8 4.5 %mlp_out.1 = (f32[1536,512]{1,0:T(8,128)}, f32[512,768]{1,0:T(8,128)}) custom-call(s32[5]{0:T(128)S(1)} %pad_add_fusion.meta_ref.starts_ref.tie_ref, bf16[576,512]{1,0:T(8,128)(2,1)} %bitcast.46.p, bf16[576,512]{1,0:T(8,128)(2,1)} %collective-permute-done.47.rp, bf16[576,512]{1,0:T(8,128)(2,1)} %bitcast.48.q, bf16[576,512]{1,0:T(8,128)(2,1)} %collective-permute-done.48.rq), custom_call_target="tpu_custom_call" | custom-call | flops 100000000 | tf_op jit(solution)/shard_map/mlp_out/pallas_call | solution.py:45
  (235 shorter events, 126.9 us)
Async XLA Ops:
  5.6 40.4 %collective-permute-start.3 = (bf16[4,192,768]{2,1,0:T(8,128)(2,1)S(1)}, bf16[4,192,768]{2,1,0:T(8,128)(2,1)S(1)}, u32[]{:S(2)}, u32[]{:S(2)}) collective-permute-start(bf16[4,192,768]{2,1,0:T(8,128)(2,1)S(1)} %pad_maximum_fusion.w0.refs_2_.refs_1_), channel_id=1, source_target_pairs={{0,1},{1,0},{2,3},{3,2},{4,5},{5,4},{6,7},{7,6},{8,9},{9,8},{10,11... | collective-permute-start | bytes 3538952 | tf_op jit(solution)/shard_map/ppermute | solution.py:584
  9.1 35.4 %collective-permute-start.2 = (bf16[256,768]{1,0:T(8,128)(2,1)}, bf16[256,768]{1,0:T(8,128)(2,1)S(1)}, u32[]{:S(2)}, u32[]{:S(2)}) collective-permute-start(bf16[256,768]{1,0:T(8,128)(2,1)} %get-tuple-element.254), channel_id=1, source_target_pairs={{0,3},{1,2},{2,1},{3,0},{4,7},{5,6},{6,5},{7,4},{8,11},{9,10},{10,... | collective-permute-start | bytes 1179656 | tf_op jit(solution)/shard_map/ppermute | solution.py:584
  11.7 34.4 %collective-permute-start.1 = (bf16[256,768]{1,0:T(8,128)(2,1)}, bf16[256,768]{1,0:T(8,128)(2,1)S(1)}, u32[]{:S(2)}, u32[]{:S(2)}) collective-permute-start(bf16[256,768]{1,0:T(8,128)(2,1)} %get-tuple-element.255), channel_id=1, source_target_pairs={{0,2},{1,3},{2,0},{3,1},{4,6},{5,7},{6,4},{7,5},{8,10},{9,11},{10,... | collective-permute-start | bytes 1179656 | tf_op jit(solution)/shard_map/ppermute | solution.py:584
  18.2 85.2 %collective-permute-start.11 = (bf16[3,768,512]{2,1,0:T(8,128)(2,1)}, bf16[3,768,512]{2,1,0:T(8,128)(2,1)}, u32[]{:S(2)}, u32[]{:S(2)}) collective-permute-start(bf16[3,768,512]{2,1,0:T(8,128)(2,1)} %maximum_convert_fusion.refs_1_), channel_id=1, source_target_pairs={{0,1},{1,0},{2,3},{3,2},{4,5},{5,4},{6,7},{7,6},{8,9},{9,8},{10,11... | collective-permute-start | bytes 7077896 | tf_op jit(solution)/shard_map/ppermute | solution.py:584
  20.3 22.4 %collective-permute-start.4 = (bf16[2,192,768]{2,1,0:T(8,128)(2,1)S(1)}, bf16[2,192,768]{2,1,0:T(8,128)(2,1)S(1)}, u32[]{:S(2)}, u32[]{:S(2)}) collective-permute-start(bf16[2,192,768]{2,1,0:T(8,128)(2,1)S(1)} %fusion), channel_id=1, source_target_pairs={{0,2},{1,3},{2,0},{3,1},{4,6},{5,7},{6,4},{7,5},{8,10},{9,11},{10,... | collective-permute-start | bytes 1769480 | tf_op jit(solution)/shard_map/ppermute | solution.py:584
  44.5 28.9 %collective-permute-start.12 = (bf16[1152,512]{1,0:T(8,128)(2,1)S(1)}, bf16[1152,512]{1,0:T(8,128)(2,1)S(1)}, u32[]{:S(2)}, u32[]{:S(2)}) collective-permute-start(bf16[1152,512]{1,0:T(8,128)(2,1)S(1)} %constant_dynamic-slice_fusion), channel_id=1, source_target_pairs={{0,2},{1,3},{2,0},{3,1},{4,6},{5,7},{6,4},{7,5},{8,10},{9,11},{10,... | collective-permute-start | bytes 3538952 | tf_op jit(solution)/shard_map/ppermute | solution.py:584
  46.1 43.5 %collective-permute-start.10 = (bf16[256,768]{1,0:T(8,128)(2,1)S(1)}, bf16[256,768]{1,0:T(8,128)(2,1)S(1)}, u32[]{:S(2)}, u32[]{:S(2)}) collective-permute-start(bf16[256,768]{1,0:T(8,128)(2,1)S(1)} %get-tuple-element.250), channel_id=1, source_target_pairs={{0,3},{1,2},{2,1},{3,0},{4,7},{5,6},{6,5},{7,4},{8,11},{9,10},{10,... | collective-permute-start | bytes 1179656 | tf_op jit(solution)/shard_map/ppermute | solution.py:584
  46.1 28.8 %collective-permute-start.6 = (bf16[2,192,768]{2,1,0:T(8,128)(2,1)S(1)}, bf16[2,192,768]{2,1,0:T(8,128)(2,1)S(1)}, u32[]{:S(2)}, u32[]{:S(2)}) collective-permute-start(bf16[2,192,768]{2,1,0:T(8,128)(2,1)S(1)} %collective-permute-done.4.d2), channel_id=1, source_target_pairs={{0,1},{1,0},{2,3},{3,2},{4,5},{5,4},{6,7},{7,6},{8,9},{9,8},{10,11... | collective-permute-start | bytes 1769480 | tf_op jit(solution)/shard_map/ppermute | solution.py:584
  74.9 28.5 %collective-permute-start.14 = (bf16[1152,512]{1,0:T(8,128)(2,1)S(1)}, bf16[1152,512]{1,0:T(8,128)(2,1)}, u32[]{:S(2)}, u32[]{:S(2)}) collective-permute-start(bf16[1152,512]{1,0:T(8,128)(2,1)S(1)} %collective-permute-done.12.refs_2_), channel_id=1, source_target_pairs={{0,4},{4,0},{8,12},{12,8},{16,20},{20,16},{24,28},{28,24},{1,5},{5... | collective-permute-start | bytes 3538952 | tf_op jit(solution)/shard_map/ppermute | solution.py:584
  89.6 34.3 %collective-permute-start.13 = (bf16[1152,512]{1,0:T(8,128)(2,1)S(1)}, bf16[1152,512]{1,0:T(8,128)(2,1)}, u32[]{:S(2)}, u32[]{:S(2)}) collective-permute-start(bf16[1152,512]{1,0:T(8,128)(2,1)S(1)} %collective-permute-done.12.refs_2_), channel_id=1, source_target_pairs={{0,1},{1,0},{2,3},{3,2},{4,5},{5,4},{6,7},{7,6},{8,9},{9,8},{10,11... | collective-permute-start | bytes 3538952 | tf_op jit(solution)/shard_map/ppermute | solution.py:584
  123.4 36.3 %collective-permute-start.18 = (bf16[3,768,512]{2,1,0:T(8,128)(2,1)}, bf16[3,768,512]{2,1,0:T(8,128)(2,1)}, u32[]{:S(2)}, u32[]{:S(2)}) collective-permute-start(bf16[3,768,512]{2,1,0:T(8,128)(2,1)} %get-tuple-element.162), channel_id=1, source_target_pairs={{0,1},{1,0},{2,3},{3,2},{4,5},{5,4},{6,7},{7,6},{8,9},{9,8},{10,11... | collective-permute-start | bytes 7077896 | tf_op jit(solution)/shard_map/ppermute | solution.py:584
  159.2 30.6 %collective-permute-start.16 = (bf16[2,256,768]{2,1,0:T(8,128)(2,1)S(1)}, bf16[2,256,768]{2,1,0:T(8,128)(2,1)S(1)}, u32[]{:S(2)}, u32[]{:S(2)}) collective-permute-start(bf16[2,256,768]{2,1,0:T(8,128)(2,1)S(1)} %get-tuple-element.156), channel_id=1, source_target_pairs={{0,2},{1,3},{2,0},{3,1},{4,6},{5,7},{6,4},{7,5},{8,10},{9,11},{10,... | collective-permute-start | bytes 2359304 | tf_op jit(solution)/shard_map/ppermute | solution.py:584
  164.7 28.2 %collective-permute-start.20 = (bf16[2,576,512]{2,1,0:T(8,128)(2,1)S(1)}, bf16[2,576,512]{2,1,0:T(8,128)(2,1)S(1)}, u32[]{:S(2)}, u32[]{:S(2)}) collective-permute-start(bf16[2,576,512]{2,1,0:T(8,128)(2,1)S(1)} %get-tuple-element.174), channel_id=1, source_target_pairs={{0,4},{4,0},{8,12},{12,8},{16,20},{20,16},{24,28},{28,24},{1,5},{5... | collective-permute-start | bytes 3538952 | tf_op jit(solution)/shard_map/ppermute | solution.py:584
  165.2 27.8 %collective-permute-start.21 = (bf16[2,576,512]{2,1,0:T(8,128)(2,1)S(1)}, bf16[2,576,512]{2,1,0:T(8,128)(2,1)S(1)}, u32[]{:S(2)}, u32[]{:S(2)}) collective-permute-start(bf16[2,576,512]{2,1,0:T(8,128)(2,1)S(1)} %get-tuple-element.176), channel_id=1, source_target_pairs={{0,8},{4,12},{8,0},{12,4},{16,24},{20,28},{24,16},{28,20},{1,9},{5... | collective-permute-start | bytes 3538952 | tf_op jit(solution)/shard_map/ppermute | solution.py:584
  166.9 31.2 %collective-permute-start.22 = (bf16[2,192,768]{2,1,0:T(8,128)(2,1)S(1)}, bf16[2,192,768]{2,1,0:T(8,128)(2,1)S(1)}, u32[]{:S(2)}, u32[]{:S(2)}) collective-permute-start(bf16[2,192,768]{2,1,0:T(8,128)(2,1)S(1)} %get-tuple-element.182), channel_id=1, source_target_pairs={{0,1},{1,0},{2,3},{3,2},{4,5},{5,4},{6,7},{7,6},{8,9},{9,8},{10,11... | collective-permute-start | bytes 1769480 | tf_op jit(solution)/shard_map/ppermute | solution.py:584
  199.1 25.4 %collective-permute-start.28 = (bf16[576,768]{1,0:T(8,128)(2,1)S(1)}, bf16[576,768]{1,0:T(8,128)(2,1)S(1)}, u32[]{:S(2)}, u32[]{:S(2)}) collective-permute-start(bf16[576,768]{1,0:T(8,128)(2,1)S(1)} %get-tuple-element.198), channel_id=1, source_target_pairs={{0,2},{1,3},{2,0},{3,1},{4,6},{5,7},{6,4},{7,5},{8,10},{9,11},{10,... | collective-permute-start | bytes 2654216 | tf_op jit(solution)/shard_map/ppermute | solution.py:584
  216.3 27.7 %collective-permute-start.29 = (bf16[2,288,512]{2,1,0:T(8,128)(2,1)}, bf16[2,288,512]{2,1,0:T(8,128)(2,1)}, u32[]{:S(2)}, u32[]{:S(2)}) collective-permute-start(bf16[2,288,512]{2,1,0:T(8,128)(2,1)} %get-tuple-element.204), channel_id=1, source_target_pairs={{0,2},{1,3},{2,0},{3,1},{4,6},{5,7},{6,4},{7,5},{8,10},{9,11},{10,... | collective-permute-start | bytes 1769480 | tf_op jit(solution)/shard_map/ppermute | solution.py:584
  226.5 23.4 %collective-permute-start.31 = (bf16[288,768]{1,0:T(8,128)(2,1)}, bf16[288,768]{1,0:T(8,128)(2,1)}, u32[]{:S(2)}, u32[]{:S(2)}) collective-permute-start(bf16[288,768]{1,0:T(8,128)(2,1)} %get-tuple-element.209), channel_id=1, source_target_pairs={{0,4},{4,0},{8,12},{12,8},{16,20},{20,16},{24,28},{28,24},{1,5},{5... | collective-permute-start | bytes 1327112 | tf_op jit(solution)/shard_map/ppermute | solution.py:584
  227.0 21.1 %collective-permute-start.30 = (bf16[192,768]{1,0:T(8,128)(2,1)}, bf16[192,768]{1,0:T(8,128)(2,1)}, u32[]{:S(2)}, u32[]{:S(2)}) collective-permute-start(bf16[192,768]{1,0:T(8,128)(2,1)} %get-tuple-element.207), channel_id=1, source_target_pairs={{0,2},{1,3},{2,0},{3,1},{4,6},{5,7},{6,4},{7,5},{8,10},{9,11},{10,... | collective-permute-start | bytes 884744 | tf_op jit(solution)/shard_map/ppermute | solution.py:584
  245.5 22.3 %collective-permute-start.33 = (bf16[2,144,512]{2,1,0:T(8,128)(2,1)S(1)}, bf16[2,144,512]{2,1,0:T(8,128)(2,1)S(1)}, u32[]{:S(2)}, u32[]{:S(2)}) collective-permute-start(bf16[2,144,512]{2,1,0:T(8,128)(2,1)S(1)} %get-tuple-element.215), channel_id=1, source_target_pairs={{0,16},{4,20},{8,24},{12,28},{16,0},{20,4},{24,8},{28,12},{1,17},{... | collective-permute-start | bytes 884744 | tf_op jit(solution)/shard_map/ppermute | solution.py:584
  251.7 33.6 %all-to-all-start = ((bf16[8,24,768]{2,1,0:T(8,128)(2,1)}), bf16[8,24,768]{2,1,0:T(8,128)(2,1)S(1)}, u32[]{:S(2)}, u32[]{:S(2)}) async-start(bf16[8,24,768]{2,1,0:T(8,128)(2,1)} %bitcast.37), calls=%async_computation | async-start | bytes 589824 | tf_op jit(solution)/shard_map/all_to_all | solution.py:902
  269.5 42.1 %collective-permute-start.44 = (bf16[2,256,768]{2,1,0:T(8,128)(2,1)}, bf16[2,256,768]{2,1,0:T(8,128)(2,1)}, u32[]{:S(2)}, u32[]{:S(2)}) collective-permute-start(bf16[2,256,768]{2,1,0:T(8,128)(2,1)} %get-tuple-element.231), channel_id=1, source_target_pairs={{0,2},{1,3},{2,0},{3,1},{4,6},{5,7},{6,4},{7,5},{8,10},{9,11},{10,... | collective-permute-start | bytes 2359304 | tf_op jit(solution)/shard_map/ppermute | solution.py:584
  293.3 28.6 %all-to-all-start.1 = ((bf16[8,32,768]{2,1,0:T(8,128)(2,1)}), bf16[8,32,768]{2,1,0:T(8,128)(2,1)S(1)}, u32[]{:S(2)}, u32[]{:S(2)}) async-start(bf16[8,32,768]{2,1,0:T(8,128)(2,1)} %copy-done.37), calls=%async_computation.1 | async-start | bytes 786432 | tf_op jit(solution)/shard_map/all_to_all | solution.py:902
  311.6 21.2 %collective-permute-start.47 = (bf16[576,512]{1,0:T(8,128)(2,1)}, bf16[576,512]{1,0:T(8,128)(2,1)}, u32[]{:S(2)}, u32[]{:S(2)}) collective-permute-start(bf16[576,512]{1,0:T(8,128)(2,1)} %bitcast.46.p), channel_id=1, source_target_pairs={{0,4},{4,0},{8,12},{12,8},{16,20},{20,16},{24,28},{28,24},{1,5},{5... | collective-permute-start | bytes 1769480 | tf_op jit(solution)/shard_map/ppermute | solution.py:584
  (77 other events, 975.6 us)

commit v5 on v4

--- a/solution.py
+++ b/solution.py
@@ -519,7 +519,7 @@
     )
 
 
-def token_grad_body(turns, last, meta_ref, *refs):
+def token_grad_body(turns, meta_ref, *refs):
     dts = refs[: len(turns)]
     weights = refs[len(turns) : len(turns) + 4]
     rest = refs[len(turns) + 4 :]
@@ -530,11 +530,7 @@
             w = jnp.concatenate([w[part, turn * HD : (turn + 1) * HD, :] for w in weights], axis=0)
             more = nn(dt[part].T, w)
             total = more if total is None else total + more
-    if not last:
-        rest[0][...] = total
-        return
-    before_ref, x_ref, da_ref, g_ref, gain_ref, e0, e1, e23, gain_out = rest
-    total = total + before_ref[...]
+    x_ref, da_ref, g_ref, gain_ref, e0, e1, e23, gain_out = rest
     back, gain_grad = norm_back(total, x_ref[...].astype(F32), gain_ref[...])
     give(meta_ref, (da_ref[...] - g_ref[...].astype(F32) + back).astype(BF16), (e0, e1, e23))
 
@@ -545,31 +541,22 @@
     gain_out[...] += gain_grad
 
 
-def token_grad(meta, turns, dts, weights, rest=None):
+def token_grad(meta, turns, dts, weights, rest):
     width = weights[0].shape[2]
     step = 256
     rows = pl.BlockSpec((step, width), lambda i: (i, 0))
     full = lambda a: pl.BlockSpec(a.shape, lambda i, n=a.ndim: (0,) * n)
     cols = pl.BlockSpec((3, 4 * HD, step), lambda i: (0, 0, i))
-    specs = [SM] + [cols] * len(dts) + [full(w) for w in weights]
-    args = (meta, *dts, *weights)
-    if rest is None:
-        out = [struct((LEN, width), F32)]
-        out_specs = [rows]
-    else:
-        out = [struct((step, width), BF16)] * 2 + [struct((2, step, width), BF16), struct((1, width), F32)]
-        out_specs = [full(o) for o in out]
-        specs = specs + [rows] * 4 + [full(rest[4])]
-        args = args + tuple(rest)
-    return call(
-        functools.partial(token_grad_body, turns, rest is not None),
+    out = [struct((step, width), BF16)] * 2 + [struct((2, step, width), BF16), struct((1, width), F32)]
+    return call(
+        functools.partial(token_grad_body, turns),
         "token_grad",
         out,
-        args,
-        12,
+        (meta, *dts, *weights, *rest),
+        16,
         grid=(LEN // step,),
-        in_specs=specs,
-        out_specs=out_specs,
+        in_specs=[SM] + [cols] * len(dts) + [full(w) for w in weights] + [rows] * 3 + [full(rest[3])],
+        out_specs=[full(o) for o in out],
     )
 
 
@@ -622,7 +609,7 @@
         "start_sums",
         out,
         (meta, *parts),
-        16,
+        10,
         grid=(4,),
         in_specs=[SM] + [pl.BlockSpec((1, rows, cols), lambda i: (i, 0, 0))] * 4,
         out_specs=[pl.BlockSpec((2, rows, cols), lambda i: (0, 0, 0))] * 4,
@@ -647,7 +634,7 @@
         "second_sums",
         [struct((2, 2, half, cols), BF16)] + [struct((2, half, cols), BF16)] * 2,
         (meta, *[p.reshape(2, 2, half, cols) for p in pieces]),
-        20,
+        10,
         grid=(2,),
         in_specs=[SM] + [pl.BlockSpec((2, 1, half, cols), lambda i: (0, i, 0, 0))] * 4,
         out_specs=[full(2), full(1), full(1)],
@@ -673,7 +660,7 @@
         "third_sums",
         [struct((2, rows, cols), BF16)] * 2,
         (meta, a, bp, bq),
-        12,
+        8,
         grid=(2,),
         in_specs=[SM, pl.BlockSpec((1, 2, rows, cols), lambda i: (i, 0, 0, 0)), whole, whole],
         out_specs=[block, block],
@@ -697,7 +684,7 @@
         "halve_sums",
         [struct((2, half, cols), BF16)] * 2,
         (bit.reshape(1), a.reshape(2, 2, half, cols), b.reshape(2, 2, half, cols)),
-        12,
+        8,
         grid=(2,),
         in_specs=[SM] + [pl.BlockSpec((2, 1, half, cols), lambda i: (0, i, 0, 0))] * 2,
         out_specs=[pl.BlockSpec((2, half, cols), lambda i: (0, 0, 0))] * 2,
@@ -709,7 +696,7 @@
 
 
 def plain_sum(tie, a, b):
-    return call(plain_body, "plain_sum", [struct(a.shape, BF16)], (tie, a, b), 12, in_specs=[SM, VM, VM], out_specs=[VM])[0]
+    return call(plain_body, "plain_sum", [struct(a.shape, BF16)], (tie, a, b), 6, in_specs=[SM, VM, VM], out_specs=[VM])[0]
 
 
 def split_body(bit_ref, a, b, keep, send):
@@ -728,7 +715,7 @@
         "split_sums",
         [struct((half, cols), BF16)] * 2,
         (bit.reshape(1), a.reshape(2, half, cols), b.reshape(2, half, cols)),
-        12,
+        6,
         grid=(2,),
         in_specs=[SM] + [pl.BlockSpec((1, half, cols), lambda i: (i, 0, 0))] * 2,
         out_specs=[pl.BlockSpec((half, cols), lambda i: (0, 0))] * 2,
@@ -748,7 +735,7 @@
         "merge",
         [struct((2, rows, cols), BF16)],
         (bit.reshape(1), a, b),
-        12,
+        6,
         in_specs=[SM, VM, VM],
         out_specs=[VM],
     )[0]
@@ -769,7 +756,7 @@
         "pair_join",
         [struct((2, 2, rows, cols), BF16)],
         (bit.reshape(1), a, b),
-        12,
+        6,
         in_specs=[SM, VM, VM],
         out_specs=[VM],
     )[0]
@@ -792,7 +779,7 @@
         "cross_join",
         [struct((2, rows, cols), BF16)] * 2,
         (meta, a, bp, bq),
-        12,
+        6,
         in_specs=[SM, VM, VM, VM],
         out_specs=[VM, VM],
     )
@@ -823,7 +810,7 @@
         "mlp_out",
         [struct((2 * width, units), F32), struct((units, width), F32)],
         (meta, p, rp, q, rq),
-        24,
+        14,
         in_specs=[SM] + [VM] * 4,
         out_specs=[VM] * 2,
         scratch_shapes=[pltpu.VMEM((4, rows, units), BF16)],
@@ -848,7 +835,7 @@
         "core_sums",
         [struct((count * rows, cols), BF16)] * 2,
         args,
-        16,
+        8,
         in_specs=[SM] + [VM] * (2 * count),
         out_specs=[VM] * 2,
     )
@@ -930,7 +917,7 @@
         "attn_out",
         [struct((3, width, 3 * HD), F32), struct((3 * HD, width), F32), struct((2, width), F32)],
         (meta, own, other, late),
-        20,
+        12,
         in_specs=[SM, VM, VM, VM],
         out_specs=[VM, VM, VM],
         scratch_shapes=[pltpu.VMEM((3 * HD, width), F32), pltpu.VMEM((2,) + own.shape, BF16)],
@@ -955,7 +942,7 @@
         "add_home",
         [struct(base.shape, F32)],
         (meta, base, *pieces),
-        16,
+        8,
         grid=(count,),
         in_specs=[SM, block] + [full(p) for p in pieces],
         out_specs=[block],
@@ -1047,10 +1034,9 @@
     pieces = tensor(send, mask=2)
     late, late_send = run(core_sums, meta, (even2,), (in2,))
     late_recv = tensor(late_send, mask=2)
-    (before,) = run(lambda m: token_grad(m, (0, 1), (dt0, dt1), wa), meta)
     early, early_send = run(split_sums, bits[0], early, early_recv)
     early_recv = dp(early_send, mask=1)
-    *grads, gain_one = run(lambda m: token_grad(m, (2,), (dt2,), wa, (before, x, da, g, one)), meta)
+    *grads, gain_one = run(lambda m: token_grad(m, (0, 1, 2), (dt0, dt1, dt2), wa, (x, da, g, one)), meta)
     for shift in range(2, len(bits)):
         keep, send = run(halve_sums, bits[shift], keep, pieces)
         pieces = dp(send, mask=1 << shift)

time: 342 us -> 340 us (level)
  local copies, waits for them, and re-layouts: 38.5 us -> 43.1 us
  waiting for transfers between devices: 78.7 us -> 74.4 us
    unnamed x102 -> x114, local copies, waits for them, and re-layouts: 31.3 us -> 35.8 us
    ppermute x49, waiting for transfers between devices: 78.7 us -> 74.4 us  [swap(): return lax.ppermute(value, axis, [(i, i ^ mask) for i in range(size)])]
    pallas_call x34 -> x33, Pallas kernels: 159 us -> 158 us  [call(): pl.pallas_call(body, name=name, out_shape=out_shape, compiler_params=pltp...]
  transfers between devices with their start and end apart: 51 -> 51, of which waited for: 13 -> 14; matrix products, arithmetic and copies ran while one was open for 5% -> 5% of each run, Pallas kernels for 46% -> 46%
where the time goes in v5:
time: 340 us; the launch traced here: 336 us
  Pallas kernels  158 us (46%)
  waiting for transfers between devices  74.4 us (22%)
  starting transfers between devices  48.1 us (14%)
  local copies, waits for them, and re-layouts  43.1 us (13%)
  other arithmetic  10.9 us (3%)
    pallas_call x33, Pallas kernels, call(): pl.pallas_call(body, name=name, out_shape=out_shape, compiler_params=pltp...  158 us
    ppermute x49, waiting for transfers between devices, swap(): return lax.ppermute(value, axis, [(i, i ^ mask) for i in range(size)])  74.4 us
    ppermute x49, starting transfers between devices, swap(): return lax.ppermute(value, axis, [(i, i ^ mask) for i in range(size)])  39.5 us
    unnamed x114, local copies, waits for them, and re-layouts  35.8 us
    all_to_all x2, starting transfers between devices, exchange(): return lax.all_to_all(value, 'dp', 0, 0)  8.55 us
  transfers between devices with their start and end apart: 51, of which 14 were waited for; matrix products, arithmetic and copies ran while one was open for 5% of the time, Pallas kernels for 46%

profile of v5, /device:TPU:0, one launch (start us, length us, event | category | flops | bytes accessed | tf_op | source)
XLA Modules:
  0.0 335.8 jit_solution(17492730941863603398)
XLA Ops:
  14.4 3.8 %maximum_convert_fusion.refs_1_ = bf16[3,768,512]{2,1,0:T(8,128)(2,1)} fusion(bf16[1,768,512]{2,1,0:T(8,128)(2,1)} %bitcast.77, f32[2,768,512]{2,1,0:T(8,128)} %param.12), kind=kLoop, calls=%fused_computation | loop fusion | flops 1179648 | bytes 6291456 | tf_op jit(solution)/shard_map/convert_element_type | solution.py:991
  24.4 18.2 %collective-permute-done.4.d2 = bf16[2,192,768]{2,1,0:T(8,128)(2,1)S(1)} collective-permute-done((bf16[2,192,768]{2,1,0:T(8,128)(2,1)S(1)}, bf16[2,192,768]{2,1,0:T(8,128)(2,1)S(1)}, u32[]{:S(2)}, u32[]{:S(2)}) %collective-permute-start.4) | collective-permute-done | bytes 589856 | tf_op jit(solution)/shard_map/ppermute | solution.py:571
  50.7 5.0 %project_first.1 = (bf16[1024,768]{1,0:T(8,128)(2,1)S(1)}, bf16[1024,768]{1,0:T(8,128)(2,1)S(1)}, bf16[3,128,1024]{2,1,0:T(8,128)(2,1)S(1)}, bf16[3,128,1024]{2,1,0:T(8,128)(2,1)S(1)}, bf16[3,128,1024]{2,1,0:T(8,128)(2,1)S(1)}) custom-call(s32[5]{0:T(128)S(1)} %pad_add_fusion.meta_ref.starts_ref.tie_ref, bf16[256,768]{1,0:T(8,128)(2,1)S(1)} %get-tuple-element.255.p0, ...), custom_call_target="tpu_custom_call" | custom-call | flops 5000000000 | tf_op jit(solution)/shard_map/project_first/pallas_call | solution.py:45
  57.8 10.3 %attend.2 = (bf16[3,128,1024]{2,1,0:T(8,128)(2,1)S(1)}, bf16[1024,384]{1,0:T(8,128)(2,1)S(1)}, f32[3,2,1024]{2,1,0:T(2,128)S(1)}) custom-call(s32[5]{0:T(128)S(1)} %pad_add_fusion.meta_ref.starts_ref.tie_ref, bf16[3,128,1024]{2,1,0:T(8,128)(2,1)S(1)} %get-tuple-element.126.q_ref.refs_0_, bf16[3,128,1024]{2,1,0:T(8,128)(2,1)S(1)} %get-tuple-element.127.k_ref.refs_1_, ...), custom_call_target="tpu_custom_call" | custom-call | flops 10000000000 | tf_op jit(solution)/shard_map/attend/pallas_call | solution.py:45
  68.1 6.0 %collective-permute-done.12.refs_2_ = bf16[1152,512]{1,0:T(8,128)(2,1)S(1)} collective-permute-done((bf16[1152,512]{1,0:T(8,128)(2,1)S(1)}, bf16[1152,512]{1,0:T(8,128)(2,1)S(1)}, u32[]{:S(2)}, u32[]{:S(2)}) %collective-permute-start.12) | collective-permute-done | bytes 1179680 | tf_op jit(solution)/shard_map/ppermute | solution.py:571
  76.2 3.8 %project_next.1 = (bf16[3,128,1024]{2,1,0:T(8,128)(2,1)S(1)}, bf16[3,128,1024]{2,1,0:T(8,128)(2,1)S(1)}, bf16[3,128,1024]{2,1,0:T(8,128)(2,1)S(1)}, bf16[4,192,7...) custom-call(s32[5]{0:T(128)S(1)} %pad_add_fusion.meta_ref.starts_ref.tie_ref, ...), custom_call_target="tpu_custom_call" | custom-call | flops 5000000000 | tf_op jit(solution)/shard_map/project_next/pallas_call | solution.py:45
  80.0 10.3 %attend.3 = (bf16[3,128,1024]{2,1,0:T(8,128)(2,1)S(1)}, bf16[1024,384]{1,0:T(8,128)(2,1)S(1)}, f32[3,2,1024]{2,1,0:T(2,128)S(1)}) custom-call(s32[5]{0:T(128)S(1)} %pad_add_fusion.meta_ref.starts_ref.tie_ref, bf16[3,128,1024]{2,1,0:T(8,128)(2,1)S(1)} %get-tuple-element.133.q_ref.refs_5_, bf16[3,128,1024]{2,1,0:T(8,128)(2,1)S(1)} %get-tuple-element.135.k_ref.refs_6_, ...), custom_call_target="tpu_custom_call" | custom-call | flops 10000000000 | tf_op jit(solution)/shard_map/attend/pallas_call | solution.py:45
  90.6 4.7 %after_attention.1 = (f32[1024,768]{1,0:T(8,128)S(1)}, bf16[1024,768]{1,0:T(8,128)(2,1)S(1)}, bf16[768,1024]{1,0:T(8,128)(2,1)S(1)}, bf16[1024,768]{1,0:T(8,128)(2,1)S(1)}, bf16[768,1024]{1,0:T(8,128)(2,1)S(1)}) custom-call(s32[5]{0:T(128)S(1)} %pad_add_fusion.meta_ref.starts_ref.tie_ref, bf16[1024,768]{1,0:T(8,128)(2,1)S(1)} %get-tuple-element.124.x_ref.refs_7_, ...), custom_call_target="tpu_custom_call" | custom-call | flops 5000000000 | tf_op jit(solution)/shard_map/after_attention/pallas_call | solution.py:45
  95.3 8.8 %collective-permute-done.14.refs_3_ = bf16[1152,512]{1,0:T(8,128)(2,1)} collective-permute-done((bf16[1152,512]{1,0:T(8,128)(2,1)S(1)}, bf16[1152,512]{1,0:T(8,128)(2,1)}, u32[]{:S(2)}, u32[]{:S(2)}) %collective-permute-start.14) | collective-permute-done | bytes 1179680 | tf_op jit(solution)/shard_map/ppermute | solution.py:571
  104.1 18.7 %mlp.2 = (f32[1024,768]{1,0:T(8,128)S(1)}, f32[1024,768]{1,0:T(8,128)S(1)}, bf16[3,768,512]{2,1,0:T(8,128)(2,1)}, bf16[3,768,512]{2,1,0:T(8,128)(2,1)S(1)}) custom-call(s32[5]{0:T(128)S(1)} %pad_add_fusion.meta_ref.starts_ref.tie_ref, bf16[1024,768]{1,0:T(8,128)(2,1)S(1)} %get-tuple-element.145.n2_ref, bf16[768,1024]{1,0:T(8,128)(2,1)S(1)} %get-tuple-element.146.n2t_ref, ...), custom_call_target="tpu_custom_call" | custom-call | flops 15000000512 | tf_op jit(solution)/shard_map/mlp/pallas_call | solution.py:45
  127.6 18.9 %mlp.3 = (f32[1024,768]{1,0:T(8,128)S(1)}, f32[1024,768]{1,0:T(8,128)S(1)}, bf16[3,768,512]{2,1,0:T(8,128)(2,1)S(1)}, bf16[3,768,512]{2,1,0:T(8,128)(2,1)S(1)}) custom-call(s32[5]{0:T(128)S(1)} %pad_add_fusion.meta_ref.starts_ref.tie_ref, bf16[1024,768]{1,0:T(8,128)(2,1)S(1)} %get-tuple-element.145.n2_ref, ...), custom_call_target="tpu_custom_call", output_to_operand_aliasing={{0}: (9, {}), {1}: (10, {})} | custom-call | flops 15000000512 | tf_op jit(solution)/shard_map/mlp/pallas_call | solution.py:45
  152.0 8.1 %middle.1 = (bf16[256,768]{1,0:T(8,128)(2,1)S(1)}, bf16[256,768]{1,0:T(8,128)(2,1)}, bf16[2,256,768]{2,1,0:T(8,128)(2,1)S(1)}, f32[1024,768]{1,0:T(8,128)S(1)}, ...) custom-call(s32[5]{0:T(128)S(1)} %pad_add_fusion.meta_ref.starts_ref, ...), custom_call_target="tpu_custom_call" | custom-call | flops 3000000000 | tf_op jit(solution)/shard_map/middle/pallas_call | solution.py:45
  160.6 4.5 %start_sums.1 = (bf16[2,576,512]{2,1,0:T(8,128)(2,1)S(1)}, bf16[2,576,512]{2,1,0:T(8,128)(2,1)S(1)}, bf16[2,576,512]{2,1,0:T(8,128)(2,1)S(1)}, bf16[2,576,512]{2,1,0:T(8,128)(2,1)S(1)}) custom-call(s32[5]{0:T(128)S(1)} %pad_add_fusion.meta_ref.starts_ref.tie_ref, bf16[4,576,512]{2,1,0:T(8,128)(2,1)S(1)} %bitcast.64, bf16[4,576,512]{2,1,0:T(8,128)(2,1)} %bitcast.18.b0, ...), custom_call_target="tpu_custom_call" | custom-call | flops 1000000000 | tf_op jit(solution)/shard_map/start_sums/pallas_call | solution.py:45
  167.3 11.1 %attend_back.3 = (bf16[3,256,1024]{2,1,0:T(8,128)(2,1)S(1)}, bf16[2,192,768]{2,1,0:T(8,128)(2,1)S(1)}, bf16[2,192,768]{2,1,0:T(8,128)(2,1)S(1)}) custom-call(s32[5]{0:T(128)S(1)} %pad_add_fusion.meta_ref.starts_ref.tie_ref, f32[32,1024]{1,0:T(8,128)S(1)} %get-tuple-element.259.cos_ref, f32[32,1024]{1,0:T(8,128)S(1)} %get-tuple-element.258.sin_ref, ...), custom_call_target="tpu_custom_call" | custom-call | flops 2000000000 | tf_op jit(solution)/shard_map/attend_back/pallas_call | solution.py:45
  180.1 11.5 %attend_back.4 = (bf16[3,256,1024]{2,1,0:T(8,128)(2,1)S(1)}, bf16[2,192,768]{2,1,0:T(8,128)(2,1)S(1)}, bf16[2,192,768]{2,1,0:T(8,128)(2,1)S(1)}) custom-call(s32[5]{0:T(128)S(1)} %pad_add_fusion.meta_ref.starts_ref.tie_ref, f32[32,1024]{1,0:T(8,128)S(1)} %get-tuple-element.259.cos_ref, f32[32,1024]{1,0:T(8,128)S(1)} %get-tuple-element.258.sin_ref, ...), custom_call_target="tpu_custom_call" | custom-call | flops 2000000000 | tf_op jit(solution)/shard_map/attend_back/pallas_call | solution.py:45
  200.8 11.1 %attend_back.5 = (bf16[3,256,1024]{2,1,0:T(8,128)(2,1)S(1)}, bf16[2,192,768]{2,1,0:T(8,128)(2,1)S(1)}, bf16[2,192,768]{2,1,0:T(8,128)(2,1)S(1)}) custom-call(s32[5]{0:T(128)S(1)} %pad_add_fusion.meta_ref.starts_ref.tie_ref, f32[32,1024]{1,0:T(8,128)S(1)} %get-tuple-element.259.cos_ref, f32[32,1024]{1,0:T(8,128)S(1)} %get-tuple-element.258.sin_ref, ...), custom_call_target="tpu_custom_call" | custom-call | flops 2000000000 | tf_op jit(solution)/shard_map/attend_back/pallas_call | solution.py:45
  235.7 7.9 %token_grad.1 = (bf16[256,768]{1,0:T(8,128)(2,1)S(1)}, bf16[256,768]{1,0:T(8,128)(2,1)S(1)}, bf16[2,256,768]{2,1,0:T(8,128)(2,1)}, f32[1,768]{1,0:T(1,128)S(1)}) custom-call(s32[5]{0:T(128)S(1)} %pad_add_fusion.meta_ref.starts_ref.tie_ref, bf16[3,256,1024]{2,1,0:T(8,128)(2,1)S(1)} %copy-done.28, bf16[3,256,1024]{2,1,0:T(8,128)(2,1)S(1)} %copy-done.30, ...), custom_call_target="tpu_custom_call" | custom-call | flops 500000000 | tf_op jit(solution)/shard_map/token_grad/pallas_call | solution.py:45
  252.5 3.4 %all-to-all-start = ((bf16[8,24,768]{2,1,0:T(8,128)(2,1)}), bf16[8,24,768]{2,1,0:T(8,128)(2,1)S(1)}, u32[]{:S(2)}, u32[]{:S(2)}) async-start(bf16[8,24,768]{2,1,0:T(8,128)(2,1)} %bitcast.37), calls=%async_computation | async-start | bytes 589824 | tf_op jit(solution)/shard_map/all_to_all | solution.py:889
  256.0 4.8 %collective-permute-done.32 = bf16[144,768]{1,0:T(8,128)(2,1)S(1)} collective-permute-done((bf16[144,768]{1,0:T(8,128)(2,1)S(1)}, bf16[144,768]{1,0:T(8,128)(2,1)S(1)}, u32[]{:S(2)}, u32[]{:S(2)}) %collective-permute-start.32) | collective-permute-done | bytes 221216 | tf_op jit(solution)/shard_map/ppermute | solution.py:571
  266.6 17.1 %collective-permute-done.34.b = bf16[72,768]{1,0:T(8,128)(2,1)S(1)} collective-permute-done((bf16[72,768]{1,0:T(8,128)(2,1)S(1)}, bf16[72,768]{1,0:T(8,128)(2,1)S(1)}, u32[]{:S(2)}, u32[]{:S(2)}) %collective-permute-start.34) | collective-permute-done | bytes 110624 | tf_op jit(solution)/shard_map/ppermute | solution.py:571
  292.2 5.1 %all-to-all-start.1 = ((bf16[8,32,768]{2,1,0:T(8,128)(2,1)}), bf16[8,32,768]{2,1,0:T(8,128)(2,1)S(1)}, u32[]{:S(2)}, u32[]{:S(2)}) async-start(bf16[8,32,768]{2,1,0:T(8,128)(2,1)} %copy-done.39), calls=%async_computation.1 | async-start | bytes 786432 | tf_op jit(solution)/shard_map/all_to_all | solution.py:889
  297.3 5.2 %collective-permute-done.39.b = bf16[144,768]{1,0:T(8,128)(2,1)} collective-permute-done((bf16[144,768]{1,0:T(8,128)(2,1)}, bf16[144,768]{1,0:T(8,128)(2,1)}, u32[]{:S(2)}, u32[]{:S(2)}) %collective-permute-start.39) | collective-permute-done | bytes 221216 | tf_op jit(solution)/shard_map/ppermute | solution.py:571
  326.1 5.0 %collective-permute-done.47.rp = bf16[576,512]{1,0:T(8,128)(2,1)} collective-permute-done((bf16[576,512]{1,0:T(8,128)(2,1)}, bf16[576,512]{1,0:T(8,128)(2,1)}, u32[]{:S(2)}, u32[]{:S(2)}) %collective-permute-start.47) | collective-permute-done | bytes 589856 | tf_op jit(solution)/shard_map/ppermute | solution.py:571
  331.0 4.5 %mlp_out.1 = (f32[1536,512]{1,0:T(8,128)}, f32[512,768]{1,0:T(8,128)}) custom-call(s32[5]{0:T(128)S(1)} %pad_add_fusion.meta_ref.starts_ref.tie_ref, bf16[576,512]{1,0:T(8,128)(2,1)} %bitcast.46.p, bf16[576,512]{1,0:T(8,128)(2,1)} %collective-permute-done.47.rp, bf16[576,512]{1,0:T(8,128)(2,1)} %bitcast.48.q, bf16[576,512]{1,0:T(8,128)(2,1)} %collective-permute-done.48.rq), custom_call_target="tpu_custom_call" | custom-call | flops 100000000 | tf_op jit(solution)/shard_map/mlp_out/pallas_call | solution.py:45
  (246 shorter events, 126.4 us)
Async XLA Ops:
  5.6 41.1 %collective-permute-start.3 = (bf16[4,192,768]{2,1,0:T(8,128)(2,1)S(1)}, bf16[4,192,768]{2,1,0:T(8,128)(2,1)S(1)}, u32[]{:S(2)}, u32[]{:S(2)}) collective-permute-start(bf16[4,192,768]{2,1,0:T(8,128)(2,1)S(1)} %pad_maximum_fusion.w0.refs_3_), channel_id=1, source_target_pairs={{0,1},{1,0},{2,3},{3,2},{4,5},{5,4},{6,7},{7,6},{8,9},{9,8},{10,11... | collective-permute-start | bytes 3538952 | tf_op jit(solution)/shard_map/ppermute | solution.py:571
  9.1 35.4 %collective-permute-start.2 = (bf16[256,768]{1,0:T(8,128)(2,1)}, bf16[256,768]{1,0:T(8,128)(2,1)S(1)}, u32[]{:S(2)}, u32[]{:S(2)}) collective-permute-start(bf16[256,768]{1,0:T(8,128)(2,1)} %get-tuple-element.252), channel_id=1, source_target_pairs={{0,3},{1,2},{2,1},{3,0},{4,7},{5,6},{6,5},{7,4},{8,11},{9,10},{10,... | collective-permute-start | bytes 1179656 | tf_op jit(solution)/shard_map/ppermute | solution.py:571
  11.7 35.0 %collective-permute-start.1 = (bf16[256,768]{1,0:T(8,128)(2,1)}, bf16[256,768]{1,0:T(8,128)(2,1)}, u32[]{:S(2)}, u32[]{:S(2)}) collective-permute-start(bf16[256,768]{1,0:T(8,128)(2,1)} %get-tuple-element.253), channel_id=1, source_target_pairs={{0,2},{1,3},{2,0},{3,1},{4,6},{5,7},{6,4},{7,5},{8,10},{9,11},{10,... | collective-permute-start | bytes 1179656 | tf_op jit(solution)/shard_map/ppermute | solution.py:571
  18.2 85.9 %collective-permute-start.11 = (bf16[3,768,512]{2,1,0:T(8,128)(2,1)}, bf16[3,768,512]{2,1,0:T(8,128)(2,1)}, u32[]{:S(2)}, u32[]{:S(2)}) collective-permute-start(bf16[3,768,512]{2,1,0:T(8,128)(2,1)} %maximum_convert_fusion.refs_1_), channel_id=1, source_target_pairs={{0,1},{1,0},{2,3},{3,2},{4,5},{5,4},{6,7},{7,6},{8,9},{9,8},{10,11... | collective-permute-start | bytes 7077896 | tf_op jit(solution)/shard_map/ppermute | solution.py:571
  20.3 22.3 %collective-permute-start.4 = (bf16[2,192,768]{2,1,0:T(8,128)(2,1)S(1)}, bf16[2,192,768]{2,1,0:T(8,128)(2,1)S(1)}, u32[]{:S(2)}, u32[]{:S(2)}) collective-permute-start(bf16[2,192,768]{2,1,0:T(8,128)(2,1)S(1)} %fusion), channel_id=1, source_target_pairs={{0,2},{1,3},{2,0},{3,1},{4,6},{5,7},{6,4},{7,5},{8,10},{9,11},{10,... | collective-permute-start | bytes 1769480 | tf_op jit(solution)/shard_map/ppermute | solution.py:571
  45.2 28.8 %collective-permute-start.12 = (bf16[1152,512]{1,0:T(8,128)(2,1)S(1)}, bf16[1152,512]{1,0:T(8,128)(2,1)S(1)}, u32[]{:S(2)}, u32[]{:S(2)}) collective-permute-start(bf16[1152,512]{1,0:T(8,128)(2,1)S(1)} %constant_dynamic-slice_fusion), channel_id=1, source_target_pairs={{0,2},{1,3},{2,0},{3,1},{4,6},{5,7},{6,4},{7,5},{8,10},{9,11},{10,... | collective-permute-start | bytes 3538952 | tf_op jit(solution)/shard_map/ppermute | solution.py:571
  46.7 43.6 %collective-permute-start.10 = (bf16[256,768]{1,0:T(8,128)(2,1)S(1)}, bf16[256,768]{1,0:T(8,128)(2,1)S(1)}, u32[]{:S(2)}, u32[]{:S(2)}) collective-permute-start(bf16[256,768]{1,0:T(8,128)(2,1)S(1)} %get-tuple-element.248), channel_id=1, source_target_pairs={{0,3},{1,2},{2,1},{3,0},{4,7},{5,6},{6,5},{7,4},{8,11},{9,10},{10,... | collective-permute-start | bytes 1179656 | tf_op jit(solution)/shard_map/ppermute | solution.py:571
  47.8 27.7 %collective-permute-start.6 = (bf16[2,192,768]{2,1,0:T(8,128)(2,1)S(1)}, bf16[2,192,768]{2,1,0:T(8,128)(2,1)S(1)}, u32[]{:S(2)}, u32[]{:S(2)}) collective-permute-start(bf16[2,192,768]{2,1,0:T(8,128)(2,1)S(1)} %collective-permute-done.4.d2), channel_id=1, source_target_pairs={{0,1},{1,0},{2,3},{3,2},{4,5},{5,4},{6,7},{7,6},{8,9},{9,8},{10,11... | collective-permute-start | bytes 1769480 | tf_op jit(solution)/shard_map/ppermute | solution.py:571
  75.6 28.5 %collective-permute-start.14 = (bf16[1152,512]{1,0:T(8,128)(2,1)S(1)}, bf16[1152,512]{1,0:T(8,128)(2,1)}, u32[]{:S(2)}, u32[]{:S(2)}) collective-permute-start(bf16[1152,512]{1,0:T(8,128)(2,1)S(1)} %collective-permute-done.12.refs_2_), channel_id=1, source_target_pairs={{0,4},{4,0},{8,12},{12,8},{16,20},{20,16},{24,28},{28,24},{1,5},{5... | collective-permute-start | bytes 3538952 | tf_op jit(solution)/shard_map/ppermute | solution.py:571
  90.3 34.5 %collective-permute-start.13 = (bf16[1152,512]{1,0:T(8,128)(2,1)S(1)}, bf16[1152,512]{1,0:T(8,128)(2,1)}, u32[]{:S(2)}, u32[]{:S(2)}) collective-permute-start(bf16[1152,512]{1,0:T(8,128)(2,1)S(1)} %collective-permute-done.12.refs_2_), channel_id=1, source_target_pairs={{0,1},{1,0},{2,3},{3,2},{4,5},{5,4},{6,7},{7,6},{8,9},{9,8},{10,11... | collective-permute-start | bytes 3538952 | tf_op jit(solution)/shard_map/ppermute | solution.py:571
  124.2 36.3 %collective-permute-start.18 = (bf16[3,768,512]{2,1,0:T(8,128)(2,1)}, bf16[3,768,512]{2,1,0:T(8,128)(2,1)}, u32[]{:S(2)}, u32[]{:S(2)}) collective-permute-start(bf16[3,768,512]{2,1,0:T(8,128)(2,1)} %get-tuple-element.161), channel_id=1, source_target_pairs={{0,1},{1,0},{2,3},{3,2},{4,5},{5,4},{6,7},{7,6},{8,9},{9,8},{10,11... | collective-permute-start | bytes 7077896 | tf_op jit(solution)/shard_map/ppermute | solution.py:571
  160.0 32.7 %collective-permute-start.16 = (bf16[2,256,768]{2,1,0:T(8,128)(2,1)S(1)}, bf16[2,256,768]{2,1,0:T(8,128)(2,1)S(1)}, u32[]{:S(2)}, u32[]{:S(2)}) collective-permute-start(bf16[2,256,768]{2,1,0:T(8,128)(2,1)S(1)} %get-tuple-element.155), channel_id=1, source_target_pairs={{0,2},{1,3},{2,0},{3,1},{4,6},{5,7},{6,4},{7,5},{8,10},{9,11},{10,... | collective-permute-start | bytes 2359304 | tf_op jit(solution)/shard_map/ppermute | solution.py:571
  165.1 28.2 %collective-permute-start.20 = (bf16[2,576,512]{2,1,0:T(8,128)(2,1)S(1)}, bf16[2,576,512]{2,1,0:T(8,128)(2,1)S(1)}, u32[]{:S(2)}, u32[]{:S(2)}) collective-permute-start(bf16[2,576,512]{2,1,0:T(8,128)(2,1)S(1)} %get-tuple-element.173), channel_id=1, source_target_pairs={{0,4},{4,0},{8,12},{12,8},{16,20},{20,16},{24,28},{28,24},{1,5},{5... | collective-permute-start | bytes 3538952 | tf_op jit(solution)/shard_map/ppermute | solution.py:571
  165.6 27.8 %collective-permute-start.21 = (bf16[2,576,512]{2,1,0:T(8,128)(2,1)S(1)}, bf16[2,576,512]{2,1,0:T(8,128)(2,1)S(1)}, u32[]{:S(2)}, u32[]{:S(2)}) collective-permute-start(bf16[2,576,512]{2,1,0:T(8,128)(2,1)S(1)} %get-tuple-element.175), channel_id=1, source_target_pairs={{0,8},{4,12},{8,0},{12,4},{16,24},{20,28},{24,16},{28,20},{1,9},{5... | collective-permute-start | bytes 3538952 | tf_op jit(solution)/shard_map/ppermute | solution.py:571
  167.3 31.4 %collective-permute-start.22 = (bf16[2,192,768]{2,1,0:T(8,128)(2,1)S(1)}, bf16[2,192,768]{2,1,0:T(8,128)(2,1)S(1)}, u32[]{:S(2)}, u32[]{:S(2)}) collective-permute-start(bf16[2,192,768]{2,1,0:T(8,128)(2,1)S(1)} %get-tuple-element.181), channel_id=1, source_target_pairs={{0,1},{1,0},{2,3},{3,2},{4,5},{5,4},{6,7},{7,6},{8,9},{9,8},{10,11... | collective-permute-start | bytes 1769480 | tf_op jit(solution)/shard_map/ppermute | solution.py:571
  199.7 20.9 %collective-permute-start.28 = (bf16[576,768]{1,0:T(8,128)(2,1)S(1)}, bf16[576,768]{1,0:T(8,128)(2,1)S(1)}, u32[]{:S(2)}, u32[]{:S(2)}) collective-permute-start(bf16[576,768]{1,0:T(8,128)(2,1)S(1)} %get-tuple-element.196), channel_id=1, source_target_pairs={{0,2},{1,3},{2,0},{3,1},{4,6},{5,7},{6,4},{7,5},{8,10},{9,11},{10,... | collective-permute-start | bytes 2654216 | tf_op jit(solution)/shard_map/ppermute | solution.py:571
  216.2 27.5 %collective-permute-start.29 = (bf16[2,288,512]{2,1,0:T(8,128)(2,1)}, bf16[2,288,512]{2,1,0:T(8,128)(2,1)}, u32[]{:S(2)}, u32[]{:S(2)}) collective-permute-start(bf16[2,288,512]{2,1,0:T(8,128)(2,1)} %get-tuple-element.202), channel_id=1, source_target_pairs={{0,2},{1,3},{2,0},{3,1},{4,6},{5,7},{6,4},{7,5},{8,10},{9,11},{10,... | collective-permute-start | bytes 1769480 | tf_op jit(solution)/shard_map/ppermute | solution.py:571
  222.5 27.1 %collective-permute-start.31 = (bf16[288,768]{1,0:T(8,128)(2,1)}, bf16[288,768]{1,0:T(8,128)(2,1)}, u32[]{:S(2)}, u32[]{:S(2)}) collective-permute-start(bf16[288,768]{1,0:T(8,128)(2,1)} %get-tuple-element.207), channel_id=1, source_target_pairs={{0,4},{4,0},{8,12},{12,8},{16,20},{20,16},{24,28},{28,24},{1,5},{5... | collective-permute-start | bytes 1327112 | tf_op jit(solution)/shard_map/ppermute | solution.py:571
  223.1 24.8 %collective-permute-start.30 = (bf16[192,768]{1,0:T(8,128)(2,1)}, bf16[192,768]{1,0:T(8,128)(2,1)}, u32[]{:S(2)}, u32[]{:S(2)}) collective-permute-start(bf16[192,768]{1,0:T(8,128)(2,1)} %get-tuple-element.205), channel_id=1, source_target_pairs={{0,2},{1,3},{2,0},{3,1},{4,6},{5,7},{6,4},{7,5},{8,10},{9,11},{10,... | collective-permute-start | bytes 884744 | tf_op jit(solution)/shard_map/ppermute | solution.py:571
  252.5 31.9 %all-to-all-start = ((bf16[8,24,768]{2,1,0:T(8,128)(2,1)}), bf16[8,24,768]{2,1,0:T(8,128)(2,1)S(1)}, u32[]{:S(2)}, u32[]{:S(2)}) async-start(bf16[8,24,768]{2,1,0:T(8,128)(2,1)} %bitcast.37), calls=%async_computation | async-start | bytes 589824 | tf_op jit(solution)/shard_map/all_to_all | solution.py:889
  261.5 23.5 %collective-permute-start.37 = (bf16[2,144,512]{2,1,0:T(8,128)(2,1)S(1)}, bf16[2,144,512]{2,1,0:T(8,128)(2,1)S(1)}, u32[]{:S(2)}, u32[]{:S(2)}) collective-permute-start(bf16[2,144,512]{2,1,0:T(8,128)(2,1)S(1)} %plain_sum.4.a), channel_id=1, source_target_pairs={{0,16},{4,20},{8,24},{12,28},{16,0},{20,4},{24,8},{28,12},{1,17},{... | collective-permute-start | bytes 884744 | tf_op jit(solution)/shard_map/ppermute | solution.py:571
  262.7 47.6 %collective-permute-start.44 = (bf16[2,256,768]{2,1,0:T(8,128)(2,1)}, bf16[2,256,768]{2,1,0:T(8,128)(2,1)}, u32[]{:S(2)}, u32[]{:S(2)}) collective-permute-start(bf16[2,256,768]{2,1,0:T(8,128)(2,1)} %get-tuple-element.229), channel_id=1, source_target_pairs={{0,2},{1,3},{2,0},{3,1},{4,6},{5,7},{6,4},{7,5},{8,10},{9,11},{10,... | collective-permute-start | bytes 2359304 | tf_op jit(solution)/shard_map/ppermute | solution.py:571
  292.2 28.4 %all-to-all-start.1 = ((bf16[8,32,768]{2,1,0:T(8,128)(2,1)}), bf16[8,32,768]{2,1,0:T(8,128)(2,1)S(1)}, u32[]{:S(2)}, u32[]{:S(2)}) async-start(bf16[8,32,768]{2,1,0:T(8,128)(2,1)} %copy-done.39), calls=%async_computation.1 | async-start | bytes 786432 | tf_op jit(solution)/shard_map/all_to_all | solution.py:889
  310.3 20.7 %collective-permute-start.47 = (bf16[576,512]{1,0:T(8,128)(2,1)}, bf16[576,512]{1,0:T(8,128)(2,1)}, u32[]{:S(2)}, u32[]{:S(2)}) collective-permute-start(bf16[576,512]{1,0:T(8,128)(2,1)} %bitcast.46.p), channel_id=1, source_target_pairs={{0,4},{4,0},{8,12},{12,8},{16,20},{20,16},{24,28},{28,24},{1,5},{5... | collective-permute-start | bytes 1769480 | tf_op jit(solution)/shard_map/ppermute | solution.py:571
  (83 other events, 896.3 us)

commit v6 on v5

--- a/solution.py
+++ b/solution.py
@@ -1040,17 +1040,18 @@
     for shift in range(2, len(bits)):
         keep, send = run(halve_sums, bits[shift], keep, pieces)
         pieces = dp(send, mask=1 << shift)
-    late = run(plain_sum, meta, late, late_recv)
-    late = exchange(late.reshape(n_dp, -1, width))
     grads = homeward(grads[0], grads[1], tie(grads[2], late_recv))
     early, early_send = run(split_sums, bits[1], early, early_recv)
     early_recv = dp(early_send, mask=2)
     gains = jnp.concatenate([gain_one, gain_two])
     gains = gains + tensor(gains, mask=1)
     gains = gains + tensor(gains, mask=2)
+    outputs = run(add_home, meta, inputs, home)
     for shift in range(2, len(bits)):
         early, early_send = run(split_sums, bits[shift], early, early_recv)
         early_recv = dp(early_send, mask=1 << shift)
+    late = run(plain_sum, meta, late, late_recv)
+    late = exchange(late.reshape(n_dp, -1, width))
     piece = run(plain_sum, meta, keep, pieces)
     other = dp(piece, mask=1 << (len(bits) - 1))
     early = run(plain_sum, meta, early, early_recv)
@@ -1070,7 +1071,6 @@
     p, q = run(cross_join, meta, piece, recv_p, recv_q)
     recv_p = dp(p, mask=1)
     recv_q = dp(q, mask=2)
-    outputs = run(add_home, meta, inputs, home)
     input_grad = run(add_home, meta, out_grad, grads)
     grad_qkv, grad_out, gains = run(attn_out, meta, early, early_recv, late)
     grad_pair, grad_down = run(mlp_out, meta, p, recv_p, q, recv_q, width)

time: 340 us -> 346 us (1.018)
  waiting for transfers between devices: 74.4 us -> 80.5 us
    ppermute x49, waiting for transfers between devices: 74.4 us -> 80.5 us  [swap(): return lax.ppermute(value, axis, [(i, i ^ mask) for i in range(size)])]
    unnamed x114 -> x122, local copies, waits for them, and re-layouts: 35.8 us -> 36.5 us
  transfers between devices with their start and end apart: 51 -> 51, of which waited for: 14 -> 16; matrix products, arithmetic and copies ran while one was open for 5% -> 5% of each run, Pallas kernels for 46% -> 44%
where the time goes in v6:
time: 346 us; the launch traced here: 342 us
  Pallas kernels  155 us (45%)
  waiting for transfers between devices  80.5 us (23%)
  starting transfers between devices  49.9 us (14%)
  local copies, waits for them, and re-layouts  43.8 us (13%)
  other arithmetic  10.9 us (3%)
    pallas_call x33, Pallas kernels, call(): pl.pallas_call(body, name=name, out_shape=out_shape, compiler_params=pltp...  155 us
    ppermute x49, waiting for transfers between devices, swap(): return lax.ppermute(value, axis, [(i, i ^ mask) for i in range(size)])  80.5 us
    ppermute x49, starting transfers between devices, swap(): return lax.ppermute(value, axis, [(i, i ^ mask) for i in range(size)])  40 us
    unnamed x122, local copies, waits for them, and re-layouts  36.5 us
    all_to_all x2, starting transfers between devices, exchange(): return lax.all_to_all(value, 'dp', 0, 0)  9.91 us
  transfers between devices with their start and end apart: 51, of which 16 were waited for; matrix products, arithmetic and copies ran while one was open for 5% of the time, Pallas kernels for 44%

profile of v6, /device:TPU:0, one launch (start us, length us, event | category | flops | bytes accessed | tf_op | source)
XLA Modules:
  0.0 342.0 jit_solution(2811343731947573627)
XLA Ops:
  14.4 3.8 %maximum_convert_fusion.refs_1_ = bf16[3,768,512]{2,1,0:T(8,128)(2,1)} fusion(bf16[1,768,512]{2,1,0:T(8,128)(2,1)} %bitcast.79, f32[2,768,512]{2,1,0:T(8,128)} %param.12), kind=kLoop, calls=%fused_computation | loop fusion | flops 1179648 | bytes 6291456 | tf_op jit(solution)/shard_map/convert_element_type | solution.py:991
  24.4 18.2 %collective-permute-done.4.d2 = bf16[2,192,768]{2,1,0:T(8,128)(2,1)S(1)} collective-permute-done((bf16[2,192,768]{2,1,0:T(8,128)(2,1)S(1)}, bf16[2,192,768]{2,1,0:T(8,128)(2,1)S(1)}, u32[]{:S(2)}, u32[]{:S(2)}) %collective-permute-start.4) | collective-permute-done | bytes 589856 | tf_op jit(solution)/shard_map/ppermute | solution.py:571
  50.7 5.0 %project_first.1 = (bf16[1024,768]{1,0:T(8,128)(2,1)S(1)}, bf16[1024,768]{1,0:T(8,128)(2,1)S(1)}, bf16[3,128,1024]{2,1,0:T(8,128)(2,1)S(1)}, bf16[3,128,1024]{2,1,0:T(8,128)(2,1)S(1)}, bf16[3,128,1024]{2,1,0:T(8,128)(2,1)S(1)}) custom-call(s32[5]{0:T(128)S(1)} %pad_add_fusion.meta_ref.starts_ref.tie_ref, bf16[256,768]{1,0:T(8,128)(2,1)S(1)} %get-tuple-element.255.p0, ...), custom_call_target="tpu_custom_call" | custom-call | flops 5000000000 | tf_op jit(solution)/shard_map/project_first/pallas_call | solution.py:45
  57.8 10.3 %attend.2 = (bf16[3,128,1024]{2,1,0:T(8,128)(2,1)S(1)}, bf16[1024,384]{1,0:T(8,128)(2,1)S(1)}, f32[3,2,1024]{2,1,0:T(2,128)S(1)}) custom-call(s32[5]{0:T(128)S(1)} %pad_add_fusion.meta_ref.starts_ref.tie_ref, bf16[3,128,1024]{2,1,0:T(8,128)(2,1)S(1)} %get-tuple-element.126.q_ref.refs_0_, bf16[3,128,1024]{2,1,0:T(8,128)(2,1)S(1)} %get-tuple-element.127.k_ref.refs_1_, ...), custom_call_target="tpu_custom_call" | custom-call | flops 10000000000 | tf_op jit(solution)/shard_map/attend/pallas_call | solution.py:45
  68.1 6.0 %collective-permute-done.12.refs_2_ = bf16[1152,512]{1,0:T(8,128)(2,1)S(1)} collective-permute-done((bf16[1152,512]{1,0:T(8,128)(2,1)S(1)}, bf16[1152,512]{1,0:T(8,128)(2,1)S(1)}, u32[]{:S(2)}, u32[]{:S(2)}) %collective-permute-start.12) | collective-permute-done | bytes 1179680 | tf_op jit(solution)/shard_map/ppermute | solution.py:571
  76.2 3.8 %project_next.1 = (bf16[3,128,1024]{2,1,0:T(8,128)(2,1)S(1)}, bf16[3,128,1024]{2,1,0:T(8,128)(2,1)S(1)}, bf16[3,128,1024]{2,1,0:T(8,128)(2,1)S(1)}, bf16[4,192,7...) custom-call(s32[5]{0:T(128)S(1)} %pad_add_fusion.meta_ref.starts_ref.tie_ref, ...), custom_call_target="tpu_custom_call" | custom-call | flops 5000000000 | tf_op jit(solution)/shard_map/project_next/pallas_call | solution.py:45
  80.0 10.3 %attend.3 = (bf16[3,128,1024]{2,1,0:T(8,128)(2,1)S(1)}, bf16[1024,384]{1,0:T(8,128)(2,1)S(1)}, f32[3,2,1024]{2,1,0:T(2,128)S(1)}) custom-call(s32[5]{0:T(128)S(1)} %pad_add_fusion.meta_ref.starts_ref.tie_ref, bf16[3,128,1024]{2,1,0:T(8,128)(2,1)S(1)} %get-tuple-element.133.q_ref.refs_5_, bf16[3,128,1024]{2,1,0:T(8,128)(2,1)S(1)} %get-tuple-element.135.k_ref.refs_6_, ...), custom_call_target="tpu_custom_call" | custom-call | flops 10000000000 | tf_op jit(solution)/shard_map/attend/pallas_call | solution.py:45
  90.6 4.7 %after_attention.1 = (f32[1024,768]{1,0:T(8,128)S(1)}, bf16[1024,768]{1,0:T(8,128)(2,1)S(1)}, bf16[768,1024]{1,0:T(8,128)(2,1)S(1)}, bf16[1024,768]{1,0:T(8,128)(2,1)S(1)}, bf16[768,1024]{1,0:T(8,128)(2,1)S(1)}) custom-call(s32[5]{0:T(128)S(1)} %pad_add_fusion.meta_ref.starts_ref.tie_ref, bf16[1024,768]{1,0:T(8,128)(2,1)S(1)} %get-tuple-element.124.x_ref.refs_7_, ...), custom_call_target="tpu_custom_call" | custom-call | flops 5000000000 | tf_op jit(solution)/shard_map/after_attention/pallas_call | solution.py:45
  95.3 8.8 %collective-permute-done.14.refs_3_ = bf16[1152,512]{1,0:T(8,128)(2,1)} collective-permute-done((bf16[1152,512]{1,0:T(8,128)(2,1)S(1)}, bf16[1152,512]{1,0:T(8,128)(2,1)}, u32[]{:S(2)}, u32[]{:S(2)}) %collective-permute-start.14) | collective-permute-done | bytes 1179680 | tf_op jit(solution)/shard_map/ppermute | solution.py:571
  104.1 18.7 %mlp.2 = (f32[1024,768]{1,0:T(8,128)S(1)}, f32[1024,768]{1,0:T(8,128)S(1)}, bf16[3,768,512]{2,1,0:T(8,128)(2,1)}, bf16[3,768,512]{2,1,0:T(8,128)(2,1)S(1)}) custom-call(s32[5]{0:T(128)S(1)} %pad_add_fusion.meta_ref.starts_ref.tie_ref, bf16[1024,768]{1,0:T(8,128)(2,1)S(1)} %get-tuple-element.145.n2_ref, bf16[768,1024]{1,0:T(8,128)(2,1)S(1)} %get-tuple-element.146.n2t_ref, ...), custom_call_target="tpu_custom_call" | custom-call | flops 15000000512 | tf_op jit(solution)/shard_map/mlp/pallas_call | solution.py:45
  127.6 18.9 %mlp.3 = (f32[1024,768]{1,0:T(8,128)S(1)}, f32[1024,768]{1,0:T(8,128)S(1)}, bf16[3,768,512]{2,1,0:T(8,128)(2,1)S(1)}, bf16[3,768,512]{2,1,0:T(8,128)(2,1)S(1)}) custom-call(s32[5]{0:T(128)S(1)} %pad_add_fusion.meta_ref.starts_ref.tie_ref, bf16[1024,768]{1,0:T(8,128)(2,1)S(1)} %get-tuple-element.145.n2_ref, ...), custom_call_target="tpu_custom_call", output_to_operand_aliasing={{0}: (9, {}), {1}: (10, {})} | custom-call | flops 15000000512 | tf_op jit(solution)/shard_map/mlp/pallas_call | solution.py:45
  152.0 8.0 %middle.1 = (bf16[256,768]{1,0:T(8,128)(2,1)S(1)}, bf16[256,768]{1,0:T(8,128)(2,1)}, bf16[2,256,768]{2,1,0:T(8,128)(2,1)S(1)}, f32[1024,768]{1,0:T(8,128)S(1)}, ...) custom-call(s32[5]{0:T(128)S(1)} %pad_add_fusion.meta_ref.starts_ref, ...), custom_call_target="tpu_custom_call" | custom-call | flops 3000000000 | tf_op jit(solution)/shard_map/middle/pallas_call | solution.py:45
  160.5 4.6 %start_sums.1 = (bf16[2,576,512]{2,1,0:T(8,128)(2,1)S(1)}, bf16[2,576,512]{2,1,0:T(8,128)(2,1)S(1)}, bf16[2,576,512]{2,1,0:T(8,128)(2,1)S(1)}, bf16[2,576,512]{2,1,0:T(8,128)(2,1)S(1)}) custom-call(s32[5]{0:T(128)S(1)} %pad_add_fusion.meta_ref.starts_ref.tie_ref, bf16[4,576,512]{2,1,0:T(8,128)(2,1)S(1)} %bitcast.64, bf16[4,576,512]{2,1,0:T(8,128)(2,1)} %bitcast.18.b0, ...), custom_call_target="tpu_custom_call" | custom-call | flops 1000000000 | tf_op jit(solution)/shard_map/start_sums/pallas_call | solution.py:45
  167.3 11.1 %attend_back.3 = (bf16[3,256,1024]{2,1,0:T(8,128)(2,1)S(1)}, bf16[2,192,768]{2,1,0:T(8,128)(2,1)S(1)}, bf16[2,192,768]{2,1,0:T(8,128)(2,1)S(1)}) custom-call(s32[5]{0:T(128)S(1)} %pad_add_fusion.meta_ref.starts_ref.tie_ref, f32[32,1024]{1,0:T(8,128)S(1)} %get-tuple-element.259.cos_ref, f32[32,1024]{1,0:T(8,128)S(1)} %get-tuple-element.258.sin_ref, ...), custom_call_target="tpu_custom_call" | custom-call | flops 2000000000 | tf_op jit(solution)/shard_map/attend_back/pallas_call | solution.py:45
  180.0 11.5 %attend_back.4 = (bf16[3,256,1024]{2,1,0:T(8,128)(2,1)S(1)}, bf16[2,192,768]{2,1,0:T(8,128)(2,1)S(1)}, bf16[2,192,768]{2,1,0:T(8,128)(2,1)S(1)}) custom-call(s32[5]{0:T(128)S(1)} %pad_add_fusion.meta_ref.starts_ref.tie_ref, f32[32,1024]{1,0:T(8,128)S(1)} %get-tuple-element.259.cos_ref, f32[32,1024]{1,0:T(8,128)S(1)} %get-tuple-element.258.sin_ref, ...), custom_call_target="tpu_custom_call" | custom-call | flops 2000000000 | tf_op jit(solution)/shard_map/attend_back/pallas_call | solution.py:45
  200.8 11.1 %attend_back.5 = (bf16[3,256,1024]{2,1,0:T(8,128)(2,1)S(1)}, bf16[2,192,768]{2,1,0:T(8,128)(2,1)S(1)}, bf16[2,192,768]{2,1,0:T(8,128)(2,1)S(1)}) custom-call(s32[5]{0:T(128)S(1)} %pad_add_fusion.meta_ref.starts_ref.tie_ref, f32[32,1024]{1,0:T(8,128)S(1)} %get-tuple-element.259.cos_ref, f32[32,1024]{1,0:T(8,128)S(1)} %get-tuple-element.258.sin_ref, ...), custom_call_target="tpu_custom_call" | custom-call | flops 2000000000 | tf_op jit(solution)/shard_map/attend_back/pallas_call | solution.py:45
  235.7 8.0 %token_grad.1 = (bf16[256,768]{1,0:T(8,128)(2,1)S(1)}, bf16[256,768]{1,0:T(8,128)(2,1)}, bf16[2,256,768]{2,1,0:T(8,128)(2,1)}, f32[1,768]{1,0:T(1,128)S(1)}) custom-call(s32[5]{0:T(128)S(1)} %pad_add_fusion.meta_ref.starts_ref.tie_ref, bf16[3,256,1024]{2,1,0:T(8,128)(2,1)S(1)} %copy-done.28, bf16[3,256,1024]{2,1,0:T(8,128)(2,1)S(1)} %copy-done.30, ...), custom_call_target="tpu_custom_call" | custom-call | flops 500000000 | tf_op jit(solution)/shard_map/token_grad/pallas_call | solution.py:45
  253.9 4.6 %collective-permute-done.32 = bf16[144,768]{1,0:T(8,128)(2,1)S(1)} collective-permute-done((bf16[144,768]{1,0:T(8,128)(2,1)S(1)}, bf16[144,768]{1,0:T(8,128)(2,1)S(1)}, u32[]{:S(2)}, u32[]{:S(2)}) %collective-permute-start.32) | collective-permute-done | bytes 221216 | tf_op jit(solution)/shard_map/ppermute | solution.py:571
  260.0 4.8 %all-to-all-start = ((bf16[8,24,768]{2,1,0:T(8,128)(2,1)}), bf16[8,24,768]{2,1,0:T(8,128)(2,1)S(1)}, u32[]{:S(2)}, u32[]{:S(2)}) async-start(bf16[8,24,768]{2,1,0:T(8,128)(2,1)} %bitcast.37), calls=%async_computation | async-start | bytes 589824 | tf_op jit(solution)/shard_map/all_to_all | solution.py:889
  272.3 19.0 %collective-permute-done.35.b = bf16[72,768]{1,0:T(8,128)(2,1)S(1)} collective-permute-done((bf16[72,768]{1,0:T(8,128)(2,1)S(1)}, bf16[72,768]{1,0:T(8,128)(2,1)S(1)}, u32[]{:S(2)}, u32[]{:S(2)}) %collective-permute-start.35) | collective-permute-done | bytes 110624 | tf_op jit(solution)/shard_map/ppermute | solution.py:571
  298.9 5.1 %all-to-all-start.1 = ((bf16[8,32,768]{2,1,0:T(8,128)(2,1)}), bf16[8,32,768]{2,1,0:T(8,128)(2,1)S(1)}, u32[]{:S(2)}, u32[]{:S(2)}) async-start(bf16[8,32,768]{2,1,0:T(8,128)(2,1)} %copy-done.43), calls=%async_computation.1 | async-start | bytes 786432 | tf_op jit(solution)/shard_map/all_to_all | solution.py:889
  304.0 5.3 %collective-permute-done.40.b = bf16[144,768]{1,0:T(8,128)(2,1)} collective-permute-done((bf16[144,768]{1,0:T(8,128)(2,1)}, bf16[144,768]{1,0:T(8,128)(2,1)}, u32[]{:S(2)}, u32[]{:S(2)}) %collective-permute-start.40) | collective-permute-done | bytes 221216 | tf_op jit(solution)/shard_map/ppermute | solution.py:571
  332.1 5.1 %collective-permute-done.47.rp = bf16[576,512]{1,0:T(8,128)(2,1)} collective-permute-done((bf16[576,512]{1,0:T(8,128)(2,1)}, bf16[576,512]{1,0:T(8,128)(2,1)}, u32[]{:S(2)}, u32[]{:S(2)}) %collective-permute-start.47) | collective-permute-done | bytes 589856 | tf_op jit(solution)/shard_map/ppermute | solution.py:571
  337.3 4.5 %mlp_out.1 = (f32[1536,512]{1,0:T(8,128)}, f32[512,768]{1,0:T(8,128)}) custom-call(s32[5]{0:T(128)S(1)} %pad_add_fusion.meta_ref.starts_ref.tie_ref, bf16[576,512]{1,0:T(8,128)(2,1)} %bitcast.46.p, bf16[576,512]{1,0:T(8,128)(2,1)} %collective-permute-done.47.rp, bf16[576,512]{1,0:T(8,128)(2,1)} %bitcast.48.q, bf16[576,512]{1,0:T(8,128)(2,1)} %collective-permute-done.48.rq), custom_call_target="tpu_custom_call" | custom-call | flops 100000000 | tf_op jit(solution)/shard_map/mlp_out/pallas_call | solution.py:45
  (254 shorter events, 129.2 us)
Async XLA Ops:
  5.6 41.1 %collective-permute-start.3 = (bf16[4,192,768]{2,1,0:T(8,128)(2,1)S(1)}, bf16[4,192,768]{2,1,0:T(8,128)(2,1)S(1)}, u32[]{:S(2)}, u32[]{:S(2)}) collective-permute-start(bf16[4,192,768]{2,1,0:T(8,128)(2,1)S(1)} %pad_maximum_fusion.w0.refs_3_), channel_id=1, source_target_pairs={{0,1},{1,0},{2,3},{3,2},{4,5},{5,4},{6,7},{7,6},{8,9},{9,8},{10,11... | collective-permute-start | bytes 3538952 | tf_op jit(solution)/shard_map/ppermute | solution.py:571
  9.1 35.4 %collective-permute-start.2 = (bf16[256,768]{1,0:T(8,128)(2,1)}, bf16[256,768]{1,0:T(8,128)(2,1)S(1)}, u32[]{:S(2)}, u32[]{:S(2)}) collective-permute-start(bf16[256,768]{1,0:T(8,128)(2,1)} %get-tuple-element.252), channel_id=1, source_target_pairs={{0,3},{1,2},{2,1},{3,0},{4,7},{5,6},{6,5},{7,4},{8,11},{9,10},{10,... | collective-permute-start | bytes 1179656 | tf_op jit(solution)/shard_map/ppermute | solution.py:571
  11.7 35.0 %collective-permute-start.1 = (bf16[256,768]{1,0:T(8,128)(2,1)}, bf16[256,768]{1,0:T(8,128)(2,1)}, u32[]{:S(2)}, u32[]{:S(2)}) collective-permute-start(bf16[256,768]{1,0:T(8,128)(2,1)} %get-tuple-element.253), channel_id=1, source_target_pairs={{0,2},{1,3},{2,0},{3,1},{4,6},{5,7},{6,4},{7,5},{8,10},{9,11},{10,... | collective-permute-start | bytes 1179656 | tf_op jit(solution)/shard_map/ppermute | solution.py:571
  18.2 85.9 %collective-permute-start.11 = (bf16[3,768,512]{2,1,0:T(8,128)(2,1)}, bf16[3,768,512]{2,1,0:T(8,128)(2,1)}, u32[]{:S(2)}, u32[]{:S(2)}) collective-permute-start(bf16[3,768,512]{2,1,0:T(8,128)(2,1)} %maximum_convert_fusion.refs_1_), channel_id=1, source_target_pairs={{0,1},{1,0},{2,3},{3,2},{4,5},{5,4},{6,7},{7,6},{8,9},{9,8},{10,11... | collective-permute-start | bytes 7077896 | tf_op jit(solution)/shard_map/ppermute | solution.py:571
  20.3 22.3 %collective-permute-start.4 = (bf16[2,192,768]{2,1,0:T(8,128)(2,1)S(1)}, bf16[2,192,768]{2,1,0:T(8,128)(2,1)S(1)}, u32[]{:S(2)}, u32[]{:S(2)}) collective-permute-start(bf16[2,192,768]{2,1,0:T(8,128)(2,1)S(1)} %fusion), channel_id=1, source_target_pairs={{0,2},{1,3},{2,0},{3,1},{4,6},{5,7},{6,4},{7,5},{8,10},{9,11},{10,... | collective-permute-start | bytes 1769480 | tf_op jit(solution)/shard_map/ppermute | solution.py:571
  45.2 28.8 %collective-permute-start.12 = (bf16[1152,512]{1,0:T(8,128)(2,1)S(1)}, bf16[1152,512]{1,0:T(8,128)(2,1)S(1)}, u32[]{:S(2)}, u32[]{:S(2)}) collective-permute-start(bf16[1152,512]{1,0:T(8,128)(2,1)S(1)} %constant_dynamic-slice_fusion), channel_id=1, source_target_pairs={{0,2},{1,3},{2,0},{3,1},{4,6},{5,7},{6,4},{7,5},{8,10},{9,11},{10,... | collective-permute-start | bytes 3538952 | tf_op jit(solution)/shard_map/ppermute | solution.py:571
  46.7 43.6 %collective-permute-start.10 = (bf16[256,768]{1,0:T(8,128)(2,1)S(1)}, bf16[256,768]{1,0:T(8,128)(2,1)S(1)}, u32[]{:S(2)}, u32[]{:S(2)}) collective-permute-start(bf16[256,768]{1,0:T(8,128)(2,1)S(1)} %get-tuple-element.248), channel_id=1, source_target_pairs={{0,3},{1,2},{2,1},{3,0},{4,7},{5,6},{6,5},{7,4},{8,11},{9,10},{10,... | collective-permute-start | bytes 1179656 | tf_op jit(solution)/shard_map/ppermute | solution.py:571
  47.9 27.7 %collective-permute-start.6 = (bf16[2,192,768]{2,1,0:T(8,128)(2,1)S(1)}, bf16[2,192,768]{2,1,0:T(8,128)(2,1)S(1)}, u32[]{:S(2)}, u32[]{:S(2)}) collective-permute-start(bf16[2,192,768]{2,1,0:T(8,128)(2,1)S(1)} %collective-permute-done.4.d2), channel_id=1, source_target_pairs={{0,1},{1,0},{2,3},{3,2},{4,5},{5,4},{6,7},{7,6},{8,9},{9,8},{10,11... | collective-permute-start | bytes 1769480 | tf_op jit(solution)/shard_map/ppermute | solution.py:571
  75.6 28.5 %collective-permute-start.14 = (bf16[1152,512]{1,0:T(8,128)(2,1)S(1)}, bf16[1152,512]{1,0:T(8,128)(2,1)}, u32[]{:S(2)}, u32[]{:S(2)}) collective-permute-start(bf16[1152,512]{1,0:T(8,128)(2,1)S(1)} %collective-permute-done.12.refs_2_), channel_id=1, source_target_pairs={{0,4},{4,0},{8,12},{12,8},{16,20},{20,16},{24,28},{28,24},{1,5},{5... | collective-permute-start | bytes 3538952 | tf_op jit(solution)/shard_map/ppermute | solution.py:571
  90.3 34.4 %collective-permute-start.13 = (bf16[1152,512]{1,0:T(8,128)(2,1)S(1)}, bf16[1152,512]{1,0:T(8,128)(2,1)}, u32[]{:S(2)}, u32[]{:S(2)}) collective-permute-start(bf16[1152,512]{1,0:T(8,128)(2,1)S(1)} %collective-permute-done.12.refs_2_), channel_id=1, source_target_pairs={{0,1},{1,0},{2,3},{3,2},{4,5},{5,4},{6,7},{7,6},{8,9},{9,8},{10,11... | collective-permute-start | bytes 3538952 | tf_op jit(solution)/shard_map/ppermute | solution.py:571
  124.2 36.3 %collective-permute-start.18 = (bf16[3,768,512]{2,1,0:T(8,128)(2,1)}, bf16[3,768,512]{2,1,0:T(8,128)(2,1)}, u32[]{:S(2)}, u32[]{:S(2)}) collective-permute-start(bf16[3,768,512]{2,1,0:T(8,128)(2,1)} %get-tuple-element.161), channel_id=1, source_target_pairs={{0,1},{1,0},{2,3},{3,2},{4,5},{5,4},{6,7},{7,6},{8,9},{9,8},{10,11... | collective-permute-start | bytes 7077896 | tf_op jit(solution)/shard_map/ppermute | solution.py:571
  160.0 32.6 %collective-permute-start.16 = (bf16[2,256,768]{2,1,0:T(8,128)(2,1)S(1)}, bf16[2,256,768]{2,1,0:T(8,128)(2,1)S(1)}, u32[]{:S(2)}, u32[]{:S(2)}) collective-permute-start(bf16[2,256,768]{2,1,0:T(8,128)(2,1)S(1)} %get-tuple-element.155), channel_id=1, source_target_pairs={{0,2},{1,3},{2,0},{3,1},{4,6},{5,7},{6,4},{7,5},{8,10},{9,11},{10,... | collective-permute-start | bytes 2359304 | tf_op jit(solution)/shard_map/ppermute | solution.py:571
  165.1 28.2 %collective-permute-start.20 = (bf16[2,576,512]{2,1,0:T(8,128)(2,1)S(1)}, bf16[2,576,512]{2,1,0:T(8,128)(2,1)S(1)}, u32[]{:S(2)}, u32[]{:S(2)}) collective-permute-start(bf16[2,576,512]{2,1,0:T(8,128)(2,1)S(1)} %get-tuple-element.173), channel_id=1, source_target_pairs={{0,4},{4,0},{8,12},{12,8},{16,20},{20,16},{24,28},{28,24},{1,5},{5... | collective-permute-start | bytes 3538952 | tf_op jit(solution)/shard_map/ppermute | solution.py:571
  165.6 27.8 %collective-permute-start.21 = (bf16[2,576,512]{2,1,0:T(8,128)(2,1)S(1)}, bf16[2,576,512]{2,1,0:T(8,128)(2,1)S(1)}, u32[]{:S(2)}, u32[]{:S(2)}) collective-permute-start(bf16[2,576,512]{2,1,0:T(8,128)(2,1)S(1)} %get-tuple-element.175), channel_id=1, source_target_pairs={{0,8},{4,12},{8,0},{12,4},{16,24},{20,28},{24,16},{28,20},{1,9},{5... | collective-permute-start | bytes 3538952 | tf_op jit(solution)/shard_map/ppermute | solution.py:571
  167.3 31.4 %collective-permute-start.22 = (bf16[2,192,768]{2,1,0:T(8,128)(2,1)S(1)}, bf16[2,192,768]{2,1,0:T(8,128)(2,1)S(1)}, u32[]{:S(2)}, u32[]{:S(2)}) collective-permute-start(bf16[2,192,768]{2,1,0:T(8,128)(2,1)S(1)} %get-tuple-element.181), channel_id=1, source_target_pairs={{0,1},{1,0},{2,3},{3,2},{4,5},{5,4},{6,7},{7,6},{8,9},{9,8},{10,11... | collective-permute-start | bytes 1769480 | tf_op jit(solution)/shard_map/ppermute | solution.py:571
  199.7 20.9 %collective-permute-start.28 = (bf16[576,768]{1,0:T(8,128)(2,1)S(1)}, bf16[576,768]{1,0:T(8,128)(2,1)S(1)}, u32[]{:S(2)}, u32[]{:S(2)}) collective-permute-start(bf16[576,768]{1,0:T(8,128)(2,1)S(1)} %get-tuple-element.196), channel_id=1, source_target_pairs={{0,2},{1,3},{2,0},{3,1},{4,6},{5,7},{6,4},{7,5},{8,10},{9,11},{10,... | collective-permute-start | bytes 2654216 | tf_op jit(solution)/shard_map/ppermute | solution.py:571
  216.1 27.6 %collective-permute-start.29 = (bf16[2,288,512]{2,1,0:T(8,128)(2,1)}, bf16[2,288,512]{2,1,0:T(8,128)(2,1)}, u32[]{:S(2)}, u32[]{:S(2)}) collective-permute-start(bf16[2,288,512]{2,1,0:T(8,128)(2,1)} %get-tuple-element.202), channel_id=1, source_target_pairs={{0,2},{1,3},{2,0},{3,1},{4,6},{5,7},{6,4},{7,5},{8,10},{9,11},{10,... | collective-permute-start | bytes 1769480 | tf_op jit(solution)/shard_map/ppermute | solution.py:571
  222.5 22.7 %collective-permute-start.30 = (bf16[288,768]{1,0:T(8,128)(2,1)}, bf16[288,768]{1,0:T(8,128)(2,1)}, u32[]{:S(2)}, u32[]{:S(2)}) collective-permute-start(bf16[288,768]{1,0:T(8,128)(2,1)} %get-tuple-element.205), channel_id=1, source_target_pairs={{0,4},{4,0},{8,12},{12,8},{16,20},{20,16},{24,28},{28,24},{1,5},{5... | collective-permute-start | bytes 1327112 | tf_op jit(solution)/shard_map/ppermute | solution.py:571
  223.1 27.5 %collective-permute-start.31 = (bf16[256,768]{1,0:T(8,128)(2,1)}, bf16[256,768]{1,0:T(8,128)(2,1)}, u32[]{:S(2)}, u32[]{:S(2)}) collective-permute-start(bf16[256,768]{1,0:T(8,128)(2,1)} %get-tuple-element.208), channel_id=1, source_target_pairs={{0,1},{1,0},{2,3},{3,2},{4,5},{5,4},{6,7},{7,6},{8,9},{9,8},{10,11... | collective-permute-start | bytes 1179656 | tf_op jit(solution)/shard_map/ppermute | solution.py:571
  223.1 35.5 %collective-permute-start.33 = (bf16[192,768]{1,0:T(8,128)(2,1)}, bf16[192,768]{1,0:T(8,128)(2,1)S(1)}, u32[]{:S(2)}, u32[]{:S(2)}) collective-permute-start(bf16[192,768]{1,0:T(8,128)(2,1)} %copy-done.52), channel_id=1, source_target_pairs={{0,2},{1,3},{2,0},{3,1},{4,6},{5,7},{6,4},{7,5},{8,10},{9,11},{10,... | collective-permute-start | bytes 884744 | tf_op jit(solution)/shard_map/ppermute | solution.py:571
  260.0 32.0 %all-to-all-start = ((bf16[8,24,768]{2,1,0:T(8,128)(2,1)}), bf16[8,24,768]{2,1,0:T(8,128)(2,1)S(1)}, u32[]{:S(2)}, u32[]{:S(2)}) async-start(bf16[8,24,768]{2,1,0:T(8,128)(2,1)} %bitcast.37), calls=%async_computation | async-start | bytes 589824 | tf_op jit(solution)/shard_map/all_to_all | solution.py:889
  265.5 27.0 %collective-permute-start.38 = (bf16[2,144,512]{2,1,0:T(8,128)(2,1)S(1)}, bf16[2,144,512]{2,1,0:T(8,128)(2,1)S(1)}, u32[]{:S(2)}, u32[]{:S(2)}) collective-permute-start(bf16[2,144,512]{2,1,0:T(8,128)(2,1)S(1)} %plain_sum.4.a), channel_id=1, source_target_pairs={{0,16},{4,20},{8,24},{12,28},{16,0},{20,4},{24,8},{28,12},{1,17},{... | collective-permute-start | bytes 884744 | tf_op jit(solution)/shard_map/ppermute | solution.py:571
  269.4 47.3 %collective-permute-start.44 = (bf16[2,256,768]{2,1,0:T(8,128)(2,1)}, bf16[2,256,768]{2,1,0:T(8,128)(2,1)}, u32[]{:S(2)}, u32[]{:S(2)}) collective-permute-start(bf16[2,256,768]{2,1,0:T(8,128)(2,1)} %get-tuple-element.229), channel_id=1, source_target_pairs={{0,2},{1,3},{2,0},{3,1},{4,6},{5,7},{6,4},{7,5},{8,10},{9,11},{10,... | collective-permute-start | bytes 2359304 | tf_op jit(solution)/shard_map/ppermute | solution.py:571
  298.9 27.0 %all-to-all-start.1 = ((bf16[8,32,768]{2,1,0:T(8,128)(2,1)}), bf16[8,32,768]{2,1,0:T(8,128)(2,1)S(1)}, u32[]{:S(2)}, u32[]{:S(2)}) async-start(bf16[8,32,768]{2,1,0:T(8,128)(2,1)} %copy-done.43), calls=%async_computation.1 | async-start | bytes 786432 | tf_op jit(solution)/shard_map/all_to_all | solution.py:889
  (87 other events, 935.5 us)
